TPU v7x, 32 devices: a whole 2x2x4 slice. The times are simulated.
32 devices in a mesh: gx: 16 (over z, y, core), gy: 2 (over x).
Axes of the slice: x: 2, y: 2, z: 4, core: 2. Of those that a mesh axis runs over, the one named last changes fastest.
Arguments:
- tangent: bfloat16 [256, 1024, 256], P(None, 'gx', 'gy'), may hold values from -6 to 6
- courant_x: float32 [1024, 256], P('gx', 'gy'), may hold values from -0.5 to 0.5
- courant_y: float32 [1024, 256], P('gx', 'gy'), may hold values from -0.5 to 0.5
- growth: float32 [1024, 256], P('gx', 'gy'), may hold values from -0.15 to 0.15
Outputs:
- basis: bfloat16 [256, 1024, 256], P(None, 'gx', 'gy')
- factor: float32 [256, 256], replicated
- exponents: float32 [256], replicated
All inputs are finite; a program needn't handle non-finite values.
Results may differ from a plain program's by a relative error of at most 0.001.
The roundings to bfloat16 on the way count: a program that leaves them out, or rounds other values in their place, can miss the bound.
Values may be sent and summed in bfloat16 or wider, within the bound.
No kernel may reach another device: no remote copies, remote signals or barrier semaphores. Data moves between devices by JAX's collectives and lax.ppermute only.
A program may use at most 128 MiB of HBM per device.

v0:
```python
import jax
import jax.numpy as jnp
from jax import lax
from jax.sharding import PartitionSpec as P

SUBSTEPS = 4


def extended(block, sides, width):
    for axis, dim in sides:
        count = lax.axis_size(axis)
        forward = [(i, i + 1) for i in range(count - 1)]
        forward.append((count - 1, 0))
        backward = [(target, source) for source, target in forward]
        low = lax.ppermute(
            lax.slice_in_dim(block, block.shape[dim] - width, None, axis=dim), axis, forward
        )
        high = lax.ppermute(lax.slice_in_dim(block, 0, width, axis=dim), axis, backward)
        block = jnp.concatenate([low, block, high], axis=dim)
    return block


def advance(padded, courant_x, courant_y, growth):
    centre = padded[:, 1:-1, 1:-1]
    north = padded[:, 2:, 1:-1]
    south = padded[:, :-2, 1:-1]
    east = padded[:, 1:-1, 2:]
    west = padded[:, 1:-1, :-2]
    return (
        centre
        + 0.2 * (north + south + east + west - 4.0 * centre)
        - courant_x * (north - south)
        - courant_y * (east - west)
        + growth * centre
    )


def inner_products(left, right):
    return lax.dot_general(
        left, right, (((1,), (1,)), ((), ())), preferred_element_type=jnp.float32
    )


def per_device(tangent, courant_x, courant_y, growth):
    fields, rows, cols = tangent.shape
    steps = SUBSTEPS
    state = tangent.astype(jnp.float32)
    for step in range(steps):
        padded = extended(state, (("gx", 1), ("gy", 2)), 1)
        state = advance(padded, courant_x, courant_y, growth)
    evolved = state.astype(jnp.bfloat16).reshape(fields, rows * cols)
    total = jnp.float32(rows * lax.axis_size("gx") * cols * lax.axis_size("gy"))
    gram = lax.psum(inner_products(evolved, evolved), ("gx", "gy"))
    gram = gram / total
    lower = jnp.linalg.cholesky(gram)
    inverse = lax.linalg.triangular_solve(
        lower, jnp.eye(fields, dtype=jnp.float32), left_side=True, lower=True
    ).astype(jnp.bfloat16)
    basis = jnp.dot(inverse, evolved, preferred_element_type=jnp.float32)
    exponents = jnp.log(jnp.diagonal(lower))
    return (basis.astype(jnp.bfloat16).reshape(fields, rows, cols), lower.T, exponents)


def solution(mesh):
    placed = (P(None, "gx", "gy"), P("gx", "gy"), P("gx", "gy"), P("gx", "gy"))
    return jax.shard_map(
        per_device,
        mesh=mesh,
        in_specs=placed,
        out_specs=(P(None, "gx", "gy"), P(), P()),
        check_vma=False,
    )
```

profile of v0, /device:TPU:0, one launch (start us, length us, event | category | flops | bytes accessed | tf_op | source)
XLA Modules:
  0.0 358.3 jit_solution(11706130082598331027)
XLA Ops:
  7.2 6.8 %copy.53 = bf16[256,64,128]{0,2,1:T(8,128)(2,1)} copy(bf16[256,64,128]{2,1,0:T(8,128)(2,1)} %param.4) | data formatting | bytes 8388608 | tf_op args[0]
  15.0 5.5 %collective-permute-start = (f32[256,1,128]{2,0,1:T(8,128)S(1)}, f32[256,1,128]{2,0,1:T(8,128)S(1)}, u32[]{:S(2)}, u32[]{:S(2)}) collective-permute-start(f32[256,1,128]{2,0,1:T(8,128)S(1)} %copy.54), channel_id=1, source_target_pairs={{2,0},{4,2},{6,4},{8,6},{10,8},{12,10},{14,12},{16,14},{18,16},{20... | collective-permute-start | bytes 393224 | tf_op jit(solution)/shard_map/ppermute | solution.py:18
  20.7 6.6 %convert_element_type.11 = f32[256,64,128]{0,2,1:T(8,128)} convert(bf16[256,64,128]{0,2,1:T(8,128)(2,1)} %copy.53) | non-fusion elementwise | flops 2097152 | bytes 12582912 | tf_op jit(solution)/shard_map/convert_element_type | solution.py:47
  27.9 1.5 pad_maximum_fusion.43
  29.4 1.6 collective-permute-start.2
  31.5 2.3 collective-permute-done.2
  33.9 1.4 collective-permute-done.3
  35.4 14.9 %multiply_add_fusion.2 = f32[256,64,128]{0,2,1:T(8,128)S(1)} fusion(f32[256,64,128]{0,2,1:T(8,128)S(1)} %copy-done.6, f32[256,1,128]{0,2,1:T(8,128)S(1)} %copy.55, f32[256,1,128]{0,2,1:T(8,128)S(1)} %copy.57, f32[256,66,1]{0,2,1:T(1,128)S(1)} %copy.63, f32[256,66,1]{0,2,1:T(1,128)S(1)} %copy.61, f32[64,128]{1,0:T(8,128)S(1)} %copy-done.8, ...), kind=kLoop, calls=%fused_computation.39 | loop fusion | flops 48234496 | bytes 17272832 | tf_op jit(solution)/shard_map/add | solution.py:30
  50.4 3.3 copy-done.2
  53.7 2.7 collective-permute-start.4
  56.6 2.4 collective-permute-done.4
  59.1 4.6 %collective-permute-done.5 = f32[256,1,128]{2,0,1:T(8,128)S(1)} collective-permute-done((f32[256,1,128]{2,0,1:T(8,128)S(1)}, f32[256,1,128]{2,0,1:T(8,128)S(1)}, u32[]{:S(2)}, u32[]{:S(2)}) %collective-permute-start.5) | collective-permute-done | bytes 131104 | tf_op jit(solution)/shard_map/ppermute | solution.py:15
  63.8 1.5 pad_maximum_fusion.40
  65.2 1.1 collective-permute-start.6
  67.3 2.3 collective-permute-done.6
  69.7 1.0 collective-permute-done.7
  70.8 14.9 %multiply_add_fusion.1 = f32[256,64,128]{0,2,1:T(8,128)S(1)} fusion(f32[256,64,128]{0,2,1:T(8,128)S(1)} %copy-done.3, f32[256,1,128]{0,2,1:T(8,128)S(1)} %copy.65, f32[256,1,128]{0,2,1:T(8,128)S(1)} %copy.67, f32[256,66,1]{0,2,1:T(1,128)S(1)} %copy.73, f32[256,66,1]{0,2,1:T(1,128)S(1)} %copy.71, f32[64,128]{1,0:T(8,128)S(1)} %copy-done.8, ...), kind=kLoop, calls=%fused_computation.38 | loop fusion | flops 48234496 | bytes 17272832 | tf_op jit(solution)/shard_map/add | solution.py:30
  85.8 3.3 copy-done.4
  89.9 1.9 collective-permute-done.8
  91.8 4.6 %collective-permute-done.9 = f32[256,1,128]{2,0,1:T(8,128)S(1)} collective-permute-done((f32[256,1,128]{2,0,1:T(8,128)S(1)}, f32[256,1,128]{2,0,1:T(8,128)S(1)}, u32[]{:S(2)}, u32[]{:S(2)}) %collective-permute-start.9) | collective-permute-done | bytes 131104 | tf_op jit(solution)/shard_map/ppermute | solution.py:15
  96.6 1.5 pad_maximum_fusion.37
  98.0 1.0 collective-permute-start.10
  99.1 1.1 collective-permute-start.11
  100.1 2.3 collective-permute-done.10
  103.5 14.9 %multiply_add_fusion = f32[256,64,128]{0,2,1:T(8,128)S(1)} fusion(f32[256,64,128]{0,2,1:T(8,128)S(1)} %copy-done.5, f32[256,1,128]{0,2,1:T(8,128)S(1)} %copy.75, f32[256,1,128]{0,2,1:T(8,128)S(1)} %copy.77, f32[256,66,1]{0,2,1:T(1,128)S(1)} %copy.83, f32[256,66,1]{0,2,1:T(1,128)S(1)} %copy.81, f32[64,128]{1,0:T(8,128)S(1)} %copy-done.8, ...), kind=kLoop, calls=%fused_computation.37 | loop fusion | flops 48234496 | bytes 17272832 | tf_op jit(solution)/shard_map/add | solution.py:30
  118.4 3.3 copy-done
  122.5 1.9 collective-permute-done.12
  124.5 4.6 %collective-permute-done.13 = f32[256,1,128]{2,0,1:T(8,128)S(1)} collective-permute-done((f32[256,1,128]{2,0,1:T(8,128)S(1)}, f32[256,1,128]{2,0,1:T(8,128)S(1)}, u32[]{:S(2)}, u32[]{:S(2)}) %collective-permute-start.13) | collective-permute-done | bytes 131104 | tf_op jit(solution)/shard_map/ppermute | solution.py:15
  129.2 1.5 pad_maximum_fusion.34
  130.7 1.1 collective-permute-start.14
  132.8 2.3 collective-permute-done.14
  135.2 1.0 collective-permute-done.15
  136.3 15.4 %add_convert_fusion = bf16[256,64,128]{0,2,1:T(8,128)(2,1)S(1)} fusion(f32[256,64,128]{0,2,1:T(8,128)S(1)} %copy-done.1, f32[256,1,128]{0,2,1:T(8,128)S(1)} %copy.85, f32[256,1,128]{0,2,1:T(8,128)S(1)} %copy.87, f32[256,66,1]{0,2,1:T(1,128)S(1)} %copy.93, f32[256,66,1]{0,2,1:T(1,128)S(1)} %copy.91, f32[64,128]{1,0:T(8,128)S(1)} %copy-done.8, ...), kind=kLoop, calls=%fused_computation.36 | loop fusion | flops 50331648 | bytes 13078528 | tf_op jit(solution)/shard_map/convert_element_type | solution.py:51
  151.7 2.0 copy-done.7
  153.7 2.5 convolution_bitcast_fusion
  156.3 121.8 %all-reduce.3.cloned.1.call-done = f32[256,256]{0,1:T(8,128)} async-done(((f32[256,256]{0,1:T(8,128)}), f32[256,256]{0,1:T(8,128)}) %all-reduce.3.cloned.1.call-update) | async-done | bytes 262160 | tf_op jit(solution)/shard_map/psum | solution.py:53
  278.0 1.0 broadcast_multiply_fusion
  279.1 1.0 fusion.1
  280.1 11.7 %cholesky.50 = f32[128,128]{1,0:T(8,128)S(1)} custom-call(f32[128,128]{1,0:T(8,128)S(1)} %cholesky.118), custom_call_target="Cholesky" | custom-call | tf_op jit(solution)/shard_map/jit(cholesky)/cholesky | solution.py:55
  291.9 9.8 %custom-call.14 = f32[1,128,128]{1,2,0:T(8,128)S(1)} custom-call(f32[1,128,128]{2,1,0:T(8,128)S(1)} %get-tuple-element.54), custom_call_target="InvertDiagBlocksLowerTriangular" | custom-call | tf_op jit(solution)/shard_map/jit(cholesky)/cholesky | solution.py:55
  302.2 11.7 %cholesky.105 = f32[128,128]{1,0:T(8,128)S(1)} custom-call(f32[128,128]{1,0:T(8,128)S(1)} %convolution_subtract_fusion.1), custom_call_target="Cholesky" | custom-call | tf_op jit(solution)/shard_map/jit(cholesky)/cholesky | solution.py:55
  316.2 4.3 %while.1 = (s32[]{:T(128)}, f32[256,256]{1,0:T(8,128)S(1)}, s32[2,2]{1,0:T(2,128)S(1)}, f32[2,128,128]{2,1,0:T(8,128)S(1)}, s32[]{:T(128)}) while((s32[]{:T(128)}, f32[256,256]{1,0:T(8,128)S(1)}, s32[2,2]{1,0:T(2,128)S(1)}, f32[2,128,128]{2,1,0:T(8,128)S(1)}, s32[]{:T(128)}) %tuple.41), condition=%wide.while_cond, body=%wide.while_body.sunk | while | flops 2 | bytes 131181 | solution.py:56
  316.9 1.4 bitcast_dynamic-update-slice_fusion.2
  319.0 1.4 bitcast_dynamic-update-slice_fusion.2
  320.4 19.7 %custom-call.15 = f32[2,128,128]{1,2,0:T(8,128)S(1)} custom-call(f32[2,128,128]{2,1,0:T(8,128)S(1)} %get-tuple-element.10), custom_call_target="InvertDiagBlocksLowerTriangular" | custom-call | tf_op jit(solution)/shard_map/triangular_solve | solution.py:56
  341.0 3.5 fusion
  344.5 3.2 copy.103
  348.5 2.3 gather_fusion
  (91 shorter events, 13.2 us)
Async XLA Ops:
  7.2 270.9 %all-reduce.3.cloned.1.call-start = ((), (), s32[]{:S(2)}) async-start(), calls=%async_computation | async-start | bytes 524288 | tf_op jit(solution)/shard_map/psum | solution.py:53
  15.0 12.3 %collective-permute-start = (f32[256,1,128]{2,0,1:T(8,128)S(1)}, f32[256,1,128]{2,0,1:T(8,128)S(1)}, u32[]{:S(2)}, u32[]{:S(2)}) collective-permute-start(f32[256,1,128]{2,0,1:T(8,128)S(1)} %copy.54), channel_id=1, source_target_pairs={{2,0},{4,2},{6,4},{8,6},{10,8},{12,10},{14,12},{16,14},{18,16},{20... | collective-permute-start | bytes 393224 | tf_op jit(solution)/shard_map/ppermute | solution.py:18
  20.6 14.8 %copy-start.8 = (f32[64,128]{1,0:T(8,128)S(1)}, f32[64,128]{1,0:T(8,128)}, u32[]{:S(2)}) copy-start(f32[64,128]{1,0:T(8,128)} %param.7) | copy-start | bytes 98308
  20.6 14.8 %copy-start.9 = (f32[64,128]{1,0:T(8,128)S(1)}, f32[64,128]{1,0:T(8,128)}, u32[]{:S(2)}) copy-start(f32[64,128]{1,0:T(8,128)} %param.6) | copy-start | bytes 98308
  20.7 14.7 %copy-start.10 = (f32[64,128]{1,0:T(8,128)S(1)}, f32[64,128]{1,0:T(8,128)}, u32[]{:S(2)}) copy-start(f32[64,128]{1,0:T(8,128)} %param.5) | copy-start | bytes 98308
  20.7 7.1 %collective-permute-start.1 = (f32[256,1,128]{2,0,1:T(8,128)S(1)}, f32[256,1,128]{2,0,1:T(8,128)S(1)}, u32[]{:S(2)}, u32[]{:S(2)}) collective-permute-start(f32[256,1,128]{2,0,1:T(8,128)S(1)} %copy.56), channel_id=1, source_target_pairs={{0,2},{2,4},{4,6},{6,8},{8,10},{10,12},{12,14},{14,16},{16,18},{18... | collective-permute-start | bytes 393224 | tf_op jit(solution)/shard_map/ppermute | solution.py:15
  27.9 7.5 %copy-start.6 = (f32[256,64,128]{0,2,1:T(8,128)S(1)}, f32[256,64,128]{0,2,1:T(8,128)}, u32[]{:S(2)}) copy-start(f32[256,64,128]{0,2,1:T(8,128)} %convert_element_type.11) | copy-start | bytes 25165828
  29.4 4.4 %collective-permute-start.2 = (f32[256,66,1]{0,1,2:T(8,128)S(1)}, f32[256,66,1]{0,1,2:T(8,128)S(1)}, u32[]{:S(2)}, u32[]{:S(2)}) collective-permute-start(f32[256,66,1]{0,1,2:T(8,128)S(1)} %copy.60), channel_id=1, source_target_pairs={{1,0},{0,1},{3,2},{2,3},{5,4},{4,5},{7,6},{6,7},{9,8},{8,9},{11,10... | collective-permute-start | bytes 202760 | tf_op jit(solution)/shard_map/ppermute | solution.py:18
  30.9 4.4 %collective-permute-start.3 = (f32[256,66,1]{0,1,2:T(8,128)S(1)}, f32[256,66,1]{0,1,2:T(8,128)S(1)}, u32[]{:S(2)}, u32[]{:S(2)}) collective-permute-start(f32[256,66,1]{0,1,2:T(8,128)S(1)} %copy.62), channel_id=1, source_target_pairs={{0,1},{1,0},{2,3},{3,2},{4,5},{5,4},{6,7},{7,6},{8,9},{9,8},{10,11... | collective-permute-start | bytes 202760 | tf_op jit(solution)/shard_map/ppermute | solution.py:15
  50.4 3.3 copy-start.2
  53.7 5.2 %collective-permute-start.4 = (f32[256,1,128]{2,0,1:T(8,128)S(1)}, f32[256,1,128]{2,0,1:T(8,128)S(1)}, u32[]{:S(2)}, u32[]{:S(2)}) collective-permute-start(f32[256,1,128]{2,0,1:T(8,128)S(1)} %copy.64), channel_id=1, source_target_pairs={{2,0},{4,2},{6,4},{8,6},{10,8},{12,10},{14,12},{16,14},{18,16},{20... | collective-permute-start | bytes 393224 | tf_op jit(solution)/shard_map/ppermute | solution.py:18
  56.5 7.1 %collective-permute-start.5 = (f32[256,1,128]{2,0,1:T(8,128)S(1)}, f32[256,1,128]{2,0,1:T(8,128)S(1)}, u32[]{:S(2)}, u32[]{:S(2)}) collective-permute-start(f32[256,1,128]{2,0,1:T(8,128)S(1)} %copy.66), channel_id=1, source_target_pairs={{0,2},{2,4},{4,6},{6,8},{8,10},{10,12},{12,14},{14,16},{16,18},{18... | collective-permute-start | bytes 393224 | tf_op jit(solution)/shard_map/ppermute | solution.py:15
  63.8 7.0 %copy-start.3 = (f32[256,64,128]{0,2,1:T(8,128)S(1)}, f32[256,64,128]{0,2,1:T(8,128)}, u32[]{:S(2)}) copy-start(f32[256,64,128]{0,2,1:T(8,128)} %copy-done.2) | copy-start | bytes 25165828
  65.2 4.4 %collective-permute-start.6 = (f32[256,66,1]{0,1,2:T(8,128)S(1)}, f32[256,66,1]{0,1,2:T(8,128)S(1)}, u32[]{:S(2)}, u32[]{:S(2)}) collective-permute-start(f32[256,66,1]{0,1,2:T(8,128)S(1)} %copy.70), channel_id=1, source_target_pairs={{1,0},{0,1},{3,2},{2,3},{5,4},{4,5},{7,6},{6,7},{9,8},{8,9},{11,10... | collective-permute-start | bytes 202760 | tf_op jit(solution)/shard_map/ppermute | solution.py:18
  66.4 4.4 %collective-permute-start.7 = (f32[256,66,1]{0,1,2:T(8,128)S(1)}, f32[256,66,1]{0,1,2:T(8,128)S(1)}, u32[]{:S(2)}, u32[]{:S(2)}) collective-permute-start(f32[256,66,1]{0,1,2:T(8,128)S(1)} %copy.72), channel_id=1, source_target_pairs={{0,1},{1,0},{2,3},{3,2},{4,5},{5,4},{6,7},{7,6},{8,9},{9,8},{10,11... | collective-permute-start | bytes 202760 | tf_op jit(solution)/shard_map/ppermute | solution.py:15
  85.8 3.3 copy-start.4
  89.1 2.6 collective-permute-start.8
  89.3 7.1 %collective-permute-start.9 = (f32[256,1,128]{2,0,1:T(8,128)S(1)}, f32[256,1,128]{2,0,1:T(8,128)S(1)}, u32[]{:S(2)}, u32[]{:S(2)}) collective-permute-start(f32[256,1,128]{2,0,1:T(8,128)S(1)} %copy.76), channel_id=1, source_target_pairs={{0,2},{2,4},{4,6},{6,8},{8,10},{10,12},{12,14},{14,16},{16,18},{18... | collective-permute-start | bytes 393224 | tf_op jit(solution)/shard_map/ppermute | solution.py:15
  96.5 6.9 %copy-start.5 = (f32[256,64,128]{0,2,1:T(8,128)S(1)}, f32[256,64,128]{0,2,1:T(8,128)}, u32[]{:S(2)}) copy-start(f32[256,64,128]{0,2,1:T(8,128)} %copy-done.4) | copy-start | bytes 25165828
  98.0 4.4 %collective-permute-start.10 = (f32[256,66,1]{0,1,2:T(8,128)S(1)}, f32[256,66,1]{0,1,2:T(8,128)S(1)}, u32[]{:S(2)}, u32[]{:S(2)}) collective-permute-start(f32[256,66,1]{0,1,2:T(8,128)S(1)} %copy.80), channel_id=1, source_target_pairs={{1,0},{0,1},{3,2},{2,3},{5,4},{4,5},{7,6},{6,7},{9,8},{8,9},{11,10... | collective-permute-start | bytes 202760 | tf_op jit(solution)/shard_map/ppermute | solution.py:18
  99.1 4.4 %collective-permute-start.11 = (f32[256,66,1]{0,1,2:T(8,128)S(1)}, f32[256,66,1]{0,1,2:T(8,128)S(1)}, u32[]{:S(2)}, u32[]{:S(2)}) collective-permute-start(f32[256,66,1]{0,1,2:T(8,128)S(1)} %copy.82), channel_id=1, source_target_pairs={{0,1},{1,0},{2,3},{3,2},{4,5},{5,4},{6,7},{7,6},{8,9},{9,8},{10,11... | collective-permute-start | bytes 202760 | tf_op jit(solution)/shard_map/ppermute | solution.py:15
  118.4 3.3 copy-start
  121.8 2.6 collective-permute-start.12
  122.0 7.1 %collective-permute-start.13 = (f32[256,1,128]{2,0,1:T(8,128)S(1)}, f32[256,1,128]{2,0,1:T(8,128)S(1)}, u32[]{:S(2)}, u32[]{:S(2)}) collective-permute-start(f32[256,1,128]{2,0,1:T(8,128)S(1)} %copy.86), channel_id=1, source_target_pairs={{0,2},{2,4},{4,6},{6,8},{8,10},{10,12},{12,14},{14,16},{16,18},{18... | collective-permute-start | bytes 393224 | tf_op jit(solution)/shard_map/ppermute | solution.py:15
  129.2 7.0 %copy-start.1 = (f32[256,64,128]{0,2,1:T(8,128)S(1)}, f32[256,64,128]{0,2,1:T(8,128)}, u32[]{:S(2)}) copy-start(f32[256,64,128]{0,2,1:T(8,128)} %copy-done) | copy-start | bytes 25165828
  130.7 4.4 %collective-permute-start.14 = (f32[256,66,1]{0,1,2:T(8,128)S(1)}, f32[256,66,1]{0,1,2:T(8,128)S(1)}, u32[]{:S(2)}, u32[]{:S(2)}) collective-permute-start(f32[256,66,1]{0,1,2:T(8,128)S(1)} %copy.90), channel_id=1, source_target_pairs={{1,0},{0,1},{3,2},{2,3},{5,4},{4,5},{7,6},{6,7},{9,8},{8,9},{11,10... | collective-permute-start | bytes 202760 | tf_op jit(solution)/shard_map/ppermute | solution.py:18
  131.8 4.4 %collective-permute-start.15 = (f32[256,66,1]{0,1,2:T(8,128)S(1)}, f32[256,66,1]{0,1,2:T(8,128)S(1)}, u32[]{:S(2)}, u32[]{:S(2)}) collective-permute-start(f32[256,66,1]{0,1,2:T(8,128)S(1)} %copy.92), channel_id=1, source_target_pairs={{0,1},{1,0},{2,3},{3,2},{4,5},{5,4},{6,7},{7,6},{8,9},{9,8},{10,11... | collective-permute-start | bytes 202760 | tf_op jit(solution)/shard_map/ppermute | solution.py:15
  151.7 2.0 copy-start.7
Sparse Core Ops, SparseCore 0:
  156.3 121.6 all-reduce.2
where the time goes:
time: 359 us; the launch traced here: 358 us
  waiting for transfers between devices  156 us (43%)
  other arithmetic  128 us (36%)
  local copies, waits for them, and re-layouts  32.9 us (9%)
  starting transfers between devices  17.9 us (5%)
  between operations  15.9 us (4%)
  matrix products  7.3 us (2%)
    psum x1, waiting for transfers between devices, per_device(): gram = lax.psum(inner_products(evolved, evolved), ('gx', 'gy'))  122 us
    add x3, other arithmetic, advance(): centre + 0.2 * (north + south + east + west - 4.0 * centre)  44.8 us
    another operation x6, other arithmetic, per_device(): lower = jnp.linalg.cholesky(gram)  34 us
    unnamed x25, local copies, waits for them, and re-layouts  22.7 us
    another operation x3, other arithmetic, per_device(): lax.linalg.triangular_solve(lower, jnp.eye(fields, dtype=jnp.float32), le...  19.7 us
    ppermute x8, waiting for transfers between devices, extended(): lax.ppermute(lax.slice_in_dim(block, block.shape[dim] - width, None, axis...  18.5 us
    convert_element_type x1, other arithmetic, per_device(): evolved = state.astype(jnp.bfloat16).reshape(fields, rows * cols)  15.4 us
    ppermute x8, waiting for transfers between devices, extended(): lax.ppermute(lax.slice_in_dim(block, 0, width, axis=dim), axis, backward)  15.4 us
  transfers between devices with their start and end apart: 17, of which 16 were waited for; matrix products, arithmetic and copies ran while one was open for 2% of the time, Pallas kernels for 0%

commit v1 on v0

v1 whole, which is shorter than its diff:
```python
import functools

import jax
import jax.numpy as jnp
from jax import lax
from jax.experimental import pallas as pl
from jax.experimental.pallas import tpu as pltpu
from jax.sharding import PartitionSpec as P

F32 = jnp.float32
BF16 = jnp.bfloat16
SUBSTEPS = 4
LANES = 128
HALO = SUBSTEPS
GROUP = 8
EDGE = 2 * HALO
PACKED = 16


def spread(row):
    return jnp.broadcast_to(row, (8, 128))

def factor_block(v):
    sub = lax.broadcasted_iota(jnp.int32, (8, 128), 0)
    n = 8
    for p in range(16):
        c0 = p * n
        diag = v[c0:c0 + n, 0:128]
        column = [jnp.broadcast_to(diag[:, c0 + j:c0 + j + 1], (n, 128)) for j in range(n)]
        d = {(i, j): spread(column[j][i:i + 1]) for j in range(n) for i in range(j + 1)}
        inv, r, x = {}, {}, {}
        for j in range(n):
            inv[j] = lax.rsqrt(d[j, j])
            for k in range(j + 1, n):
                r[j, k] = d[j, k] * inv[j]
            for i in range(j + 1, n):
                for k in range(i, n):
                    d[i, k] = d[i, k] - r[j, i] * r[j, k]
        for j in range(n):
            x[j, j] = inv[j]
            for i in range(j + 1, n):
                acc = r[j, i] * x[j, j]
                for k in range(j + 1, i):
                    acc = acc + r[k, i] * x[k, j]
                x[i, j] = -(inv[i] * acc)
        dinv = {}
        for a in range(n):
            for b in range(a, n):
                acc = x[b, a] * x[b, b]
                for m in range(b + 1, n):
                    acc = acc + x[m, a] * x[m, b]
                dinv[a, b] = dinv[b, a] = acc
        ys = []
        for t in range(3):
            cols = slice(128 * t, 128 * t + 128)
            rows = [spread(v[c0 + k:c0 + k + 1, cols]) for k in range(n)]
            ys.append([sum(dinv[a, k] * rows[k] for k in range(n)) for a in range(n)])
            out = x[0, 0] * rows[0]
            for i in range(1, n):
                out = jnp.where(sub == i, sum(x[i, k] * rows[k] for k in range(i + 1)), out)
            v[c0:c0 + n, cols] = out
        for g in range(p + 1, 16):
            ag = v[n * g:n * g + n, 0:128]
            ab = [jnp.broadcast_to(ag[:, c0 + j:c0 + j + 1], (n, 128)) for j in range(n)]
            for t in range(3):
                cols = slice(128 * t, 128 * t + 128)
                acc = v[n * g:n * g + n, cols]
                for j in range(n):
                    acc = acc - ab[j] * ys[t][j]
                v[n * g:n * g + n, cols] = acc

def dot_t(a, b):
    return lax.dot_general(a, b, (((0,), (0,)), ((), ())), precision=lax.Precision.HIGHEST, preferred_element_type=F32)

def factor_kernel(total, pay, factor, inverse, exponents, v):
    h = 128
    ri = lax.broadcasted_iota(jnp.int32, (h, h), 0)
    ci = lax.broadcasted_iota(jnp.int32, (h, h), 1)
    eye = jnp.where(ri == ci, 1.0, 0.0).astype(F32)
    fold = pay[0:h, :] / total
    turned = fold.T
    diag0 = jnp.broadcast_to(pay[2 * h:2 * h + 1, :], (h, h)) / total
    v[:, 0:h] = jnp.where(ri == ci, diag0, jnp.where(ri < ci, turned, fold))
    v[:, h:2 * h] = pay[h:2 * h, :] / total
    v[:, 2 * h:3 * h] = eye
    rest = jnp.where(ri <= ci, fold, turned)
    factor_block(v)
    r00 = jnp.where(ri <= ci, v[:, 0:h], 0.0)
    r01 = v[:, h:2 * h]
    l00 = jnp.where(ri >= ci, v[:, 2 * h:3 * h], 0.0)
    factor[0:h, 0:h] = r00
    factor[0:h, h:2 * h] = r01
    inverse[0:h, 0:h] = l00.astype(jnp.bfloat16)
    inverse[0:h, h:2 * h] = jnp.zeros((h, h), jnp.bfloat16)
    exponents[:, 0:h] = jnp.log(jnp.sum(r00 * eye, axis=0, keepdims=True))
    v[:, 0:h] = rest - dot_t(r01, r01)
    v[:, h:2 * h] = -dot_t(r01, l00)
    v[:, 2 * h:3 * h] = eye
    factor_block(v)
    r11 = jnp.where(ri <= ci, v[:, 0:h], 0.0)
    factor[h:2 * h, 0:h] = jnp.zeros((h, h), F32)
    factor[h:2 * h, h:2 * h] = r11
    inverse[h:2 * h, 0:h] = v[:, h:2 * h].astype(jnp.bfloat16)
    inverse[h:2 * h, h:2 * h] = jnp.where(ri >= ci, v[:, 2 * h:3 * h], 0.0).astype(jnp.bfloat16)
    exponents[:, h:2 * h] = jnp.log(jnp.sum(r11 * eye, axis=0, keepdims=True))

def factorize(pay, total):
    return pl.pallas_call(
        functools.partial(factor_kernel, total),
        out_shape=(jax.ShapeDtypeStruct((256,256),F32), jax.ShapeDtypeStruct((256,256),jnp.bfloat16), jax.ShapeDtypeStruct((1,256),F32)),
        scratch_shapes=[pltpu.VMEM((128,384),F32)],
        compiler_params=pltpu.CompilerParams(vmem_limit_bytes=16<<20),
    )(pay)

def arrange_kernel(tangent, arranged, wide):
    fields, rows, lanes = tangent.shape
    block = lax.broadcasted_iota(jnp.int32, (PACKED, lanes), 1) // EDGE

    def spread_field(f, carry):
        values = tangent[f].astype(F32)
        for part in range(rows // GROUP):
            wide[pl.ds(f + fields * GROUP * part, GROUP, stride=fields), :] = values[GROUP * part:GROUP * (part + 1)]
        return carry

    lax.fori_loop(0, fields, spread_field, 0, unroll=8)

    def pack_row(r, carry):
        start = pl.multiple_of(r * fields, fields)
        arranged[r, 0:fields] = wide[pl.ds(start, fields), :].astype(BF16)
        edge = None
        for b in range(fields // PACKED):
            part = wide[pl.ds(start + PACKED * b, PACKED), :]
            moved = pltpu.roll(part, (EDGE * b + HALO) % lanes, 1)
            edge = moved if edge is None else jnp.where(block == b, moved, edge)
        arranged[r, fields:fields + PACKED] = edge.astype(BF16)
        return carry

    lax.fori_loop(0, rows, pack_row, 0)


def arrange(tangent):
    fields, rows, lanes = tangent.shape
    step = 16
    return pl.pallas_call(
        arrange_kernel,
        grid=(rows // step,),
        in_specs=[pl.BlockSpec((fields, step, lanes), lambda i: (0, i, 0))],
        out_specs=pl.BlockSpec((step, fields + PACKED, lanes), lambda i: (i, 0, 0)),
        out_shape=jax.ShapeDtypeStruct((rows, fields + PACKED, lanes), BF16),
        scratch_shapes=[pltpu.VMEM((step * fields, lanes), F32)],
        compiler_params=pltpu.CompilerParams(vmem_limit_bytes=32 << 20),
    )(tangent)


def evolve_kernel(own, low, high, west, east, low_west, low_east, high_west, high_east, inner, left, right,
                  evolved, payload, first, second, gram):
    rows, _, lanes = own.shape
    fields = own.shape[1] - PACKED
    lane = lax.broadcasted_iota(jnp.int32, (GROUP, lanes), 1)
    in_edge = lane % EDGE
    lane16 = lax.broadcasted_iota(jnp.int32, (PACKED, lanes), 1) % EDGE
    west_at, east_at = fields, fields + PACKED

    def fill(target, mine, from_west, from_east):
        first[target, 0:fields] = mine[0:fields].astype(F32)
        edge = mine[fields:fields + PACKED].astype(F32)
        first[target, west_at:west_at + PACKED] = jnp.where(lane16 < HALO, from_west.astype(F32), edge)
        first[target, east_at:east_at + PACKED] = jnp.where(lane16 < HALO, edge, from_east.astype(F32))

    for i in range(HALO):
        fill(i, low[i], low_west[i], low_east[i])
        fill(HALO + rows + i, high[i], high_west[i], high_east[i])

    def fill_own(r, carry):
        fill(HALO + r, own[r], west[r], east[r])
        return carry

    lax.fori_loop(0, rows, fill_own, 0)

    def coefficients(table, r):
        return [jnp.broadcast_to(table[m, pl.ds(r, 1)], (GROUP, lanes)) for m in range(5)]

    def combine(coef, c, n, s, e, w):
        return coef[0] * c + (coef[1] * n + coef[2] * s) + (coef[3] * e + coef[4] * w)

    def joints(source, r):
        out = []
        for h in range(PACKED // GROUP):
            from_west = source[r, west_at + GROUP * h:west_at + GROUP * (h + 1)]
            from_east = source[r, east_at + GROUP * h:east_at + GROUP * (h + 1)]
            out.append(jnp.where(in_edge == HALO - 1, from_west, pltpu.roll(from_east, lanes - 2, 1)))
        return out

    def interior(source, r, k, coef, joint):
        at = slice(GROUP * k, GROUP * (k + 1))
        b, h = divmod(k, PACKED // GROUP)
        beyond = pltpu.roll(joint[h], (lanes - (EDGE * b + HALO - 1)) % lanes, 1)
        c = source[r, at]
        e = jnp.where(lane == lanes - 1, beyond, pltpu.roll(c, lanes - 1, 1))
        w = jnp.where(lane == 0, beyond, pltpu.roll(c, 1, 1))
        return combine(coef, c, source[r + 1, at], source[r - 1, at], e, w)

    def substep(source, target, step):
        def row(r, carry):
            coef = coefficients(inner, r)
            joint = joints(source, r)
            for k in range(fields // GROUP):
                target[r, GROUP * k:GROUP * (k + 1)] = interior(source, r, k, coef, joint)
            for table, at in ((left, west_at), (right, east_at)):
                coef = coefficients(table, r)
                for h in range(PACKED // GROUP):
                    where = slice(at + GROUP * h, at + GROUP * (h + 1))
                    c = source[r, where]
                    target[r, where] = combine(
                        coef, c, source[r + 1, where], source[r - 1, where],
                        pltpu.roll(c, lanes - 1, 1), pltpu.roll(c, 1, 1))
            return carry

        lax.fori_loop(step, 2 * HALO + rows - step, row, 0)

    buffers = [first, second]
    for step in range(1, SUBSTEPS):
        substep(buffers[(step - 1) % 2], buffers[step % 2], step)
    source = buffers[(SUBSTEPS - 1) % 2]
    gram[...] = jnp.zeros_like(gram)
    chunk = 8

    def last_chunk(q, carry):
        def row(i, inner_carry):
            r = q * chunk + i
            coef = coefficients(inner, HALO + r)
            joint = joints(source, HALO + r)
            at = pl.multiple_of(r * lanes, lanes)
            for k in range(0, fields // GROUP, 2):
                pair = [interior(source, HALO + r, k + h, coef, joint) for h in range(2)]
                evolved[GROUP * k:GROUP * (k + 2), pl.ds(at, lanes)] = jnp.concatenate(pair, axis=0).astype(BF16)
            return inner_carry

        lax.fori_loop(0, chunk, row, 0)
        part = evolved[:, pl.ds(pl.multiple_of(q * chunk * lanes, chunk * lanes), chunk * lanes)]
        gram[...] += lax.dot_general(part, part, (((1,), (1,)), ((), ())), preferred_element_type=F32)
        return carry

    lax.fori_loop(0, rows // chunk, last_chunk, 0)
    h = fields // 2
    ri = lax.broadcasted_iota(jnp.int32, (h, h), 0)
    ci = lax.broadcasted_iota(jnp.int32, (h, h), 1)
    corner = gram[0:h, 0:h]
    payload[0:h] = jnp.where(ri <= ci, gram[h:2 * h, h:2 * h], corner)
    payload[h:2 * h] = gram[0:h, h:2 * h]
    diagonal = jnp.sum(jnp.where(ri == ci, corner, 0.0), axis=0, keepdims=True)
    payload[2 * h:] = jnp.broadcast_to(diagonal, (PACKED, h))


def evolve(own, halos, tables):
    rows, tall, lanes = own.shape
    fields = tall - PACKED
    extended = (rows + 2 * HALO, fields + 2 * PACKED, lanes)
    return pl.pallas_call(
        evolve_kernel,
        out_shape=(
            jax.ShapeDtypeStruct((fields, rows * lanes), BF16),
            jax.ShapeDtypeStruct((fields + PACKED, fields // 2), F32),
        ),
        scratch_shapes=[
            pltpu.VMEM(extended, F32),
            pltpu.VMEM(extended, F32),
            pltpu.VMEM((fields, fields), F32),
        ],
        compiler_params=pltpu.CompilerParams(vmem_limit_bytes=56 << 20),
    )(own, *halos, *tables)


def project_kernel(inverse, evolved, basis, wide):
    fields, rows, lanes = basis.shape
    for r in range(0, rows, 2):
        part = jnp.dot(inverse[...], evolved[:, r * lanes:(r + 2) * lanes], preferred_element_type=F32)
        for i in range(2):
            wide[pl.ds(r + i, fields, stride=rows), :] = part[:, i * lanes:(i + 1) * lanes]
    basis[...] = wide[...].reshape(fields, rows, lanes).astype(BF16)


def project(inverse, evolved, rows):
    fields, cells = evolved.shape
    lanes = cells // rows
    step = 16
    return pl.pallas_call(
        project_kernel,
        grid=(rows // step,),
        in_specs=[
            pl.BlockSpec((fields, fields), lambda i: (0, 0)),
            pl.BlockSpec((fields, step * lanes), lambda i: (0, i)),
        ],
        out_specs=pl.BlockSpec((fields, step, lanes), lambda i: (0, i, 0)),
        out_shape=jax.ShapeDtypeStruct((fields, rows, lanes), BF16),
        scratch_shapes=[pltpu.VMEM((step * fields, lanes), F32)],
        compiler_params=pltpu.CompilerParams(vmem_limit_bytes=32 << 20),
    )(inverse, evolved)


def shifted(block, down, right):
    nx, ny = lax.axis_size("gx"), lax.axis_size("gy")
    pairs = []
    for x in range(nx):
        for y in range(ny):
            pairs.append((x * ny + y, (x + down) % nx * ny + (y + right) % ny))
    return lax.ppermute(block, ("gx", "gy"), pairs)


def swapped(block, axis, bit):
    return lax.ppermute(block, axis, [(i, i ^ bit) for i in range(lax.axis_size(axis))])


def summed(payload):
    nx, ny = lax.axis_size("gx"), lax.axis_size("gy")
    if nx & (nx - 1) or ny & (ny - 1) or nx < 2:
        return lax.psum(payload, ("gx", "gy"))
    half = payload.shape[0] // 2
    side = lax.axis_index("gx") % 2
    kept = lax.dynamic_slice_in_dim(payload, side * half, half, 0)
    given = lax.dynamic_slice_in_dim(payload, (1 - side) * half, half, 0)
    total = kept + swapped(given, "gx", 1)
    for axis, bits in (("gy", range(ny.bit_length() - 1)), ("gx", range(1, nx.bit_length() - 1))):
        for bit in bits:
            total = total + swapped(total, axis, 1 << bit)
    other = swapped(total, "gx", 1)
    return jnp.where(side == 0, jnp.concatenate([total, other]), jnp.concatenate([other, total]))


def stencil_tables(courant_x, courant_y, growth, two):
    block = jnp.stack([courant_x, courant_y, growth])
    last, begin = block[:, :, -HALO:], block[:, :, :HALO]
    if two:
        both = shifted(jnp.concatenate([last, begin], axis=2), 0, 1)
        low, high = both[:, :, :HALO], both[:, :, HALO:]
    else:
        low, high = shifted(last, 0, 1), shifted(begin, 0, -1)
    block = jnp.concatenate([low, block, high], axis=2)
    low = shifted(block[:, -HALO:], 1, 0)
    high = shifted(block[:, :HALO], -1, 0)
    block = jnp.concatenate([low, block, high], axis=1)
    cx, cy, gr = block[0], block[1], block[2]
    table = jnp.stack([0.2 + gr, 0.2 - cx, 0.2 + cx, 0.2 - cy, 0.2 + cy])
    times = LANES // EDGE
    return (
        table[:, :, HALO:-HALO],
        jnp.tile(table[:, :, :EDGE], (1, 1, times)),
        jnp.tile(table[:, :, -EDGE:], (1, 1, times)),
    )


def per_device(tangent, courant_x, courant_y, growth):
    fields, rows, cols = tangent.shape
    nx, ny = lax.axis_size("gx"), lax.axis_size("gy")
    two = ny == 2
    tables = stencil_tables(courant_x, courant_y, growth, two)
    own = arrange(tangent)
    low = shifted(own[-HALO:], 1, 0)
    high = shifted(own[:HALO], -1, 0)
    edge = own[:, fields:]

    def sideways(block, down):
        west = shifted(block, down, 1)
        return west, west if two else shifted(block, down, -1)

    west, east = sideways(edge, 0)
    low_west, low_east = sideways(edge[-HALO:], 1)
    high_west, high_east = sideways(edge[:HALO], -1)
    halos = (low, high, west, east, low_west, low_east, high_west, high_east)
    evolved, payload = evolve(own, halos, tables)
    total = float(rows * nx * cols * ny)
    factor, inverse, exponents = factorize(summed(payload), total)
    return project(inverse, evolved, rows), factor, exponents.reshape(fields)


def solution(mesh):
    placed = (P(None, "gx", "gy"), P("gx", "gy"), P("gx", "gy"), P("gx", "gy"))
    return jax.shard_map(
        per_device,
        mesh=mesh,
        in_specs=placed,
        out_specs=(P(None, "gx", "gy"), P(), P()),
        check_vma=False,
    )
```

time: 359 us -> 147 us (0.41)
  waiting for transfers between devices: 156 us -> 25.9 us
  other arithmetic: 128 us -> 2.13 us
  Pallas kernels: 0 us -> 91.3 us
  local copies, waits for them, and re-layouts: 32.9 us -> 9.73 us
  between operations: 15.9 us -> 0.92 us
  matrix products: 7.3 us -> 0 us
    psum x1 -> x0, waiting for transfers between devices: 122 us -> none  [per_device(): gram = lax.psum(inner_products(evolved, evolved), ('gx', 'gy'))]
    pallas_call x0 -> x4, Pallas kernels: none -> 91.3 us  [the longest x1 62 us: evolve(): pl.pallas_call(evolve_kernel, out_shape=(jax.ShapeDtypeStruct((fields, ro...]
    another operation x9 -> x2, other arithmetic: 53.7 us -> 0.81 us  [the longest x1 0.8 us: stencil_tables(): block = jnp.stack([courant_x, courant_y, growth])]
    add x3 -> x5, other arithmetic: 44.8 us -> 0.93 us  [the longest x1 0.89 us: summed(): total = kept + swapped(given, 'gx', 1)]
    convert_element_type x2 -> x0, other arithmetic: 22 us -> none  [the longest x1 15.4 us: per_device(): evolved = state.astype(jnp.bfloat16).reshape(fields, rows * cols)]
    unnamed x25 -> x22, local copies, waits for them, and re-layouts: 22.7 us -> 5.87 us
    ppermute x16 -> x14, waiting for transfers between devices: 33.9 us -> 25.9 us  [the longest x6 21.2 us: swapped(): lax.ppermute(block, axis, [(i, i ^ bit) for i in range(lax.axis_size(axis...]
    dot_general x2 -> x0, matrix products: 5.99 us -> none  [the longest x1 3.48 us: per_device(): basis = jnp.dot(inverse, evolved, preferred_element_type=jnp.float32)]
  transfers between devices with their start and end apart: 17 -> 14, of which waited for: 16 -> 8; matrix products, arithmetic and copies ran while one was open for 2% -> 2% of each run, Pallas kernels for 0% -> 9%
where the time goes in v1:
time: 147 us; the launch traced here: 146 us
  Pallas kernels  91.3 us (62%)
  waiting for transfers between devices  25.9 us (18%)
  starting transfers between devices  16.3 us (11%)
  local copies, waits for them, and re-layouts  9.73 us (7%)
  other arithmetic  2.13 us (1%)
    pallas_call x1, Pallas kernels, evolve(): pl.pallas_call(evolve_kernel, out_shape=(jax.ShapeDtypeStruct((fields, ro...  62 us
    ppermute x6, waiting for transfers between devices, swapped(): lax.ppermute(block, axis, [(i, i ^ bit) for i in range(lax.axis_size(axis...  21.2 us
    ppermute x8, starting transfers between devices, shifted(): return lax.ppermute(block, ('gx', 'gy'), pairs)  16 us
    pallas_call x1, Pallas kernels, arrange(): pl.pallas_call(arrange_kernel, grid=(rows // step,), in_specs=[pl.BlockSp...  13 us
    pallas_call x1, Pallas kernels, factorize(): pl.pallas_call(functools.partial(factor_kernel, total), out_shape=(jax.Sh...  11.6 us
    unnamed x22, local copies, waits for them, and re-layouts  5.87 us
    pallas_call x1, Pallas kernels, project(): pl.pallas_call(project_kernel, grid=(rows // step,), in_specs=[pl.BlockSp...  4.79 us
    ppermute x8, waiting for transfers between devices, shifted(): return lax.ppermute(block, ('gx', 'gy'), pairs)  4.76 us
  transfers between devices with their start and end apart: 14, of which 8 were waited for; matrix products, arithmetic and copies ran while one was open for 2% of the time, Pallas kernels for 9%

profile of v1, /device:TPU:0, one launch (start us, length us, event | category | flops | bytes accessed | tf_op | source)
XLA Modules:
  0.0 146.4 jit_solution(2873210746937319115)
XLA Ops:
  0.6 0.8 pad_maximum_fusion.1
  1.4 0.1 fusion.5
  1.5 0.1 pad_maximum_fusion.2
  1.6 3.0 %collective-permute-start.5 = (f32[3,64,8]{2,1,0:T(8,128)S(1)}, f32[3,64,8]{2,1,0:T(8,128)S(1)}, u32[]{:S(2)}, u32[]{:S(2)}) collective-permute-start(f32[3,64,8]{2,1,0:T(8,128)S(1)} %pad_maximum_fusion.2), channel_id=1, source_target_pairs={{0,1},{1,0},{2,3},{3,2},{4,5},{5,4},{6,7},{7,6},{8,9},{9,8},{10,11... | collective-permute-start | bytes 18440 | tf_op jit(solution)/shard_map/ppermute | solution.py:307
  4.6 2.2 %copy-done.1 = bf16[256,64,128]{2,1,0:T(8,128)(2,1)S(1)} copy-done((bf16[256,64,128]{2,1,0:T(8,128)(2,1)S(1)}, bf16[256,64,128]{2,1,0:T(8,128)(2,1)}, u32[]{:S(2)}) %copy-start.1) | copy-done | bytes 4194328
  6.8 13.0 %shard_map.67.own = bf16[64,272,128]{2,1,0:T(8,128)(2,1)S(1)} custom-call(bf16[256,64,128]{2,1,0:T(8,128)(2,1)S(1)} %copy-done.1), custom_call_target="tpu_custom_call" | custom-call | tf_op jit(solution)/shard_map/pallas_call | solution.py:144
  19.8 0.1 collective-permute-start
  19.9 4.4 %collective-permute-start.1 = (bf16[4,272,128]{2,1,0:T(8,128)(2,1)S(1)}, bf16[4,272,128]{2,1,0:T(8,128)(2,1)S(1)}, u32[]{:S(2)}, u32[]{:S(2)}) collective-permute-start(bf16[4,272,128]{2,1,0:T(8,128)(2,1)S(1)} %get-tuple-element.15), channel_id=1, source_target_pairs={{0,30},{1,31},{2,0},{3,1},{4,2},{5,3},{6,4},{7,5},{8,6},{9,7},{10,... | collective-permute-start | bytes 835592 | tf_op jit(solution)/shard_map/ppermute | solution.py:307
  24.3 0.0 collective-permute-done.5
  24.3 0.1 fusion.4
  24.5 0.1 pad_maximum_fusion.7
  24.6 0.1 collective-permute-start.6
  24.6 4.4 %collective-permute-start.7 = (f32[3,4,136]{2,1,0:T(4,128)S(1)}, f32[3,4,136]{2,1,0:T(4,128)S(1)}, u32[]{:S(2)}, u32[]{:S(2)}) collective-permute-start(f32[3,4,136]{2,1,0:T(4,128)S(1)} %get-tuple-element.20), channel_id=1, source_target_pairs={{0,30},{1,31},{2,0},{3,1},{4,2},{5,3},{6,4},{7,5},{8,6},{9,7},{10,... | collective-permute-start | bytes 19592 | tf_op jit(solution)/shard_map/ppermute | solution.py:307
  29.1 0.0 collective-permute-start.3
  29.1 1.4 collective-permute-done.6
  30.5 4.0 %collective-permute-start.4 = (bf16[4,16,128]{2,1,0:T(8,128)(2,1)S(1)}, bf16[4,16,128]{2,1,0:T(8,128)(2,1)S(1)}, u32[]{:S(2)}, u32[]{:S(2)}) collective-permute-start(bf16[4,16,128]{2,1,0:T(8,128)(2,1)S(1)} %get-tuple-element.13), channel_id=1, source_target_pairs={{0,31},{1,30},{2,1},{3,0},{4,3},{5,2},{6,5},{7,4},{8,7},{9,6},{10,... | collective-permute-start | bytes 49160 | tf_op jit(solution)/shard_map/ppermute | solution.py:307
  34.5 0.0 collective-permute-done.7
  34.5 0.0 collective-permute-start.2
  34.5 0.2 pad_maximum_fusion
  34.8 0.1 copy.18
  34.9 0.1 copy.19
  35.1 0.8 slice.82.inner
  35.9 0.8 copy.20.left
  36.7 0.8 copy.21.right
  37.5 0.0 collective-permute-done.3.low_west.low_east
  37.5 0.0 collective-permute-done.4.high_west.high_east
  37.6 3.3 %collective-permute-done.2.west.east = bf16[64,16,128]{2,1,0:T(8,128)(2,1)S(1)} collective-permute-done((bf16[64,16,128]{2,1,0:T(8,128)(2,1)S(1)}, bf16[64,16,128]{2,1,0:T(8,128)(2,1)S(1)}, u32[]{:S(2)}, u32[]{:S(2)}) %collective-permute-start.2) | collective-permute-done | bytes 262176 | tf_op jit(solution)/shard_map/ppermute | solution.py:307
  40.9 0.0 collective-permute-done.low
  40.9 0.7 copy-done.3
  41.6 0.1 copy-done.7
  41.7 0.7 copy-done.8
  42.4 62.0 %shard_map.68 = (bf16[256,8192]{1,0:T(8,128)(2,1)}, f32[272,128]{1,0:T(8,128)}) custom-call(bf16[64,272,128]{2,1,0:T(8,128)(2,1)} %copy-done, bf16[4,272,128]{2,1,0:T(8,128)(2,1)} %copy-done.7, bf16[4,272,128]{2,1,0:T(8,128)(2,1)} %copy-done.8, bf16[64,16,128]{2,1,0:T(8,128)(2,1)} %copy-done.3, bf16[64,16,128]{2,1,0:T(8,128)(2,1)} %copy-done.3, ...), custom_call_target="tpu_custom_call" | custom-call | tf_op jit(solution)/shard_map/pallas_call | solution.py:259
  104.4 0.9 constant_dynamic-slice_fusion
  105.2 1.3 collective-permute-done.8
  106.5 0.9 dynamic-slice_add_fusion
  107.4 0.1 collective-permute-start.9
  107.5 4.3 %collective-permute-done.9 = f32[136,128]{1,0:T(8,128)S(1)} collective-permute-done((f32[136,128]{1,0:T(8,128)S(1)}, f32[136,128]{1,0:T(8,128)S(1)}, u32[]{:S(2)}, u32[]{:S(2)}) %collective-permute-start.9) | collective-permute-done | bytes 69664 | tf_op jit(solution)/shard_map/ppermute | solution.py:311
  111.8 0.1 collective-permute-start.10
  111.9 4.3 %collective-permute-done.10 = f32[136,128]{1,0:T(8,128)S(1)} collective-permute-done((f32[136,128]{1,0:T(8,128)S(1)}, f32[136,128]{1,0:T(8,128)S(1)}, u32[]{:S(2)}, u32[]{:S(2)}) %collective-permute-start.10) | collective-permute-done | bytes 69664 | tf_op jit(solution)/shard_map/ppermute | solution.py:311
  116.2 0.1 collective-permute-start.11
  116.2 4.3 %collective-permute-done.11 = f32[136,128]{1,0:T(8,128)S(1)} collective-permute-done((f32[136,128]{1,0:T(8,128)S(1)}, f32[136,128]{1,0:T(8,128)S(1)}, u32[]{:S(2)}, u32[]{:S(2)}) %collective-permute-start.11) | collective-permute-done | bytes 69664 | tf_op jit(solution)/shard_map/ppermute | solution.py:311
  120.6 0.1 collective-permute-start.12
  120.6 5.8 %collective-permute-done.12 = f32[136,128]{1,0:T(8,128)S(1)} collective-permute-done((f32[136,128]{1,0:T(8,128)S(1)}, f32[136,128]{1,0:T(8,128)S(1)}, u32[]{:S(2)}, u32[]{:S(2)}) %collective-permute-start.12) | collective-permute-done | bytes 69664 | tf_op jit(solution)/shard_map/ppermute | solution.py:311
  126.5 0.1 collective-permute-start.13
  126.5 1.2 collective-permute-done.13
  127.8 11.6 %shard_map.69 = (f32[256,256]{1,0:T(8,128)}, bf16[256,256]{1,0:T(8,128)(2,1)S(1)}, f32[1,256]{1,0:T(1,128)}) custom-call(f32[272,128]{1,0:T(8,128)S(1)} %maximum_select_fusion.pay), custom_call_target="tpu_custom_call" | custom-call | tf_op jit(solution)/shard_map/pallas_call | solution.py:108
  139.4 2.2 %copy-done.2 = bf16[256,8192]{1,0:T(8,128)(2,1)S(1)} copy-done((bf16[256,8192]{1,0:T(8,128)(2,1)S(1)}, bf16[256,8192]{1,0:T(8,128)(2,1)}, u32[]{:S(2)}) %copy-start.2) | copy-done | bytes 4194328
  141.6 4.8 %shard_map.70 = bf16[256,64,128]{2,1,0:T(8,128)(2,1)} custom-call(bf16[256,256]{1,0:T(8,128)(2,1)S(1)} %get-tuple-element.9.inverse, bf16[256,8192]{1,0:T(8,128)(2,1)S(1)} %copy-done.2), custom_call_target="tpu_custom_call" | custom-call | tf_op jit(solution)/shard_map/pallas_call | solution.py:287
  (35 shorter events, 0.3 us)
Async XLA Ops:
  1.6 22.7 %collective-permute-start.5 = (f32[3,64,8]{2,1,0:T(8,128)S(1)}, f32[3,64,8]{2,1,0:T(8,128)S(1)}, u32[]{:S(2)}, u32[]{:S(2)}) collective-permute-start(f32[3,64,8]{2,1,0:T(8,128)S(1)} %pad_maximum_fusion.2), channel_id=1, source_target_pairs={{0,1},{1,0},{2,3},{3,2},{4,5},{5,4},{6,7},{7,6},{8,9},{9,8},{10,11... | collective-permute-start | bytes 18440 | tf_op jit(solution)/shard_map/ppermute | solution.py:307
  4.6 2.2 %copy-start.1 = (bf16[256,64,128]{2,1,0:T(8,128)(2,1)S(1)}, bf16[256,64,128]{2,1,0:T(8,128)(2,1)}, u32[]{:S(2)}) copy-start(bf16[256,64,128]{2,1,0:T(8,128)(2,1)} %tangent.1) | copy-start | bytes 12582916
  6.8 17.6 %copy-start.4 = (f32[64,128]{1,0:T(8,128)S(1)}, f32[64,128]{1,0:T(8,128)}, u32[]{:S(2)}) copy-start(f32[64,128]{1,0:T(8,128)} %param.7) | copy-start | bytes 98308
  6.8 17.6 %copy-start.5 = (f32[64,128]{1,0:T(8,128)S(1)}, f32[64,128]{1,0:T(8,128)}, u32[]{:S(2)}) copy-start(f32[64,128]{1,0:T(8,128)} %param.6) | copy-start | bytes 98308
  6.8 17.6 %copy-start.6 = (f32[64,128]{1,0:T(8,128)S(1)}, f32[64,128]{1,0:T(8,128)}, u32[]{:S(2)}) copy-start(f32[64,128]{1,0:T(8,128)} %param.5) | copy-start | bytes 98308
  19.8 9.3 %copy-start = (bf16[64,272,128]{2,1,0:T(8,128)(2,1)}, bf16[64,272,128]{2,1,0:T(8,128)(2,1)S(1)}, u32[]{:S(2)}) copy-start(bf16[64,272,128]{2,1,0:T(8,128)(2,1)S(1)} %shard_map.67.own) | copy-start | bytes 13369348
  19.8 21.0 %collective-permute-start = (bf16[4,272,128]{2,1,0:T(8,128)(2,1)S(1)}, bf16[4,272,128]{2,1,0:T(8,128)(2,1)S(1)}, u32[]{:S(2)}, u32[]{:S(2)}) collective-permute-start(bf16[4,272,128]{2,1,0:T(8,128)(2,1)S(1)} %get-tuple-element.16), channel_id=1, source_target_pairs={{0,2},{1,3},{2,4},{3,5},{4,6},{5,7},{6,8},{7,9},{8,10},{9,11},{10,... | collective-permute-start | bytes 835592 | tf_op jit(solution)/shard_map/ppermute | solution.py:307
  19.9 21.0 %collective-permute-start.1 = (bf16[4,272,128]{2,1,0:T(8,128)(2,1)S(1)}, bf16[4,272,128]{2,1,0:T(8,128)(2,1)S(1)}, u32[]{:S(2)}, u32[]{:S(2)}) collective-permute-start(bf16[4,272,128]{2,1,0:T(8,128)(2,1)S(1)} %get-tuple-element.15), channel_id=1, source_target_pairs={{0,30},{1,31},{2,0},{3,1},{4,2},{5,3},{6,4},{7,5},{8,6},{9,7},{10,... | collective-permute-start | bytes 835592 | tf_op jit(solution)/shard_map/ppermute | solution.py:307
  24.6 6.0 %collective-permute-start.6 = (f32[3,4,136]{2,1,0:T(4,128)S(1)}, f32[3,4,136]{2,1,0:T(4,128)S(1)}, u32[]{:S(2)}, u32[]{:S(2)}) collective-permute-start(f32[3,4,136]{2,1,0:T(4,128)S(1)} %get-tuple-element.19), channel_id=1, source_target_pairs={{0,2},{1,3},{2,4},{3,5},{4,6},{5,7},{6,8},{7,9},{8,10},{9,11},{10,... | collective-permute-start | bytes 19592 | tf_op jit(solution)/shard_map/ppermute | solution.py:307
  24.6 9.9 %collective-permute-start.7 = (f32[3,4,136]{2,1,0:T(4,128)S(1)}, f32[3,4,136]{2,1,0:T(4,128)S(1)}, u32[]{:S(2)}, u32[]{:S(2)}) collective-permute-start(f32[3,4,136]{2,1,0:T(4,128)S(1)} %get-tuple-element.20), channel_id=1, source_target_pairs={{0,30},{1,31},{2,0},{3,1},{4,2},{5,3},{6,4},{7,5},{8,6},{9,7},{10,... | collective-permute-start | bytes 19592 | tf_op jit(solution)/shard_map/ppermute | solution.py:307
  29.1 8.5 %collective-permute-start.3 = (bf16[4,16,128]{2,1,0:T(8,128)(2,1)S(1)}, bf16[4,16,128]{2,1,0:T(8,128)(2,1)S(1)}, u32[]{:S(2)}, u32[]{:S(2)}) collective-permute-start(bf16[4,16,128]{2,1,0:T(8,128)(2,1)S(1)} %get-tuple-element.14), channel_id=1, source_target_pairs={{0,3},{1,2},{2,5},{3,4},{4,7},{5,6},{6,9},{7,8},{8,11},{9,10},{10,... | collective-permute-start | bytes 49160 | tf_op jit(solution)/shard_map/ppermute | solution.py:307
  30.5 7.0 %collective-permute-start.4 = (bf16[4,16,128]{2,1,0:T(8,128)(2,1)S(1)}, bf16[4,16,128]{2,1,0:T(8,128)(2,1)S(1)}, u32[]{:S(2)}, u32[]{:S(2)}) collective-permute-start(bf16[4,16,128]{2,1,0:T(8,128)(2,1)S(1)} %get-tuple-element.13), channel_id=1, source_target_pairs={{0,31},{1,30},{2,1},{3,0},{4,3},{5,2},{6,5},{7,4},{8,7},{9,6},{10,... | collective-permute-start | bytes 49160 | tf_op jit(solution)/shard_map/ppermute | solution.py:307
  34.5 6.4 %collective-permute-start.2 = (bf16[64,16,128]{2,1,0:T(8,128)(2,1)S(1)}, bf16[64,16,128]{2,1,0:T(8,128)(2,1)S(1)}, u32[]{:S(2)}, u32[]{:S(2)}) collective-permute-start(bf16[64,16,128]{2,1,0:T(8,128)(2,1)S(1)} %slice.72), channel_id=1, source_target_pairs={{0,1},{1,0},{2,3},{3,2},{4,5},{5,4},{6,7},{7,6},{8,9},{9,8},{10,11... | collective-permute-start | bytes 786440 | tf_op jit(solution)/shard_map/ppermute | solution.py:307
  37.5 3.4 %copy-start.9 = (bf16[4,16,128]{2,1,0:T(8,128)(2,1)}, bf16[4,16,128]{2,1,0:T(8,128)(2,1)S(1)}, u32[]{:S(2)}) copy-start(bf16[4,16,128]{2,1,0:T(8,128)(2,1)S(1)} %collective-permute-done.3.low_west.low_east) | copy-start | bytes 49156
  37.5 3.4 %copy-start.10 = (bf16[4,16,128]{2,1,0:T(8,128)(2,1)}, bf16[4,16,128]{2,1,0:T(8,128)(2,1)S(1)}, u32[]{:S(2)}) copy-start(bf16[4,16,128]{2,1,0:T(8,128)(2,1)S(1)} %collective-permute-done.4.high_west.high_east) | copy-start | bytes 49156
  40.9 0.7 copy-start.3
  40.9 0.8 copy-start.7
  41.7 0.7 copy-start.8
  105.2 1.3 collective-permute-start.8
  107.4 4.4 %collective-permute-start.9 = (f32[136,128]{1,0:T(8,128)S(1)}, f32[136,128]{1,0:T(8,128)S(1)}, u32[]{:S(2)}, u32[]{:S(2)}) collective-permute-start(f32[136,128]{1,0:T(8,128)S(1)} %dynamic-slice_add_fusion), channel_id=1, source_target_pairs={{0,1},{1,0},{2,3},{3,2},{4,5},{5,4},{6,7},{7,6},{8,9},{9,8},{10,11... | collective-permute-start | bytes 208904 | tf_op jit(solution)/shard_map/ppermute | solution.py:311
  111.8 4.4 %collective-permute-start.10 = (f32[136,128]{1,0:T(8,128)S(1)}, f32[136,128]{1,0:T(8,128)S(1)}, u32[]{:S(2)}, u32[]{:S(2)}) collective-permute-start(f32[136,128]{1,0:T(8,128)S(1)} %add.44), channel_id=1, source_target_pairs={{0,4},{2,6},{4,0},{6,2},{8,12},{10,14},{12,8},{14,10},{16,20},{18,... | collective-permute-start | bytes 208904 | tf_op jit(solution)/shard_map/ppermute | solution.py:311
  116.2 4.4 %collective-permute-start.11 = (f32[136,128]{1,0:T(8,128)S(1)}, f32[136,128]{1,0:T(8,128)S(1)}, u32[]{:S(2)}, u32[]{:S(2)}) collective-permute-start(f32[136,128]{1,0:T(8,128)S(1)} %add.45), channel_id=1, source_target_pairs={{0,8},{2,10},{4,12},{6,14},{8,0},{10,2},{12,4},{14,6},{16,24},{18,... | collective-permute-start | bytes 208904 | tf_op jit(solution)/shard_map/ppermute | solution.py:311
  120.6 5.9 %collective-permute-start.12 = (f32[136,128]{1,0:T(8,128)S(1)}, f32[136,128]{1,0:T(8,128)S(1)}, u32[]{:S(2)}, u32[]{:S(2)}) collective-permute-start(f32[136,128]{1,0:T(8,128)S(1)} %add.46), channel_id=1, source_target_pairs={{0,16},{2,18},{4,20},{6,22},{8,24},{10,26},{12,28},{14,30},{16,0},... | collective-permute-start | bytes 208904 | tf_op jit(solution)/shard_map/ppermute | solution.py:311
  126.5 1.3 collective-permute-start.13
  139.4 2.2 %copy-start.2 = (bf16[256,8192]{1,0:T(8,128)(2,1)S(1)}, bf16[256,8192]{1,0:T(8,128)(2,1)}, u32[]{:S(2)}) copy-start(bf16[256,8192]{1,0:T(8,128)(2,1)} %get-tuple-element.10.evolved) | copy-start | bytes 12582916

commit v2 on v1

v2 whole, which is shorter than its diff:
```python
import functools

import jax
import jax.numpy as jnp
from jax import lax
from jax.experimental import pallas as pl
from jax.experimental.pallas import tpu as pltpu
from jax.sharding import PartitionSpec as P

F32 = jnp.float32
BF16 = jnp.bfloat16
SUBSTEPS = 4
LANES = 128
HALO = SUBSTEPS
GROUP = 8
EDGE = 2 * HALO
PACKED = 16


def spread(row):
    return jnp.broadcast_to(row, (8, 128))

def factor_block(v):
    sub = lax.broadcasted_iota(jnp.int32, (8, 128), 0)
    n = 8
    for p in range(16):
        c0 = p * n
        diag = v[c0:c0 + n, 0:128]
        column = [jnp.broadcast_to(diag[:, c0 + j:c0 + j + 1], (n, 128)) for j in range(n)]
        d = {(i, j): spread(column[j][i:i + 1]) for j in range(n) for i in range(j + 1)}
        inv, r, x = {}, {}, {}
        for j in range(n):
            inv[j] = lax.rsqrt(d[j, j])
            for k in range(j + 1, n):
                r[j, k] = d[j, k] * inv[j]
            for i in range(j + 1, n):
                for k in range(i, n):
                    d[i, k] = d[i, k] - r[j, i] * r[j, k]
        for j in range(n):
            x[j, j] = inv[j]
            for i in range(j + 1, n):
                acc = r[j, i] * x[j, j]
                for k in range(j + 1, i):
                    acc = acc + r[k, i] * x[k, j]
                x[i, j] = -(inv[i] * acc)
        dinv = {}
        for a in range(n):
            for b in range(a, n):
                acc = x[b, a] * x[b, b]
                for m in range(b + 1, n):
                    acc = acc + x[m, a] * x[m, b]
                dinv[a, b] = dinv[b, a] = acc
        ys = []
        for t in range(3):
            cols = slice(128 * t, 128 * t + 128)
            rows = [spread(v[c0 + k:c0 + k + 1, cols]) for k in range(n)]
            ys.append([sum(dinv[a, k] * rows[k] for k in range(n)) for a in range(n)])
            out = x[0, 0] * rows[0]
            for i in range(1, n):
                out = jnp.where(sub == i, sum(x[i, k] * rows[k] for k in range(i + 1)), out)
            v[c0:c0 + n, cols] = out
        for g in range(p + 1, 16):
            ag = v[n * g:n * g + n, 0:128]
            ab = [jnp.broadcast_to(ag[:, c0 + j:c0 + j + 1], (n, 128)) for j in range(n)]
            for t in range(3):
                cols = slice(128 * t, 128 * t + 128)
                acc = v[n * g:n * g + n, cols]
                for j in range(n):
                    acc = acc - ab[j] * ys[t][j]
                v[n * g:n * g + n, cols] = acc

def dot_t(a, b):
    return lax.dot_general(a, b, (((0,), (0,)), ((), ())), precision=lax.Precision.HIGHEST, preferred_element_type=F32)

def factor_kernel(total, pay, factor, inverse, exponents, v):
    h = 128
    ri = lax.broadcasted_iota(jnp.int32, (h, h), 0)
    ci = lax.broadcasted_iota(jnp.int32, (h, h), 1)
    eye = jnp.where(ri == ci, 1.0, 0.0).astype(F32)
    fold = pay[0:h, :] / total
    turned = fold.T
    diag0 = jnp.broadcast_to(pay[2 * h:2 * h + 1, :], (h, h)) / total
    v[:, 0:h] = jnp.where(ri == ci, diag0, jnp.where(ri < ci, turned, fold))
    v[:, h:2 * h] = pay[h:2 * h, :] / total
    v[:, 2 * h:3 * h] = eye
    rest = jnp.where(ri <= ci, fold, turned)
    factor_block(v)
    r00 = jnp.where(ri <= ci, v[:, 0:h], 0.0)
    r01 = v[:, h:2 * h]
    l00 = jnp.where(ri >= ci, v[:, 2 * h:3 * h], 0.0)
    factor[0:h, 0:h] = r00
    factor[0:h, h:2 * h] = r01
    inverse[0:h, 0:h] = l00.astype(jnp.bfloat16)
    inverse[0:h, h:2 * h] = jnp.zeros((h, h), jnp.bfloat16)
    exponents[:, 0:h] = jnp.log(jnp.sum(r00 * eye, axis=0, keepdims=True))
    v[:, 0:h] = rest - dot_t(r01, r01)
    v[:, h:2 * h] = -dot_t(r01, l00)
    v[:, 2 * h:3 * h] = eye
    factor_block(v)
    r11 = jnp.where(ri <= ci, v[:, 0:h], 0.0)
    factor[h:2 * h, 0:h] = jnp.zeros((h, h), F32)
    factor[h:2 * h, h:2 * h] = r11
    inverse[h:2 * h, 0:h] = v[:, h:2 * h].astype(jnp.bfloat16)
    inverse[h:2 * h, h:2 * h] = jnp.where(ri >= ci, v[:, 2 * h:3 * h], 0.0).astype(jnp.bfloat16)
    exponents[:, h:2 * h] = jnp.log(jnp.sum(r11 * eye, axis=0, keepdims=True))

def factorize(pay, total):
    return pl.pallas_call(
        functools.partial(factor_kernel, total),
        out_shape=(jax.ShapeDtypeStruct((256,256),F32), jax.ShapeDtypeStruct((256,256),jnp.bfloat16), jax.ShapeDtypeStruct((1,256),F32)),
        scratch_shapes=[pltpu.VMEM((128,384),F32)],
        compiler_params=pltpu.CompilerParams(vmem_limit_bytes=16<<20),
    )(pay)

def turn_kernel(tangent, turned, wide):
    fields, rows, lanes = tangent.shape
    pitch = rows + 1

    def widen(f, carry):
        wide[pl.ds(f * pitch, rows), :] = tangent[f].astype(F32)
        return carry

    lax.fori_loop(0, fields, widen, 0, unroll=8)

    def turn(r, carry):
        turned[r] = wide[pl.ds(r, fields, stride=pitch), :].T.astype(BF16)
        return carry

    lax.fori_loop(0, rows, turn, 0, unroll=2)


def turn(tangent):
    fields, rows, lanes = tangent.shape
    return pl.pallas_call(
        turn_kernel,
        out_shape=jax.ShapeDtypeStruct((rows, lanes, fields), BF16),
        scratch_shapes=[pltpu.VMEM((fields * (rows + 1), lanes), F32)],
        compiler_params=pltpu.CompilerParams(vmem_limit_bytes=16 << 20),
    )(tangent)


def evolve_kernel(own, low, high, sides, table, evolved, payload, first, second, coef, gram, held):
    rows, lanes, fields = own.shape
    width = lanes + 2 * HALO
    halves = fields // LANES
    start_of = lambda r: GROUP + r * width

    def spread(q, carry):
        for m in range(3):
            line = jnp.broadcast_to(table[m, pl.ds(q, 1)], (LANES, LANES))
            coef[m, pl.ds(pl.multiple_of(q * LANES, LANES), LANES), :] = line.T
        return carry

    lax.fori_loop(0, table.shape[1], spread, 0, unroll=2)

    def fill(row, block):
        for h in range(halves):
            first[h, pl.ds(start_of(row) + HALO, lanes), :] = block[:, LANES * h:LANES * (h + 1)].astype(F32)

    for i in range(HALO):
        fill(i, low[i])
        fill(HALO + rows + i, high[i])

    def fill_own(r, carry):
        fill(HALO + r, own[r])
        return carry

    lax.fori_loop(0, rows, fill_own, 0)

    def fill_sides(r, carry):
        pair = sides[r].astype(F32)
        for h in range(halves):
            first[h, pl.ds(start_of(r), HALO), :] = pair[:HALO, LANES * h:LANES * (h + 1)]
            first[h, pl.ds(start_of(r) + HALO + lanes, HALO), :] = pair[HALO:, LANES * h:LANES * (h + 1)]
        return carry

    lax.fori_loop(0, rows + 2 * HALO, fill_sides, 0)

    def weights(at):
        cx, cy, gr = [coef[m, pl.ds(at, GROUP), :] for m in range(3)]
        return 0.2 + gr, 0.2 - cx, 0.2 + cx, 0.2 - cy, 0.2 + cy

    def combine(f, c, n, s, e, w):
        return f[0] * c + (f[1] * n + f[2] * s) + (f[3] * e + f[4] * w)

    def pair_of(source, at, f):
        for h in range(halves):
            value = [source[h, pl.ds(at + width * i, GROUP), :] for i in range(-1, 3)]
            east = [source[h, pl.ds(at + width * i + 1, GROUP), :] for i in range(2)]
            west = [source[h, pl.ds(at + width * i - 1, GROUP), :] for i in range(2)]
            yield [combine(f[i], value[i + 1], value[i + 2], value[i], east[i], west[i]) for i in range(2)]

    def substep(source, target, step):
        def pair(p, carry):
            r = step + 2 * p
            for t in range(width // GROUP):
                at = pl.multiple_of(start_of(r) + GROUP * t, GROUP)
                f = [weights(at - GROUP + width * i) for i in range(2)]
                for h, out in enumerate(pair_of(source, at, f)):
                    for i in range(2):
                        target[h, pl.ds(at + width * i, GROUP), :] = out[i]
            return carry

        lax.fori_loop(0, (rows + 2 * (HALO - step)) // 2, pair, 0)

    buffers = [first, second]
    for step in range(1, SUBSTEPS):
        substep(buffers[(step - 1) % 2], buffers[step % 2], step)
    source = buffers[(SUBSTEPS - 1) % 2]
    gram[...] = jnp.zeros_like(gram)
    chunk = 8

    def last_chunk(q, carry):
        def pair(p, inner):
            r = q * chunk + 2 * p
            for t in range(0, lanes // GROUP, 2):
                parts = []
                for u in range(2):
                    at = start_of(HALO + r) + HALO + GROUP * (t + u)
                    f = [weights(at - GROUP + width * i) for i in range(2)]
                    parts.append(list(pair_of(source, at, f)))
                for i in range(2):
                    for h in range(halves):
                        both = jnp.concatenate([parts[0][h][i], parts[1][h][i]], axis=0).astype(BF16)
                        evolved[r + i, GROUP * t:GROUP * (t + 2), LANES * h:LANES * (h + 1)] = both
            return inner

        lax.fori_loop(0, chunk // 2, pair, 0)
        part = evolved[pl.ds(q * chunk, chunk)].reshape(chunk * lanes, fields)
        gram[...] += lax.dot_general(part, part, (((0,), (0,)), ((), ())), preferred_element_type=F32)
        return carry

    lax.fori_loop(0, rows // chunk, last_chunk, 0)
    h = fields // 2
    ri = lax.broadcasted_iota(jnp.int32, (h, h), 0)
    ci = lax.broadcasted_iota(jnp.int32, (h, h), 1)
    corner = gram[0:h, 0:h]
    payload[0:h] = jnp.where(ri <= ci, gram[h:2 * h, h:2 * h], corner)
    payload[h:2 * h] = gram[0:h, h:2 * h]
    diagonal = jnp.sum(jnp.where(ri == ci, corner, 0.0), axis=0, keepdims=True)
    payload[2 * h:] = jnp.broadcast_to(diagonal, (PACKED, h))


def evolve(own, low, high, sides, table):
    rows, lanes, fields = own.shape
    width = lanes + 2 * HALO
    state = (fields // LANES, (rows + 2 * HALO) * width + 2 * GROUP, LANES)
    return pl.pallas_call(
        evolve_kernel,
        out_shape=(
            jax.ShapeDtypeStruct((rows, lanes, fields), BF16),
            jax.ShapeDtypeStruct((fields + PACKED, fields // 2), F32),
        ),
        scratch_shapes=[
            pltpu.VMEM(state, F32),
            pltpu.VMEM(state, F32),
            pltpu.VMEM((3, table.shape[1] * LANES, LANES), F32),
            pltpu.VMEM((fields, fields), F32),
            pltpu.VMEM((GROUP, LANES), F32),
        ],
        compiler_params=pltpu.CompilerParams(vmem_limit_bytes=42 << 20),
    )(own, low, high, sides, table)


def project_kernel(inverse, evolved, basis, wide):
    fields, rows, lanes = basis.shape
    pitch = rows + 1
    for r in range(0, rows, 2):
        cells = evolved[r:r + 2].reshape(2 * lanes, fields)
        part = lax.dot_general(inverse[...], cells, (((1,), (1,)), ((), ())), preferred_element_type=F32)
        for i in range(2):
            wide[pl.ds(r + i, fields, stride=pitch), :] = part[:, i * lanes:(i + 1) * lanes]

    def store(f, carry):
        basis[f] = wide[pl.ds(f * pitch, rows), :].astype(BF16)
        return carry

    lax.fori_loop(0, fields, store, 0, unroll=8)


def project(inverse, evolved):
    rows, lanes, fields = evolved.shape
    step = 16
    return pl.pallas_call(
        project_kernel,
        grid=(rows // step,),
        in_specs=[
            pl.BlockSpec((fields, fields), lambda i: (0, 0)),
            pl.BlockSpec((step, lanes, fields), lambda i: (i, 0, 0)),
        ],
        out_specs=pl.BlockSpec((fields, step, lanes), lambda i: (0, i, 0)),
        out_shape=jax.ShapeDtypeStruct((fields, rows, lanes), BF16),
        scratch_shapes=[pltpu.VMEM(((step + 1) * fields, lanes), F32)],
        compiler_params=pltpu.CompilerParams(vmem_limit_bytes=32 << 20),
    )(inverse, evolved)


def shifted(block, down, right):
    nx, ny = lax.axis_size("gx"), lax.axis_size("gy")
    pairs = []
    for x in range(nx):
        for y in range(ny):
            pairs.append((x * ny + y, (x + down) % nx * ny + (y + right) % ny))
    return lax.ppermute(block, ("gx", "gy"), pairs)


def swapped(block, axis, bit):
    return lax.ppermute(block, axis, [(i, i ^ bit) for i in range(lax.axis_size(axis))])


def summed(payload):
    nx, ny = lax.axis_size("gx"), lax.axis_size("gy")
    if nx & (nx - 1) or ny & (ny - 1) or nx < 2:
        return lax.psum(payload, ("gx", "gy"))
    half = payload.shape[0] // 2
    side = lax.axis_index("gx") % 2
    kept = lax.dynamic_slice_in_dim(payload, side * half, half, 0)
    given = lax.dynamic_slice_in_dim(payload, (1 - side) * half, half, 0)
    total = kept + swapped(given, "gx", 1)
    for axis, bits in (("gy", range(ny.bit_length() - 1)), ("gx", range(1, nx.bit_length() - 1))):
        for bit in bits:
            total = total + swapped(total, axis, 1 << bit)
    other = swapped(total, "gx", 1)
    return jnp.where(side == 0, jnp.concatenate([total, other]), jnp.concatenate([other, total]))


def pieces(block):
    out = []
    for _ in range(3):
        part = lax.reduce_precision(block, 8, 7)
        out.append(part.astype(BF16))
        block = block - part
    return jnp.concatenate(out)


def joined(parts):
    count = parts.shape[0] // 3
    wide = parts.astype(F32)
    return wide[:count] + wide[count:2 * count] + wide[2 * count:]


def loaded(state, parts):
    fields = state.shape[-1]
    flat = parts.reshape(-1)
    flat = jnp.pad(flat, (0, -flat.size % (PACKED * fields)))
    return jnp.concatenate([state.reshape(-1, fields), flat.reshape(-1, fields)])


def unloaded(matrix, rows, cols):
    cells = rows * cols
    parts = matrix[cells:].reshape(-1)[:9 * cells].reshape(9, rows, cols)
    return matrix[:cells].reshape(rows, cols, -1), joined(parts)


def per_device(tangent, courant_x, courant_y, growth):
    fields, rows, cols = tangent.shape
    nx, ny = lax.axis_size("gx"), lax.axis_size("gy")
    block = jnp.stack([courant_x, courant_y, growth])
    parts = pieces(block)
    own = turn(tangent)

    def edges(x, axis):
        size = x.shape[axis]
        return lax.slice_in_dim(x, size - HALO, size, axis=axis), lax.slice_in_dim(x, 0, HALO, axis=axis)

    def sideways(state, part, down):
        state_last, state_begin = edges(state, 1)
        part_last, part_begin = edges(part, 2)
        count = state.shape[0]
        if ny == 2:
            both = loaded(jnp.concatenate([state_last, state_begin], axis=1), jnp.concatenate([part_last, part_begin], axis=2))
            return unloaded(shifted(both, down, 1), count, 2 * HALO)
        west = unloaded(shifted(loaded(state_last, part_last), down, 1), count, HALO)
        east = unloaded(shifted(loaded(state_begin, part_begin), down, -1), count, HALO)
        return jnp.concatenate([west[0], east[0]], axis=1), jnp.concatenate([west[1], east[1]], axis=2)

    side = sideways(own, parts, 0)
    state_last, state_begin = edges(own, 0)
    part_last, part_begin = edges(parts, 1)
    low = unloaded(shifted(loaded(state_last, part_last), 1, 0), HALO, cols)
    high = unloaded(shifted(loaded(state_begin, part_begin), -1, 0), HALO, cols)
    low_side = sideways(state_last, part_last, 1)
    high_side = sideways(state_begin, part_begin, -1)
    sides = jnp.concatenate([low_side[0], side[0], high_side[0]])
    middle = jnp.concatenate([low[1], block, high[1]], axis=1)
    around = jnp.concatenate([low_side[1], side[1], high_side[1]], axis=1)
    table = jnp.concatenate([around[:, :, :HALO], middle, around[:, :, HALO:]], axis=2).reshape(3, -1)
    table = jnp.pad(table, ((0, 0), (0, -table.shape[1] % LANES))).reshape(3, -1, LANES)
    evolved, payload = evolve(own, low[0], high[0], sides, table)
    total = float(rows * nx * cols * ny)
    factor, inverse, exponents = factorize(summed(payload), total)
    return project(inverse, evolved), factor, exponents.reshape(fields)


def solution(mesh):
    placed = (P(None, "gx", "gy"), P("gx", "gy"), P("gx", "gy"), P("gx", "gy"))
    return jax.shard_map(
        per_device,
        mesh=mesh,
        in_specs=placed,
        out_specs=(P(None, "gx", "gy"), P(), P()),
        check_vma=False,
    )
```

time: 147 us -> 98.8 us (0.67)
  Pallas kernels: 91.3 us -> 46 us
  starting transfers between devices: 16.3 us -> 10.9 us
  local copies, waits for them, and re-layouts: 9.73 us -> 11.8 us
    pallas_call x2, Pallas kernels: 74.9 us -> 30.4 us  [the longest x1 26.4 us: evolve(): pl.pallas_call(evolve_kernel, out_shape=(jax.ShapeDtypeStruct((rows, lane...]
    ppermute x8 -> x5, starting transfers between devices: 16 us -> 9.06 us  [shifted(): return lax.ppermute(block, ('gx', 'gy'), pairs)]
    unnamed x22 -> x16, local copies, waits for them, and re-layouts: 5.87 us -> 8.59 us
    ppermute x8 -> x5, waiting for transfers between devices: 4.76 us -> 7.4 us  [shifted(): return lax.ppermute(block, ('gx', 'gy'), pairs)]
    another operation x4 -> x0, local copies, waits for them, and re-layouts: 1.74 us -> none  [the longest x2 0.87 us: stencil_tables(): jnp.tile(table[:, :, -EDGE:], (1, 1, times))]
    ppermute x6, waiting for transfers between devices: 21.2 us -> 19.6 us  [swapped(): lax.ppermute(block, axis, [(i, i ^ bit) for i in range(lax.axis_size(axis...]
  transfers between devices with their start and end apart: 14 -> 11, of which waited for: 8 -> 8; matrix products, arithmetic and copies ran while one was open for 2% -> 3% of each run, Pallas kernels for 9% -> 0%
where the time goes in v2:
time: 98.8 us; the launch traced here: 98.5 us
  Pallas kernels  46 us (47%)
  waiting for transfers between devices  27 us (27%)
  local copies, waits for them, and re-layouts  11.8 us (12%)
  starting transfers between devices  10.9 us (11%)
  other arithmetic  1.71 us (2%)
  between operations  1.14 us (1%)
    pallas_call x1, Pallas kernels, evolve(): pl.pallas_call(evolve_kernel, out_shape=(jax.ShapeDtypeStruct((rows, lane...  26.4 us
    ppermute x6, waiting for transfers between devices, swapped(): lax.ppermute(block, axis, [(i, i ^ bit) for i in range(lax.axis_size(axis...  19.6 us
    pallas_call x1, Pallas kernels, factorize(): pl.pallas_call(functools.partial(factor_kernel, total), out_shape=(jax.Sh...  11.6 us
    ppermute x5, starting transfers between devices, shifted(): return lax.ppermute(block, ('gx', 'gy'), pairs)  9.06 us
    unnamed x16, local copies, waits for them, and re-layouts  8.59 us
    ppermute x5, waiting for transfers between devices, shifted(): return lax.ppermute(block, ('gx', 'gy'), pairs)  7.4 us
    pallas_call x1, Pallas kernels, project(): pl.pallas_call(project_kernel, grid=(rows // step,), in_specs=[pl.BlockSp...  4.06 us
    pallas_call x1, Pallas kernels, turn(): pl.pallas_call(turn_kernel, out_shape=jax.ShapeDtypeStruct((rows, lanes,...  3.98 us
  transfers between devices with their start and end apart: 11, of which 8 were waited for; matrix products, arithmetic and copies ran while one was open for 3% of the time, Pallas kernels for 0%

profile of v2, /device:TPU:0, one launch (start us, length us, event | category | flops | bytes accessed | tf_op | source)
XLA Modules:
  0.0 98.5 jit_solution(7465977091851579710)
XLA Ops:
  0.6 0.8 reduce-precision_convert_fusion.1
  1.5 0.1 fusion.7
  1.6 0.1 pad_maximum_fusion.6
  1.7 0.2 reshape.126
  1.9 2.2 %copy-done.2 = bf16[256,64,128]{2,1,0:T(8,128)(2,1)S(1)} copy-done((bf16[256,64,128]{2,1,0:T(8,128)(2,1)S(1)}, bf16[256,64,128]{2,1,0:T(8,128)(2,1)}, u32[]{:S(2)}) %copy-start.2) | copy-done | bytes 4194328
  4.1 4.0 %shard_map.67.own = bf16[64,128,256]{2,1,0:T(8,128)(2,1)S(1)} custom-call(bf16[256,64,128]{2,1,0:T(8,128)(2,1)S(1)} %copy-done.2), custom_call_target="tpu_custom_call" | custom-call | tf_op jit(solution)/shard_map/pallas_call | solution.py:134
  8.2 0.1 fusion.5
  8.3 0.1 maximum_bitcast_fusion
  8.4 3.0 %collective-permute-start.3 = (bf16[544,256]{1,0:T(8,128)(2,1)S(1)}, bf16[544,256]{1,0:T(8,128)(2,1)S(1)}, u32[]{:S(2)}, u32[]{:S(2)}) collective-permute-start(bf16[544,256]{1,0:T(8,128)(2,1)S(1)} %pad_maximum_fusion.3), channel_id=1, source_target_pairs={{0,1},{1,0},{2,3},{3,2},{4,5},{5,4},{6,7},{7,6},{8,9},{9,8},{10,11... | collective-permute-start | bytes 835592 | tf_op jit(solution)/shard_map/ppermute | solution.py:304
  11.4 0.1 fusion.3
  11.6 0.1 reshape.122
  11.7 1.0 %collective-permute-start.2 = (bf16[48,256]{1,0:T(8,128)(2,1)S(1)}, bf16[48,256]{1,0:T(8,128)(2,1)S(1)}, u32[]{:S(2)}, u32[]{:S(2)}) collective-permute-start(bf16[48,256]{1,0:T(8,128)(2,1)S(1)} %pad_maximum_fusion.8), channel_id=1, source_target_pairs={{0,3},{1,2},{2,5},{3,4},{4,7},{5,6},{6,9},{7,8},{8,11},{9,10},{10,... | collective-permute-start | bytes 73736 | tf_op jit(solution)/shard_map/ppermute | solution.py:304
  12.7 0.1 reshape.130
  12.9 4.4 %collective-permute-start.4 = (bf16[48,256]{1,0:T(8,128)(2,1)S(1)}, bf16[48,256]{1,0:T(8,128)(2,1)S(1)}, u32[]{:S(2)}, u32[]{:S(2)}) collective-permute-start(bf16[48,256]{1,0:T(8,128)(2,1)S(1)} %pad_maximum_fusion.9), channel_id=1, source_target_pairs={{0,31},{1,30},{2,1},{3,0},{4,3},{5,2},{6,5},{7,4},{8,7},{9,6},{10,... | collective-permute-start | bytes 73736 | tf_op jit(solution)/shard_map/ppermute | solution.py:304
  17.4 1.1 %fusion.6 = (bf16[4,128,256]{2,1,0:T(8,128)(2,1)S(1)}, bf16[4,128,256]{2,1,0:T(8,128)(2,1)S(1)}) fusion(bf16[64,128,256]{2,1,0:T(8,128)(2,1)} %copy-done), kind=kLoop, calls=%fused_computation.55 | loop fusion | bytes 1048576 | tf_op jit(solution)/shard_map/slice | solution.py:364
  18.5 0.5 collective-permute-start.1
  19.1 0.1 collective-permute-start
  19.2 0.2 slice.189
  19.4 0.2 slice.199
  19.7 0.1 copy.60
  19.8 0.1 copy.62
  19.9 0.1 add.84
  20.0 0.1 copy.61
  20.1 0.1 pad_maximum_fusion.10
  20.1 2.9 %collective-permute-done.1 = bf16[544,256]{1,0:T(8,128)(2,1)S(1)} collective-permute-done((bf16[544,256]{1,0:T(8,128)(2,1)S(1)}, bf16[544,256]{1,0:T(8,128)(2,1)S(1)}, u32[]{:S(2)}, u32[]{:S(2)}) %collective-permute-start.1) | collective-permute-done | bytes 278560 | tf_op jit(solution)/shard_map/ppermute | solution.py:304
  23.1 0.1 copy.63
  23.2 0.1 copy.64
  23.4 4.5 %collective-permute-done = bf16[544,256]{1,0:T(8,128)(2,1)S(1)} collective-permute-done((bf16[544,256]{1,0:T(8,128)(2,1)S(1)}, bf16[544,256]{1,0:T(8,128)(2,1)S(1)}, u32[]{:S(2)}, u32[]{:S(2)}) %collective-permute-start) | collective-permute-done | bytes 278560 | tf_op jit(solution)/shard_map/ppermute | solution.py:304
  27.9 0.2 pad_maximum_fusion.4
  28.0 0.2 reshape.133
  28.3 0.1 reshape.134.table
  28.5 2.2 %copy-done.1 = bf16[64,128,256]{2,1,0:T(8,128)(2,1)S(1)} copy-done((bf16[64,128,256]{2,1,0:T(8,128)(2,1)S(1)}, bf16[64,128,256]{2,1,0:T(8,128)(2,1)}, u32[]{:S(2)}) %copy-start.1) | copy-done | bytes 4194328
  30.7 26.4 %shard_map.68 = (bf16[64,128,256]{2,1,0:T(8,128)(2,1)S(1)}, f32[272,128]{1,0:T(8,128)S(1)}) custom-call(bf16[64,128,256]{2,1,0:T(8,128)(2,1)S(1)} %copy-done.1, bf16[4,128,256]{2,1,0:T(8,128)(2,1)S(1)} %bitcast.21, bf16[4,128,256]{2,1,0:T(8,128)(2,1)S(1)} %bitcast.20, bf16[72,8,256]{2,1,0:T(8,128)(2,1)S(1)} %pad_maximum_fusion.sides, ...), custom_call_target="tpu_custom_call" | custom-call | tf_op jit(solution)/shard_map/pallas_call | solution.py:248
  57.1 2.0 %copy-done.3 = bf16[64,128,256]{2,1,0:T(8,128)(2,1)} copy-done((bf16[64,128,256]{2,1,0:T(8,128)(2,1)}, bf16[64,128,256]{2,1,0:T(8,128)(2,1)S(1)}, u32[]{:S(2)}) %copy-start.3) | copy-done | bytes 4194328
  59.1 1.2 %collective-permute-done.5 = f32[136,128]{1,0:T(8,128)S(1)} collective-permute-done((f32[136,128]{1,0:T(8,128)S(1)}, f32[136,128]{1,0:T(8,128)S(1)}, u32[]{:S(2)}, u32[]{:S(2)}) %collective-permute-start.5) | collective-permute-done | bytes 69664 | tf_op jit(solution)/shard_map/ppermute | solution.py:308
  60.4 1.5 %collective-permute-start.6 = (f32[136,128]{1,0:T(8,128)S(1)}, f32[136,128]{1,0:T(8,128)S(1)}, u32[]{:S(2)}, u32[]{:S(2)}) collective-permute-start(f32[136,128]{1,0:T(8,128)S(1)} %dynamic-slice_add_fusion), channel_id=1, source_target_pairs={{0,1},{1,0},{2,3},{3,2},{4,5},{5,4},{6,7},{7,6},{8,9},{9,8},{10,11... | collective-permute-start | bytes 208904 | tf_op jit(solution)/shard_map/ppermute | solution.py:308
  61.9 2.9 %collective-permute-done.6 = f32[136,128]{1,0:T(8,128)S(1)} collective-permute-done((f32[136,128]{1,0:T(8,128)S(1)}, f32[136,128]{1,0:T(8,128)S(1)}, u32[]{:S(2)}, u32[]{:S(2)}) %collective-permute-start.6) | collective-permute-done | bytes 69664 | tf_op jit(solution)/shard_map/ppermute | solution.py:308
  64.8 0.1 collective-permute-start.7
  64.9 4.3 %collective-permute-done.7 = f32[136,128]{1,0:T(8,128)S(1)} collective-permute-done((f32[136,128]{1,0:T(8,128)S(1)}, f32[136,128]{1,0:T(8,128)S(1)}, u32[]{:S(2)}, u32[]{:S(2)}) %collective-permute-start.7) | collective-permute-done | bytes 69664 | tf_op jit(solution)/shard_map/ppermute | solution.py:308
  69.2 0.1 collective-permute-start.8
  69.2 4.3 %collective-permute-done.8 = f32[136,128]{1,0:T(8,128)S(1)} collective-permute-done((f32[136,128]{1,0:T(8,128)S(1)}, f32[136,128]{1,0:T(8,128)S(1)}, u32[]{:S(2)}, u32[]{:S(2)}) %collective-permute-start.8) | collective-permute-done | bytes 69664 | tf_op jit(solution)/shard_map/ppermute | solution.py:308
  73.6 0.1 collective-permute-start.9
  73.6 5.6 %collective-permute-done.9 = f32[136,128]{1,0:T(8,128)S(1)} collective-permute-done((f32[136,128]{1,0:T(8,128)S(1)}, f32[136,128]{1,0:T(8,128)S(1)}, u32[]{:S(2)}, u32[]{:S(2)}) %collective-permute-start.9) | collective-permute-done | bytes 69664 | tf_op jit(solution)/shard_map/ppermute | solution.py:308
  79.3 0.1 collective-permute-start.10
  79.4 1.2 %collective-permute-done.10 = f32[136,128]{1,0:T(8,128)S(1)} collective-permute-done((f32[136,128]{1,0:T(8,128)S(1)}, f32[136,128]{1,0:T(8,128)S(1)}, u32[]{:S(2)}, u32[]{:S(2)}) %collective-permute-start.10) | collective-permute-done | bytes 69664 | tf_op jit(solution)/shard_map/ppermute | solution.py:308
  80.6 11.6 %shard_map.69 = (f32[256,256]{1,0:T(8,128)}, bf16[256,256]{1,0:T(8,128)(2,1)S(1)}, f32[1,256]{1,0:T(1,128)}) custom-call(f32[272,128]{1,0:T(8,128)S(1)} %maximum_select_fusion.pay), custom_call_target="tpu_custom_call" | custom-call | tf_op jit(solution)/shard_map/pallas_call | solution.py:108
  92.2 2.2 %copy-done.4 = bf16[64,128,256]{2,1,0:T(8,128)(2,1)S(1)} copy-done((bf16[64,128,256]{2,1,0:T(8,128)(2,1)S(1)}, bf16[64,128,256]{2,1,0:T(8,128)(2,1)}, u32[]{:S(2)}) %copy-start.4) | copy-done | bytes 4194328
  94.4 4.1 %shard_map.70 = bf16[256,64,128]{2,1,0:T(8,128)(2,1)} custom-call(bf16[256,256]{1,0:T(8,128)(2,1)S(1)} %get-tuple-element.9.inverse, bf16[64,128,256]{2,1,0:T(8,128)(2,1)S(1)} %copy-done.4), custom_call_target="tpu_custom_call" | custom-call | tf_op jit(solution)/shard_map/pallas_call | solution.py:284
  (67 shorter events, 0.6 us)
Async XLA Ops:
  1.9 2.2 %copy-start.2 = (bf16[256,64,128]{2,1,0:T(8,128)(2,1)S(1)}, bf16[256,64,128]{2,1,0:T(8,128)(2,1)}, u32[]{:S(2)}) copy-start(bf16[256,64,128]{2,1,0:T(8,128)(2,1)} %tangent.1) | copy-start | bytes 12582916
  8.1 3.4 %copy-start = (bf16[64,128,256]{2,1,0:T(8,128)(2,1)}, bf16[64,128,256]{2,1,0:T(8,128)(2,1)S(1)}, u32[]{:S(2)}) copy-start(bf16[64,128,256]{2,1,0:T(8,128)(2,1)S(1)} %shard_map.67.own) | copy-start | bytes 12582916
  8.1 19.7 %copy-start.5 = (f32[64,128]{1,0:T(8,128)S(1)}, f32[64,128]{1,0:T(8,128)}, u32[]{:S(2)}) copy-start(f32[64,128]{1,0:T(8,128)} %param.7) | copy-start | bytes 98308
  8.1 19.7 %copy-start.6 = (f32[64,128]{1,0:T(8,128)S(1)}, f32[64,128]{1,0:T(8,128)}, u32[]{:S(2)}) copy-start(f32[64,128]{1,0:T(8,128)} %param.6) | copy-start | bytes 98308
  8.1 19.7 %copy-start.7 = (f32[64,128]{1,0:T(8,128)S(1)}, f32[64,128]{1,0:T(8,128)}, u32[]{:S(2)}) copy-start(f32[64,128]{1,0:T(8,128)} %param.5) | copy-start | bytes 98308
  8.4 11.4 %collective-permute-start.3 = (bf16[544,256]{1,0:T(8,128)(2,1)S(1)}, bf16[544,256]{1,0:T(8,128)(2,1)S(1)}, u32[]{:S(2)}, u32[]{:S(2)}) collective-permute-start(bf16[544,256]{1,0:T(8,128)(2,1)S(1)} %pad_maximum_fusion.3), channel_id=1, source_target_pairs={{0,1},{1,0},{2,3},{3,2},{4,5},{5,4},{6,7},{7,6},{8,9},{9,8},{10,11... | collective-permute-start | bytes 835592 | tf_op jit(solution)/shard_map/ppermute | solution.py:304
  11.7 7.5 %collective-permute-start.2 = (bf16[48,256]{1,0:T(8,128)(2,1)S(1)}, bf16[48,256]{1,0:T(8,128)(2,1)S(1)}, u32[]{:S(2)}, u32[]{:S(2)}) collective-permute-start(bf16[48,256]{1,0:T(8,128)(2,1)S(1)} %pad_maximum_fusion.8), channel_id=1, source_target_pairs={{0,3},{1,2},{2,5},{3,4},{4,7},{5,6},{6,9},{7,8},{8,11},{9,10},{10,... | collective-permute-start | bytes 73736 | tf_op jit(solution)/shard_map/ppermute | solution.py:304
  12.9 6.5 %collective-permute-start.4 = (bf16[48,256]{1,0:T(8,128)(2,1)S(1)}, bf16[48,256]{1,0:T(8,128)(2,1)S(1)}, u32[]{:S(2)}, u32[]{:S(2)}) collective-permute-start(bf16[48,256]{1,0:T(8,128)(2,1)S(1)} %pad_maximum_fusion.9), channel_id=1, source_target_pairs={{0,31},{1,30},{2,1},{3,0},{4,3},{5,2},{6,5},{7,4},{8,7},{9,6},{10,... | collective-permute-start | bytes 73736 | tf_op jit(solution)/shard_map/ppermute | solution.py:304
  18.5 4.6 %collective-permute-start.1 = (bf16[544,256]{1,0:T(8,128)(2,1)S(1)}, bf16[544,256]{1,0:T(8,128)(2,1)S(1)}, u32[]{:S(2)}, u32[]{:S(2)}) collective-permute-start(bf16[544,256]{1,0:T(8,128)(2,1)S(1)} %pad_maximum_fusion.2), channel_id=1, source_target_pairs={{0,30},{1,31},{2,0},{3,1},{4,2},{5,3},{6,4},{7,5},{8,6},{9,7},{10,... | collective-permute-start | bytes 835592 | tf_op jit(solution)/shard_map/ppermute | solution.py:304
  19.1 8.7 %collective-permute-start = (bf16[544,256]{1,0:T(8,128)(2,1)S(1)}, bf16[544,256]{1,0:T(8,128)(2,1)S(1)}, u32[]{:S(2)}, u32[]{:S(2)}) collective-permute-start(bf16[544,256]{1,0:T(8,128)(2,1)S(1)} %pad_maximum_fusion.1), channel_id=1, source_target_pairs={{0,2},{1,3},{2,4},{3,5},{4,6},{5,7},{6,8},{7,9},{8,10},{9,11},{10,... | collective-permute-start | bytes 835592 | tf_op jit(solution)/shard_map/ppermute | solution.py:304
  28.5 2.2 %copy-start.1 = (bf16[64,128,256]{2,1,0:T(8,128)(2,1)S(1)}, bf16[64,128,256]{2,1,0:T(8,128)(2,1)}, u32[]{:S(2)}) copy-start(bf16[64,128,256]{2,1,0:T(8,128)(2,1)} %copy-done) | copy-start | bytes 12582916
  57.1 2.0 %copy-start.3 = (bf16[64,128,256]{2,1,0:T(8,128)(2,1)}, bf16[64,128,256]{2,1,0:T(8,128)(2,1)S(1)}, u32[]{:S(2)}) copy-start(bf16[64,128,256]{2,1,0:T(8,128)(2,1)S(1)} %get-tuple-element.10.evolved) | copy-start | bytes 12582916
  59.1 1.3 %collective-permute-start.5 = (f32[136,128]{1,0:T(8,128)S(1)}, f32[136,128]{1,0:T(8,128)S(1)}, u32[]{:S(2)}, u32[]{:S(2)}) collective-permute-start(f32[136,128]{1,0:T(8,128)S(1)} %constant_dynamic-slice_fusion), channel_id=1, source_target_pairs={{0,2},{2,0},{4,6},{6,4},{8,10},{10,8},{12,14},{14,12},{16,18},{18,... | collective-permute-start | bytes 208904 | tf_op jit(solution)/shard_map/ppermute | solution.py:308
  60.4 4.4 %collective-permute-start.6 = (f32[136,128]{1,0:T(8,128)S(1)}, f32[136,128]{1,0:T(8,128)S(1)}, u32[]{:S(2)}, u32[]{:S(2)}) collective-permute-start(f32[136,128]{1,0:T(8,128)S(1)} %dynamic-slice_add_fusion), channel_id=1, source_target_pairs={{0,1},{1,0},{2,3},{3,2},{4,5},{5,4},{6,7},{7,6},{8,9},{9,8},{10,11... | collective-permute-start | bytes 208904 | tf_op jit(solution)/shard_map/ppermute | solution.py:308
  64.8 4.4 %collective-permute-start.7 = (f32[136,128]{1,0:T(8,128)S(1)}, f32[136,128]{1,0:T(8,128)S(1)}, u32[]{:S(2)}, u32[]{:S(2)}) collective-permute-start(f32[136,128]{1,0:T(8,128)S(1)} %add.96), channel_id=1, source_target_pairs={{0,4},{2,6},{4,0},{6,2},{8,12},{10,14},{12,8},{14,10},{16,20},{18,... | collective-permute-start | bytes 208904 | tf_op jit(solution)/shard_map/ppermute | solution.py:308
  69.2 4.4 %collective-permute-start.8 = (f32[136,128]{1,0:T(8,128)S(1)}, f32[136,128]{1,0:T(8,128)S(1)}, u32[]{:S(2)}, u32[]{:S(2)}) collective-permute-start(f32[136,128]{1,0:T(8,128)S(1)} %add.97), channel_id=1, source_target_pairs={{0,8},{2,10},{4,12},{6,14},{8,0},{10,2},{12,4},{14,6},{16,24},{18,... | collective-permute-start | bytes 208904 | tf_op jit(solution)/shard_map/ppermute | solution.py:308
  73.6 5.7 %collective-permute-start.9 = (f32[136,128]{1,0:T(8,128)S(1)}, f32[136,128]{1,0:T(8,128)S(1)}, u32[]{:S(2)}, u32[]{:S(2)}) collective-permute-start(f32[136,128]{1,0:T(8,128)S(1)} %add.98), channel_id=1, source_target_pairs={{0,16},{2,18},{4,20},{6,22},{8,24},{10,26},{12,28},{14,30},{16,0},... | collective-permute-start | bytes 208904 | tf_op jit(solution)/shard_map/ppermute | solution.py:308
  79.3 1.3 %collective-permute-start.10 = (f32[136,128]{1,0:T(8,128)S(1)}, f32[136,128]{1,0:T(8,128)S(1)}, u32[]{:S(2)}, u32[]{:S(2)}) collective-permute-start(f32[136,128]{1,0:T(8,128)S(1)} %add.99), channel_id=1, source_target_pairs={{0,2},{2,0},{4,6},{6,4},{8,10},{10,8},{12,14},{14,12},{16,18},{18,... | collective-permute-start | bytes 208904 | tf_op jit(solution)/shard_map/ppermute | solution.py:308
  92.2 2.2 %copy-start.4 = (bf16[64,128,256]{2,1,0:T(8,128)(2,1)S(1)}, bf16[64,128,256]{2,1,0:T(8,128)(2,1)}, u32[]{:S(2)}) copy-start(bf16[64,128,256]{2,1,0:T(8,128)(2,1)} %copy-done.3) | copy-start | bytes 12582916

commit v3 on v2

--- a/solution.py
+++ b/solution.py
@@ -104,43 +104,75 @@
     inverse[h:2 * h, h:2 * h] = jnp.where(ri >= ci, v[:, 2 * h:3 * h], 0.0).astype(jnp.bfloat16)
     exponents[:, h:2 * h] = jnp.log(jnp.sum(r11 * eye, axis=0, keepdims=True))
 
-def factorize(pay, total):
-    return pl.pallas_call(
-        functools.partial(factor_kernel, total),
-        out_shape=(jax.ShapeDtypeStruct((256,256),F32), jax.ShapeDtypeStruct((256,256),jnp.bfloat16), jax.ShapeDtypeStruct((1,256),F32)),
-        scratch_shapes=[pltpu.VMEM((128,384),F32)],
-        compiler_params=pltpu.CompilerParams(vmem_limit_bytes=16<<20),
-    )(pay)
-
-def turn_kernel(tangent, turned, wide):
+
+def turn_kernel(source, target, tangent, wide, turned, read, write):
     fields, rows, lanes = tangent.shape
     pitch = rows + 1
+    chunks = read.shape[0]
+    each, lines = fields // chunks, rows // chunks
+
+    def loading(q):
+        return pltpu.make_async_copy(source.at[pl.ds(q * each, each)], tangent.at[pl.ds(q * each, each)], read.at[q])
+
+    def storing(q):
+        return pltpu.make_async_copy(turned.at[pl.ds(q * lines, lines)], target.at[pl.ds(q * lines, lines)], write.at[q])
+
+    for q in range(chunks):
+        loading(q).start()
 
     def widen(f, carry):
         wide[pl.ds(f * pitch, rows), :] = tangent[f].astype(F32)
         return carry
 
-    lax.fori_loop(0, fields, widen, 0, unroll=8)
-
-    def turn(r, carry):
+    for q in range(chunks):
+        loading(q).wait()
+        lax.fori_loop(q * each, (q + 1) * each, widen, 0, unroll=8)
+
+    def turn_row(r, carry):
         turned[r] = wide[pl.ds(r, fields, stride=pitch), :].T.astype(BF16)
         return carry
 
-    lax.fori_loop(0, rows, turn, 0, unroll=2)
+    for q in range(chunks):
+        lax.fori_loop(q * lines, (q + 1) * lines, turn_row, 0, unroll=2)
+        storing(q).start()
+    for q in range(chunks):
+        storing(q).wait()
 
 
 def turn(tangent):
     fields, rows, lanes = tangent.shape
+    chunks = 8
     return pl.pallas_call(
         turn_kernel,
-        out_shape=jax.ShapeDtypeStruct((rows, lanes, fields), BF16),
-        scratch_shapes=[pltpu.VMEM((fields * (rows + 1), lanes), F32)],
-        compiler_params=pltpu.CompilerParams(vmem_limit_bytes=16 << 20),
-    )(tangent)
-
-
-def evolve_kernel(own, low, high, sides, table, evolved, payload, first, second, coef, gram, held):
+        in_specs=[pl.BlockSpec(memory_space=pltpu.HBM)],
+        out_specs=pl.BlockSpec(memory_space=pltpu.HBM),
+        out_shape=pltpu.HBM((rows, lanes, fields), BF16),
+        scratch_shapes=[
+            pltpu.VMEM((fields, rows, lanes), BF16),
+            pltpu.VMEM((fields * (rows + 1), lanes), F32),
+            pltpu.VMEM((rows, lanes, fields), BF16),
+            pltpu.SemaphoreType.DMA((chunks,)),
+            pltpu.SemaphoreType.DMA((chunks,)),
+        ],
+        compiler_params=pltpu.CompilerParams(vmem_limit_bytes=24 << 20),
+    )(pltpu.with_memory_space_constraint(tangent, pltpu.HBM))
+
+
+def evolve_kernel(source_block, low, high, sides, table, target_block, payload, first, second, coef, gram, own, read, write):
     rows, lanes, fields = own.shape
+    evolved = own
+    chunks = read.shape[0]
+    lines = rows // chunks
+
+    def loading(q):
+        return pltpu.make_async_copy(source_block.at[pl.ds(q * lines, lines)], own.at[pl.ds(q * lines, lines)], read.at[q])
+
+    def storing(q):
+        return pltpu.make_async_copy(
+            evolved.at[pl.ds(q * lines, lines)], target_block.at[pl.ds(q * lines, lines)], write.at[q])
+
+    for q in range(chunks):
+        loading(q).start()
     width = lanes + 2 * HALO
     halves = fields // LANES
     start_of = lambda r: GROUP + r * width
@@ -165,7 +197,9 @@
         fill(HALO + r, own[r])
         return carry
 
-    lax.fori_loop(0, rows, fill_own, 0)
+    for q in range(chunks):
+        loading(q).wait()
+        lax.fori_loop(q * lines, (q + 1) * lines, fill_own, 0)
 
     def fill_sides(r, carry):
         pair = sides[r].astype(F32)
@@ -208,7 +242,7 @@
         substep(buffers[(step - 1) % 2], buffers[step % 2], step)
     source = buffers[(SUBSTEPS - 1) % 2]
     gram[...] = jnp.zeros_like(gram)
-    chunk = 8
+    chunk = lines
 
     def last_chunk(q, carry):
         def pair(p, inner):
@@ -228,9 +262,10 @@
         lax.fori_loop(0, chunk // 2, pair, 0)
         part = evolved[pl.ds(q * chunk, chunk)].reshape(chunk * lanes, fields)
         gram[...] += lax.dot_general(part, part, (((0,), (0,)), ((), ())), preferred_element_type=F32)
-        return carry
-
-    lax.fori_loop(0, rows // chunk, last_chunk, 0)
+        storing(q).start()
+        return carry
+
+    lax.fori_loop(0, chunks, last_chunk, 0)
     h = fields // 2
     ri = lax.broadcasted_iota(jnp.int32, (h, h), 0)
     ci = lax.broadcasted_iota(jnp.int32, (h, h), 1)
@@ -239,16 +274,22 @@
     payload[h:2 * h] = gram[0:h, h:2 * h]
     diagonal = jnp.sum(jnp.where(ri == ci, corner, 0.0), axis=0, keepdims=True)
     payload[2 * h:] = jnp.broadcast_to(diagonal, (PACKED, h))
+    for q in range(chunks):
+        storing(q).wait()
 
 
 def evolve(own, low, high, sides, table):
     rows, lanes, fields = own.shape
     width = lanes + 2 * HALO
     state = (fields // LANES, (rows + 2 * HALO) * width + 2 * GROUP, LANES)
+    chunks = 8
+    hbm, vmem = pl.BlockSpec(memory_space=pltpu.HBM), pl.BlockSpec(memory_space=pltpu.VMEM)
     return pl.pallas_call(
         evolve_kernel,
+        in_specs=[hbm, vmem, vmem, vmem, vmem],
+        out_specs=(hbm, vmem),
         out_shape=(
-            jax.ShapeDtypeStruct((rows, lanes, fields), BF16),
+            pltpu.HBM((rows, lanes, fields), BF16),
             jax.ShapeDtypeStruct((fields + PACKED, fields // 2), F32),
         ),
         scratch_shapes=[
@@ -256,43 +297,71 @@
             pltpu.VMEM(state, F32),
             pltpu.VMEM((3, table.shape[1] * LANES, LANES), F32),
             pltpu.VMEM((fields, fields), F32),
-            pltpu.VMEM((GROUP, LANES), F32),
+            pltpu.VMEM((rows, lanes, fields), BF16),
+            pltpu.SemaphoreType.DMA((chunks,)),
+            pltpu.SemaphoreType.DMA((chunks,)),
         ],
         compiler_params=pltpu.CompilerParams(vmem_limit_bytes=42 << 20),
-    )(own, low, high, sides, table)
-
-
-def project_kernel(inverse, evolved, basis, wide):
-    fields, rows, lanes = basis.shape
-    pitch = rows + 1
-    for r in range(0, rows, 2):
-        cells = evolved[r:r + 2].reshape(2 * lanes, fields)
-        part = lax.dot_general(inverse[...], cells, (((1,), (1,)), ((), ())), preferred_element_type=F32)
-        for i in range(2):
-            wide[pl.ds(r + i, fields, stride=pitch), :] = part[:, i * lanes:(i + 1) * lanes]
-
-    def store(f, carry):
-        basis[f] = wide[pl.ds(f * pitch, rows), :].astype(BF16)
-        return carry
-
-    lax.fori_loop(0, fields, store, 0, unroll=8)
-
-
-def project(inverse, evolved):
+    )(pltpu.with_memory_space_constraint(own, pltpu.HBM), low, high, sides, table)
+
+
+def finish_kernel(total, pay, source, factor, exponents, basis, v, inverse, evolved, wide, out, read, write):
+    rows, lanes, fields = evolved.shape
+    chunks, step = out.shape[0], out.shape[2]
+    pitch = step + 1
+
+    def loading(q):
+        return pltpu.make_async_copy(source.at[pl.ds(q * step, step)], evolved.at[pl.ds(q * step, step)], read.at[q])
+
+    def storing(q):
+        return pltpu.make_async_copy(out.at[q], basis.at[:, pl.ds(q * step, step)], write.at[q])
+
+    for q in range(chunks):
+        loading(q).start()
+    factor_kernel(total, pay, factor, inverse, exponents, v)
+    for q in range(chunks):
+        loading(q).wait()
+        for r in range(0, step, 2):
+            cells = evolved[q * step + r:q * step + r + 2].reshape(2 * lanes, fields)
+            part = lax.dot_general(inverse[...], cells, (((1,), (1,)), ((), ())), preferred_element_type=F32)
+            for i in range(2):
+                wide[pl.ds(r + i, fields, stride=pitch), :] = part[:, i * lanes:(i + 1) * lanes]
+
+        def narrow(f, carry):
+            out[q, f] = wide[pl.ds(f * pitch, step), :].astype(BF16)
+            return carry
+
+        lax.fori_loop(0, fields, narrow, 0, unroll=8)
+        storing(q).start()
+    for q in range(chunks):
+        storing(q).wait()
+
+
+def finish(pay, evolved, total):
     rows, lanes, fields = evolved.shape
     step = 16
+    chunks = rows // step
+    hbm, vmem = pl.BlockSpec(memory_space=pltpu.HBM), pl.BlockSpec(memory_space=pltpu.VMEM)
     return pl.pallas_call(
-        project_kernel,
-        grid=(rows // step,),
-        in_specs=[
-            pl.BlockSpec((fields, fields), lambda i: (0, 0)),
-            pl.BlockSpec((step, lanes, fields), lambda i: (i, 0, 0)),
+        functools.partial(finish_kernel, total),
+        in_specs=[vmem, hbm],
+        out_specs=(vmem, vmem, hbm),
+        out_shape=(
+            jax.ShapeDtypeStruct((fields, fields), F32),
+            jax.ShapeDtypeStruct((1, fields), F32),
+            jax.ShapeDtypeStruct((fields, rows, lanes), BF16),
+        ),
+        scratch_shapes=[
+            pltpu.VMEM((LANES, 3 * LANES), F32),
+            pltpu.VMEM((fields, fields), BF16),
+            pltpu.VMEM((rows, lanes, fields), BF16),
+            pltpu.VMEM(((step + 1) * fields, lanes), F32),
+            pltpu.VMEM((chunks, fields, step, lanes), BF16),
+            pltpu.SemaphoreType.DMA((chunks,)),
+            pltpu.SemaphoreType.DMA((chunks,)),
         ],
-        out_specs=pl.BlockSpec((fields, step, lanes), lambda i: (0, i, 0)),
-        out_shape=jax.ShapeDtypeStruct((fields, rows, lanes), BF16),
-        scratch_shapes=[pltpu.VMEM(((step + 1) * fields, lanes), F32)],
-        compiler_params=pltpu.CompilerParams(vmem_limit_bytes=32 << 20),
-    )(inverse, evolved)
+        compiler_params=pltpu.CompilerParams(vmem_limit_bytes=24 << 20),
+    )(pay, pltpu.with_memory_space_constraint(evolved, pltpu.HBM))
 
 
 def shifted(block, down, right):
@@ -349,7 +418,7 @@
 def unloaded(matrix, rows, cols):
     cells = rows * cols
     parts = matrix[cells:].reshape(-1)[:9 * cells].reshape(9, rows, cols)
-    return matrix[:cells].reshape(rows, cols, -1), joined(parts)
+    return matrix[:cells].reshape(rows, cols, -1), parts
 
 
 def per_device(tangent, courant_x, courant_y, growth):
@@ -363,33 +432,33 @@
         size = x.shape[axis]
         return lax.slice_in_dim(x, size - HALO, size, axis=axis), lax.slice_in_dim(x, 0, HALO, axis=axis)
 
-    def sideways(state, part, down):
-        state_last, state_begin = edges(state, 1)
-        part_last, part_begin = edges(part, 2)
-        count = state.shape[0]
-        if ny == 2:
-            both = loaded(jnp.concatenate([state_last, state_begin], axis=1), jnp.concatenate([part_last, part_begin], axis=2))
-            return unloaded(shifted(both, down, 1), count, 2 * HALO)
-        west = unloaded(shifted(loaded(state_last, part_last), down, 1), count, HALO)
-        east = unloaded(shifted(loaded(state_begin, part_begin), down, -1), count, HALO)
-        return jnp.concatenate([west[0], east[0]], axis=1), jnp.concatenate([west[1], east[1]], axis=2)
-
-    side = sideways(own, parts, 0)
-    state_last, state_begin = edges(own, 0)
-    part_last, part_begin = edges(parts, 1)
-    low = unloaded(shifted(loaded(state_last, part_last), 1, 0), HALO, cols)
-    high = unloaded(shifted(loaded(state_begin, part_begin), -1, 0), HALO, cols)
-    low_side = sideways(state_last, part_last, 1)
-    high_side = sideways(state_begin, part_begin, -1)
-    sides = jnp.concatenate([low_side[0], side[0], high_side[0]])
-    middle = jnp.concatenate([low[1], block, high[1]], axis=1)
-    around = jnp.concatenate([low_side[1], side[1], high_side[1]], axis=1)
+    state_last, state_begin = edges(own, 1)
+    part_last, part_begin = edges(parts, 2)
+    if ny == 2:
+        both = loaded(jnp.concatenate([state_last, state_begin], axis=1), jnp.concatenate([part_last, part_begin], axis=2))
+        side, side_part = unloaded(shifted(both, 0, 1), rows, 2 * HALO)
+    else:
+        west, west_part = unloaded(shifted(loaded(state_last, part_last), 0, 1), rows, HALO)
+        east, east_part = unloaded(shifted(loaded(state_begin, part_begin), 0, -1), rows, HALO)
+        side, side_part = jnp.concatenate([west, east], axis=1), jnp.concatenate([west_part, east_part], axis=2)
+
+    def ends(state, part, count):
+        state_last, state_begin = edges(state, 0)
+        part_last, part_begin = edges(part, 1)
+        return (unloaded(shifted(loaded(state_last, part_last), 1, 0), HALO, count),
+                unloaded(shifted(loaded(state_begin, part_begin), -1, 0), HALO, count))
+
+    low, high = ends(own, parts, cols)
+    low_side, high_side = ends(side, side_part, 2 * HALO)
+    sides = jnp.concatenate([low_side[0], side, high_side[0]])
+    middle = jnp.concatenate([joined(low[1]), block, joined(high[1])], axis=1)
+    around = joined(jnp.concatenate([low_side[1], side_part, high_side[1]], axis=1))
     table = jnp.concatenate([around[:, :, :HALO], middle, around[:, :, HALO:]], axis=2).reshape(3, -1)
     table = jnp.pad(table, ((0, 0), (0, -table.shape[1] % LANES))).reshape(3, -1, LANES)
     evolved, payload = evolve(own, low[0], high[0], sides, table)
     total = float(rows * nx * cols * ny)
-    factor, inverse, exponents = factorize(summed(payload), total)
-    return project(inverse, evolved), factor, exponents.reshape(fields)
+    factor, exponents, basis = finish(summed(payload), evolved, total)
+    return basis, factor, exponents.reshape(fields)
 
 
 def solution(mesh):

time: 98.8 us -> 93.7 us (0.948)
  local copies, waits for them, and re-layouts: 11.8 us -> 3.98 us
  Pallas kernels: 46 us -> 50.3 us
  waiting for transfers between devices: 27 us -> 22.8 us
  starting transfers between devices: 10.9 us -> 13.6 us
    unnamed x16 -> x6, local copies, waits for them, and re-layouts: 8.59 us -> 0.02 us
    pallas_call x4 -> x3, Pallas kernels: 46 us -> 50.3 us  [the longest x1 27.1 us: evolve(): pl.pallas_call(evolve_kernel, in_specs=[hbm, vmem, vmem, vmem, vmem], out...]
    ppermute x5, waiting for transfers between devices: 7.4 us -> 3.8 us  [shifted(): return lax.ppermute(block, ('gx', 'gy'), pairs)]
    ppermute x5, starting transfers between devices: 9.06 us -> 11.4 us  [shifted(): return lax.ppermute(block, ('gx', 'gy'), pairs)]
    slice x3 -> x4, local copies, waits for them, and re-layouts: 0.24 us -> 1.28 us  [edges(): lax.slice_in_dim(x, size - HALO, size, axis=axis)]
  transfers between devices with their start and end apart: 11 -> 11, of which waited for: 8 -> 9; matrix products, arithmetic and copies ran while one was open for 3% -> 2% of each run, Pallas kernels for 0% -> 0%
where the time goes in v3:
time: 93.7 us; the launch traced here: 93.4 us
  Pallas kernels  50.3 us (54%)
  waiting for transfers between devices  22.8 us (24%)
  starting transfers between devices  13.6 us (15%)
  local copies, waits for them, and re-layouts  3.98 us (4%)
  other arithmetic  1.56 us (2%)
  between operations  1.26 us (1%)
    pallas_call x1, Pallas kernels, evolve(): pl.pallas_call(evolve_kernel, in_specs=[hbm, vmem, vmem, vmem, vmem], out...  27.1 us
    ppermute x6, waiting for transfers between devices, swapped(): lax.ppermute(block, axis, [(i, i ^ bit) for i in range(lax.axis_size(axis...  19 us
    pallas_call x1, Pallas kernels, finish(): pl.pallas_call(functools.partial(finish_kernel, total), in_specs=[vmem, h...  16.6 us
    ppermute x5, starting transfers between devices, shifted(): return lax.ppermute(block, ('gx', 'gy'), pairs)  11.4 us
    pallas_call x1, Pallas kernels, turn(): pl.pallas_call(turn_kernel, in_specs=[pl.BlockSpec(memory_space=pltpu.HBM...  6.52 us
    ppermute x5, waiting for transfers between devices, shifted(): return lax.ppermute(block, ('gx', 'gy'), pairs)  3.8 us
    ppermute x6, starting transfers between devices, swapped(): lax.ppermute(block, axis, [(i, i ^ bit) for i in range(lax.axis_size(axis...  2.22 us
  transfers between devices with their start and end apart: 11, of which 9 were waited for; matrix products, arithmetic and copies ran while one was open for 2% of the time, Pallas kernels for 0%

profile of v3, /device:TPU:0, one launch (start us, length us, event | category | flops | bytes accessed | tf_op | source)
XLA Modules:
  0.0 93.4 jit_solution(11621601563561824344)
XLA Ops:
  0.6 0.8 reduce-precision_convert_fusion.1
  1.5 0.1 fusion.6
  1.6 0.1 pad_maximum_fusion.6
  1.7 0.2 reshape.118
  1.9 6.5 %shard_map.67.source_block = bf16[64,128,256]{2,1,0:T(8,128)(2,1)} custom-call(bf16[256,64,128]{2,1,0:T(8,128)(2,1)} %source.1), custom_call_target="tpu_custom_call" | custom-call | tf_op jit(solution)/shard_map/pallas_call | solution.py:145
  8.4 0.0 copy-start
  8.5 0.0 copy-start.1
  8.5 0.0 copy-start.2
  8.5 1.2 %fusion.2 = (bf16[64,4,256]{2,1,0:T(4,128)(2,1)S(1)}, bf16[64,4,256]{2,1,0:T(4,128)(2,1)S(1)}) fusion(bf16[64,128,256]{2,1,0:T(8,128)(2,1)} %shard_map.67.source_block), kind=kLoop, calls=%fused_computation.34 | loop fusion | bytes 524288 | tf_op jit(solution)/shard_map/slice | solution.py:433
  9.6 0.1 maximum_bitcast_fusion
  9.8 3.0 %collective-permute-start.2 = (bf16[544,256]{1,0:T(8,128)(2,1)S(1)}, bf16[544,256]{1,0:T(8,128)(2,1)S(1)}, u32[]{:S(2)}, u32[]{:S(2)}) collective-permute-start(bf16[544,256]{1,0:T(8,128)(2,1)S(1)} %pad_maximum_fusion.3), channel_id=1, source_target_pairs={{0,1},{1,0},{2,3},{3,2},{4,5},{5,4},{6,7},{7,6},{8,9},{9,8},{10,11... | collective-permute-start | bytes 835592 | tf_op jit(solution)/shard_map/ppermute | solution.py:373
  12.8 1.1 %fusion.3 = (bf16[4,128,256]{2,1,0:T(8,128)(2,1)S(1)}, bf16[4,128,256]{2,1,0:T(8,128)(2,1)S(1)}) fusion(bf16[64,128,256]{2,1,0:T(8,128)(2,1)} %shard_map.67.source_block), kind=kLoop, calls=%fused_computation.35 | loop fusion | bytes 1048576 | tf_op jit(solution)/shard_map/slice | solution.py:433
  14.0 3.8 %collective-permute-start.1 = (bf16[544,256]{1,0:T(8,128)(2,1)S(1)}, bf16[544,256]{1,0:T(8,128)(2,1)S(1)}, u32[]{:S(2)}, u32[]{:S(2)}) collective-permute-start(bf16[544,256]{1,0:T(8,128)(2,1)S(1)} %pad_maximum_fusion.2), channel_id=1, source_target_pairs={{0,30},{1,31},{2,0},{3,1},{4,2},{5,3},{6,4},{7,5},{8,6},{9,7},{10,... | collective-permute-start | bytes 835592 | tf_op jit(solution)/shard_map/ppermute | solution.py:373
  17.8 0.1 collective-permute-start
  17.9 1.6 %collective-permute-done.2 = bf16[544,256]{1,0:T(8,128)(2,1)S(1)} collective-permute-done((bf16[544,256]{1,0:T(8,128)(2,1)S(1)}, bf16[544,256]{1,0:T(8,128)(2,1)S(1)}, u32[]{:S(2)}, u32[]{:S(2)}) %collective-permute-start.2) | collective-permute-done | bytes 278560 | tf_op jit(solution)/shard_map/ppermute | solution.py:373
  19.5 0.2 reshape.120
  19.7 0.1 reshape.121
  19.8 0.1 collective-permute-start.3
  19.9 0.1 reshape.125
  20.1 4.5 %collective-permute-start.4 = (bf16[48,256]{1,0:T(8,128)(2,1)S(1)}, bf16[48,256]{1,0:T(8,128)(2,1)S(1)}, u32[]{:S(2)}, u32[]{:S(2)}) collective-permute-start(bf16[48,256]{1,0:T(8,128)(2,1)S(1)} %pad_maximum_fusion.9), channel_id=1, source_target_pairs={{0,30},{1,31},{2,0},{3,1},{4,2},{5,3},{6,4},{7,5},{8,6},{9,7},{10,... | collective-permute-start | bytes 73736 | tf_op jit(solution)/shard_map/ppermute | solution.py:373
  24.5 0.0 collective-permute-done.1
  24.6 2.1 %collective-permute-done = bf16[544,256]{1,0:T(8,128)(2,1)S(1)} collective-permute-done((bf16[544,256]{1,0:T(8,128)(2,1)S(1)}, bf16[544,256]{1,0:T(8,128)(2,1)S(1)}, u32[]{:S(2)}, u32[]{:S(2)}) %collective-permute-start) | collective-permute-done | bytes 278560 | tf_op jit(solution)/shard_map/ppermute | solution.py:373
  26.7 0.2 collective-permute-done.3
  26.9 0.2 slice.149
  27.1 0.0 collective-permute-done.4
  27.1 0.2 slice.152
  27.4 0.1 maximum_convert_fusion
  27.5 0.1 fusion.7
  27.5 0.0 copy-done
  27.6 0.0 copy-done.1
  27.6 0.0 copy-done.2
  27.6 0.2 pad_maximum_fusion.4
  27.8 0.2 reshape.128
  28.0 0.1 reshape.129.table
  28.2 27.1 %shard_map.68 = (bf16[64,128,256]{2,1,0:T(8,128)(2,1)}, f32[272,128]{1,0:T(8,128)S(1)}) custom-call(bf16[64,128,256]{2,1,0:T(8,128)(2,1)} %shard_map.67.source_block, bf16[4,128,256]{2,1,0:T(8,128)(2,1)S(1)} %bitcast.17, bf16[4,128,256]{2,1,0:T(8,128)(2,1)S(1)} %bitcast.16, bf16[72,8,256]{2,1,0:T(8,128)(2,1)S(1)} %pad_maximum_fusion.sides, ...), custom_call_target="tpu_custom_call" | custom-call | tf_op jit(solution)/shard_map/pallas_call | solution.py:287
  55.3 0.1 collective-permute-start.5
  55.4 1.2 %collective-permute-done.5 = f32[136,128]{1,0:T(8,128)S(1)} collective-permute-done((f32[136,128]{1,0:T(8,128)S(1)}, f32[136,128]{1,0:T(8,128)S(1)}, u32[]{:S(2)}, u32[]{:S(2)}) %collective-permute-start.5) | collective-permute-done | bytes 69664 | tf_op jit(solution)/shard_map/ppermute | solution.py:377
  56.7 0.8 collective-permute-start.6
  57.4 3.6 %collective-permute-done.6 = f32[136,128]{1,0:T(8,128)S(1)} collective-permute-done((f32[136,128]{1,0:T(8,128)S(1)}, f32[136,128]{1,0:T(8,128)S(1)}, u32[]{:S(2)}, u32[]{:S(2)}) %collective-permute-start.6) | collective-permute-done | bytes 69664 | tf_op jit(solution)/shard_map/ppermute | solution.py:377
  61.1 0.3 collective-permute-start.7
  61.4 4.0 %collective-permute-done.7 = f32[136,128]{1,0:T(8,128)S(1)} collective-permute-done((f32[136,128]{1,0:T(8,128)S(1)}, f32[136,128]{1,0:T(8,128)S(1)}, u32[]{:S(2)}, u32[]{:S(2)}) %collective-permute-start.7) | collective-permute-done | bytes 69664 | tf_op jit(solution)/shard_map/ppermute | solution.py:377
  65.4 0.1 collective-permute-start.8
  65.5 4.3 %collective-permute-done.8 = f32[136,128]{1,0:T(8,128)S(1)} collective-permute-done((f32[136,128]{1,0:T(8,128)S(1)}, f32[136,128]{1,0:T(8,128)S(1)}, u32[]{:S(2)}, u32[]{:S(2)}) %collective-permute-start.8) | collective-permute-done | bytes 69664 | tf_op jit(solution)/shard_map/ppermute | solution.py:377
  69.8 0.9 collective-permute-start.9
  70.7 4.6 %collective-permute-done.9 = f32[136,128]{1,0:T(8,128)S(1)} collective-permute-done((f32[136,128]{1,0:T(8,128)S(1)}, f32[136,128]{1,0:T(8,128)S(1)}, u32[]{:S(2)}, u32[]{:S(2)}) %collective-permute-start.9) | collective-permute-done | bytes 69664 | tf_op jit(solution)/shard_map/ppermute | solution.py:377
  75.3 0.1 collective-permute-start.10
  75.4 1.2 %collective-permute-done.10 = f32[136,128]{1,0:T(8,128)S(1)} collective-permute-done((f32[136,128]{1,0:T(8,128)S(1)}, f32[136,128]{1,0:T(8,128)S(1)}, u32[]{:S(2)}, u32[]{:S(2)}) %collective-permute-start.10) | collective-permute-done | bytes 69664 | tf_op jit(solution)/shard_map/ppermute | solution.py:377
  76.6 16.6 %shard_map.69 = (f32[256,256]{1,0:T(8,128)}, f32[1,256]{1,0:T(1,128)}, bf16[256,64,128]{2,1,0:T(8,128)(2,1)}) custom-call(f32[272,128]{1,0:T(8,128)S(1)} %maximum_select_fusion.pay, bf16[64,128,256]{2,1,0:T(8,128)(2,1)} %get-tuple-element.9.source), custom_call_target="tpu_custom_call" | custom-call | tf_op jit(solution)/shard_map/pallas_call | solution.py:345
  (47 shorter events, 0.6 us)
Async XLA Ops:
  8.4 19.1 %copy-start = (f32[64,128]{1,0:T(8,128)S(1)}, f32[64,128]{1,0:T(8,128)}, u32[]{:S(2)}) copy-start(f32[64,128]{1,0:T(8,128)} %param.7) | copy-start | bytes 98308
  8.5 19.1 %copy-start.1 = (f32[64,128]{1,0:T(8,128)S(1)}, f32[64,128]{1,0:T(8,128)}, u32[]{:S(2)}) copy-start(f32[64,128]{1,0:T(8,128)} %param.6) | copy-start | bytes 98308
  8.5 19.1 %copy-start.2 = (f32[64,128]{1,0:T(8,128)S(1)}, f32[64,128]{1,0:T(8,128)}, u32[]{:S(2)}) copy-start(f32[64,128]{1,0:T(8,128)} %param.5) | copy-start | bytes 98308
  9.8 9.7 %collective-permute-start.2 = (bf16[544,256]{1,0:T(8,128)(2,1)S(1)}, bf16[544,256]{1,0:T(8,128)(2,1)S(1)}, u32[]{:S(2)}, u32[]{:S(2)}) collective-permute-start(bf16[544,256]{1,0:T(8,128)(2,1)S(1)} %pad_maximum_fusion.3), channel_id=1, source_target_pairs={{0,1},{1,0},{2,3},{3,2},{4,5},{5,4},{6,7},{7,6},{8,9},{9,8},{10,11... | collective-permute-start | bytes 835592 | tf_op jit(solution)/shard_map/ppermute | solution.py:373
  14.0 10.6 %collective-permute-start.1 = (bf16[544,256]{1,0:T(8,128)(2,1)S(1)}, bf16[544,256]{1,0:T(8,128)(2,1)S(1)}, u32[]{:S(2)}, u32[]{:S(2)}) collective-permute-start(bf16[544,256]{1,0:T(8,128)(2,1)S(1)} %pad_maximum_fusion.2), channel_id=1, source_target_pairs={{0,30},{1,31},{2,0},{3,1},{4,2},{5,3},{6,4},{7,5},{8,6},{9,7},{10,... | collective-permute-start | bytes 835592 | tf_op jit(solution)/shard_map/ppermute | solution.py:373
  17.8 8.8 %collective-permute-start = (bf16[544,256]{1,0:T(8,128)(2,1)S(1)}, bf16[544,256]{1,0:T(8,128)(2,1)S(1)}, u32[]{:S(2)}, u32[]{:S(2)}) collective-permute-start(bf16[544,256]{1,0:T(8,128)(2,1)S(1)} %pad_maximum_fusion.1), channel_id=1, source_target_pairs={{0,2},{1,3},{2,4},{3,5},{4,6},{5,7},{6,8},{7,9},{8,10},{9,11},{10,... | collective-permute-start | bytes 835592 | tf_op jit(solution)/shard_map/ppermute | solution.py:373
  19.8 7.1 %collective-permute-start.3 = (bf16[48,256]{1,0:T(8,128)(2,1)S(1)}, bf16[48,256]{1,0:T(8,128)(2,1)S(1)}, u32[]{:S(2)}, u32[]{:S(2)}) collective-permute-start(bf16[48,256]{1,0:T(8,128)(2,1)S(1)} %pad_maximum_fusion.8), channel_id=1, source_target_pairs={{0,2},{1,3},{2,4},{3,5},{4,6},{5,7},{6,8},{7,9},{8,10},{9,11},{10,... | collective-permute-start | bytes 73736 | tf_op jit(solution)/shard_map/ppermute | solution.py:373
  20.1 7.1 %collective-permute-start.4 = (bf16[48,256]{1,0:T(8,128)(2,1)S(1)}, bf16[48,256]{1,0:T(8,128)(2,1)S(1)}, u32[]{:S(2)}, u32[]{:S(2)}) collective-permute-start(bf16[48,256]{1,0:T(8,128)(2,1)S(1)} %pad_maximum_fusion.9), channel_id=1, source_target_pairs={{0,30},{1,31},{2,0},{3,1},{4,2},{5,3},{6,4},{7,5},{8,6},{9,7},{10,... | collective-permute-start | bytes 73736 | tf_op jit(solution)/shard_map/ppermute | solution.py:373
  55.3 1.3 %collective-permute-start.5 = (f32[136,128]{1,0:T(8,128)S(1)}, f32[136,128]{1,0:T(8,128)S(1)}, u32[]{:S(2)}, u32[]{:S(2)}) collective-permute-start(f32[136,128]{1,0:T(8,128)S(1)} %constant_dynamic-slice_fusion), channel_id=1, source_target_pairs={{0,2},{2,0},{4,6},{6,4},{8,10},{10,8},{12,14},{14,12},{16,18},{18,... | collective-permute-start | bytes 208904 | tf_op jit(solution)/shard_map/ppermute | solution.py:377
  56.7 4.4 %collective-permute-start.6 = (f32[136,128]{1,0:T(8,128)S(1)}, f32[136,128]{1,0:T(8,128)S(1)}, u32[]{:S(2)}, u32[]{:S(2)}) collective-permute-start(f32[136,128]{1,0:T(8,128)S(1)} %dynamic-slice_add_fusion), channel_id=1, source_target_pairs={{0,1},{1,0},{2,3},{3,2},{4,5},{5,4},{6,7},{7,6},{8,9},{9,8},{10,11... | collective-permute-start | bytes 208904 | tf_op jit(solution)/shard_map/ppermute | solution.py:377
  61.1 4.4 %collective-permute-start.7 = (f32[136,128]{1,0:T(8,128)S(1)}, f32[136,128]{1,0:T(8,128)S(1)}, u32[]{:S(2)}, u32[]{:S(2)}) collective-permute-start(f32[136,128]{1,0:T(8,128)S(1)} %add.75), channel_id=1, source_target_pairs={{0,4},{2,6},{4,0},{6,2},{8,12},{10,14},{12,8},{14,10},{16,20},{18,... | collective-permute-start | bytes 208904 | tf_op jit(solution)/shard_map/ppermute | solution.py:377
  65.4 4.4 %collective-permute-start.8 = (f32[136,128]{1,0:T(8,128)S(1)}, f32[136,128]{1,0:T(8,128)S(1)}, u32[]{:S(2)}, u32[]{:S(2)}) collective-permute-start(f32[136,128]{1,0:T(8,128)S(1)} %add.76), channel_id=1, source_target_pairs={{0,8},{2,10},{4,12},{6,14},{8,0},{10,2},{12,4},{14,6},{16,24},{18,... | collective-permute-start | bytes 208904 | tf_op jit(solution)/shard_map/ppermute | solution.py:377
  69.8 5.5 %collective-permute-start.9 = (f32[136,128]{1,0:T(8,128)S(1)}, f32[136,128]{1,0:T(8,128)S(1)}, u32[]{:S(2)}, u32[]{:S(2)}) collective-permute-start(f32[136,128]{1,0:T(8,128)S(1)} %add.77), channel_id=1, source_target_pairs={{0,16},{2,18},{4,20},{6,22},{8,24},{10,26},{12,28},{14,30},{16,0},... | collective-permute-start | bytes 208904 | tf_op jit(solution)/shard_map/ppermute | solution.py:377
  75.3 1.3 %collective-permute-start.10 = (f32[136,128]{1,0:T(8,128)S(1)}, f32[136,128]{1,0:T(8,128)S(1)}, u32[]{:S(2)}, u32[]{:S(2)}) collective-permute-start(f32[136,128]{1,0:T(8,128)S(1)} %add.78), channel_id=1, source_target_pairs={{0,2},{2,0},{4,6},{6,4},{8,10},{10,8},{12,14},{14,12},{16,18},{18,... | collective-permute-start | bytes 208904 | tf_op jit(solution)/shard_map/ppermute | solution.py:377

commit v4 on v3

--- a/solution.py
+++ b/solution.py
@@ -17,17 +17,28 @@
 PACKED = 16
 
 
-def spread(row):
-    return jnp.broadcast_to(row, (8, 128))
-
-def factor_block(v):
+def tree(terms):
+    while len(terms) > 1:
+        terms = [a + b for a, b in zip(terms[::2], terms[1::2])] + terms[len(terms) & ~1:]
+    return terms[0]
+
+
+def spread(ref, *at):
+    *block, row = at
+    return ref[(*block, pl.ds(row, GROUP, stride=0), slice(None))]
+
+
+def factor_block(v, held):
     sub = lax.broadcasted_iota(jnp.int32, (8, 128), 0)
     n = 8
     for p in range(16):
         c0 = p * n
-        diag = v[c0:c0 + n, 0:128]
+        diag = v[0, c0:c0 + n]
         column = [jnp.broadcast_to(diag[:, c0 + j:c0 + j + 1], (n, 128)) for j in range(n)]
-        d = {(i, j): spread(column[j][i:i + 1]) for j in range(n) for i in range(j + 1)}
+        base = p % 2 * n * n
+        for j in range(n):
+            held[base + n * j:base + n * (j + 1)] = column[j]
+        d = {(i, j): spread(held, base + n * j + i) for j in range(n) for i in range(j + 1)}
         inv, r, x = {}, {}, {}
         for j in range(n):
             inv[j] = lax.rsqrt(d[j, j])
@@ -39,40 +50,29 @@
         for j in range(n):
             x[j, j] = inv[j]
             for i in range(j + 1, n):
-                acc = r[j, i] * x[j, j]
-                for k in range(j + 1, i):
-                    acc = acc + r[k, i] * x[k, j]
-                x[i, j] = -(inv[i] * acc)
+                x[i, j] = -(inv[i] * tree([r[k, i] * x[k, j] for k in range(j, i)]))
         dinv = {}
         for a in range(n):
             for b in range(a, n):
-                acc = x[b, a] * x[b, b]
-                for m in range(b + 1, n):
-                    acc = acc + x[m, a] * x[m, b]
-                dinv[a, b] = dinv[b, a] = acc
+                dinv[a, b] = dinv[b, a] = tree([x[m, a] * x[m, b] for m in range(b, n)])
         ys = []
         for t in range(3):
-            cols = slice(128 * t, 128 * t + 128)
-            rows = [spread(v[c0 + k:c0 + k + 1, cols]) for k in range(n)]
-            ys.append([sum(dinv[a, k] * rows[k] for k in range(n)) for a in range(n)])
+            rows = [spread(v, t, c0 + k) for k in range(n)]
+            ys.append([tree([dinv[a, k] * rows[k] for k in range(n)]) for a in range(n)])
             out = x[0, 0] * rows[0]
             for i in range(1, n):
-                out = jnp.where(sub == i, sum(x[i, k] * rows[k] for k in range(i + 1)), out)
-            v[c0:c0 + n, cols] = out
+                out = jnp.where(sub == i, tree([x[i, k] * rows[k] for k in range(i + 1)]), out)
+            v[t, c0:c0 + n] = out
         for g in range(p + 1, 16):
-            ag = v[n * g:n * g + n, 0:128]
+            ag = v[0, n * g:n * g + n]
             ab = [jnp.broadcast_to(ag[:, c0 + j:c0 + j + 1], (n, 128)) for j in range(n)]
             for t in range(3):
-                cols = slice(128 * t, 128 * t + 128)
-                acc = v[n * g:n * g + n, cols]
-                for j in range(n):
-                    acc = acc - ab[j] * ys[t][j]
-                v[n * g:n * g + n, cols] = acc
+                v[t, n * g:n * g + n] = v[t, n * g:n * g + n] - tree([ab[j] * ys[t][j] for j in range(n)])
 
 def dot_t(a, b):
     return lax.dot_general(a, b, (((0,), (0,)), ((), ())), precision=lax.Precision.HIGHEST, preferred_element_type=F32)
 
-def factor_kernel(total, pay, factor, inverse, exponents, v):
+def factor_kernel(total, pay, factor, inverse, exponents, v, held):
     h = 128
     ri = lax.broadcasted_iota(jnp.int32, (h, h), 0)
     ci = lax.broadcasted_iota(jnp.int32, (h, h), 1)
@@ -80,32 +80,32 @@
     fold = pay[0:h, :] / total
     turned = fold.T
     diag0 = jnp.broadcast_to(pay[2 * h:2 * h + 1, :], (h, h)) / total
-    v[:, 0:h] = jnp.where(ri == ci, diag0, jnp.where(ri < ci, turned, fold))
-    v[:, h:2 * h] = pay[h:2 * h, :] / total
-    v[:, 2 * h:3 * h] = eye
+    v[0] = jnp.where(ri == ci, diag0, jnp.where(ri < ci, turned, fold))
+    v[1] = pay[h:2 * h, :] / total
+    v[2] = eye
     rest = jnp.where(ri <= ci, fold, turned)
-    factor_block(v)
-    r00 = jnp.where(ri <= ci, v[:, 0:h], 0.0)
-    r01 = v[:, h:2 * h]
-    l00 = jnp.where(ri >= ci, v[:, 2 * h:3 * h], 0.0)
+    factor_block(v, held)
+    r00 = jnp.where(ri <= ci, v[0], 0.0)
+    r01 = v[1]
+    l00 = jnp.where(ri >= ci, v[2], 0.0)
     factor[0:h, 0:h] = r00
     factor[0:h, h:2 * h] = r01
     inverse[0:h, 0:h] = l00.astype(jnp.bfloat16)
     inverse[0:h, h:2 * h] = jnp.zeros((h, h), jnp.bfloat16)
     exponents[:, 0:h] = jnp.log(jnp.sum(r00 * eye, axis=0, keepdims=True))
-    v[:, 0:h] = rest - dot_t(r01, r01)
-    v[:, h:2 * h] = -dot_t(r01, l00)
-    v[:, 2 * h:3 * h] = eye
-    factor_block(v)
-    r11 = jnp.where(ri <= ci, v[:, 0:h], 0.0)
+    v[0] = rest - dot_t(r01, r01)
+    v[1] = -dot_t(r01, l00)
+    v[2] = eye
+    factor_block(v, held)
+    r11 = jnp.where(ri <= ci, v[0], 0.0)
     factor[h:2 * h, 0:h] = jnp.zeros((h, h), F32)
     factor[h:2 * h, h:2 * h] = r11
-    inverse[h:2 * h, 0:h] = v[:, h:2 * h].astype(jnp.bfloat16)
-    inverse[h:2 * h, h:2 * h] = jnp.where(ri >= ci, v[:, 2 * h:3 * h], 0.0).astype(jnp.bfloat16)
+    inverse[h:2 * h, 0:h] = v[1].astype(jnp.bfloat16)
+    inverse[h:2 * h, h:2 * h] = jnp.where(ri >= ci, v[2], 0.0).astype(jnp.bfloat16)
     exponents[:, h:2 * h] = jnp.log(jnp.sum(r11 * eye, axis=0, keepdims=True))
 
 
-def turn_kernel(source, target, tangent, wide, turned, read, write):
+def turn_kernel(source, low_tail, high_tail, side_tail, target, last, begin, side, tangent, wide, turned, read, write):
     fields, rows, lanes = tangent.shape
     pitch = rows + 1
     chunks = read.shape[0]
@@ -128,25 +128,40 @@
         loading(q).wait()
         lax.fori_loop(q * each, (q + 1) * each, widen, 0, unroll=8)
 
-    def turn_row(r, carry):
-        turned[r] = wide[pl.ds(r, fields, stride=pitch), :].T.astype(BF16)
+    def turn_rows(p, carry):
+        ends = []
+        for i in range(2):
+            r = 2 * p + i
+            line = wide[pl.ds(r, fields, stride=pitch), :].T
+            turned[r] = line.astype(BF16)
+            ends += [line[lanes - HALO:], line[:HALO]]
+        side[pl.ds(pl.multiple_of(p * 4 * HALO, 4 * HALO), 4 * HALO), :] = jnp.concatenate(ends).astype(BF16)
         return carry
 
     for q in range(chunks):
-        lax.fori_loop(q * lines, (q + 1) * lines, turn_row, 0, unroll=2)
+        lax.fori_loop(q * lines // 2, (q + 1) * lines // 2, turn_rows, 0)
         storing(q).start()
+    count = HALO * lanes
+    last[0:count] = turned[rows - HALO:].reshape(count, fields)
+    last[count:] = low_tail[...]
+    begin[0:count] = turned[:HALO].reshape(count, fields)
+    begin[count:] = high_tail[...]
+    side[2 * HALO * rows:] = side_tail[...]
     for q in range(chunks):
         storing(q).wait()
 
 
-def turn(tangent):
+def turn(tangent, tails):
     fields, rows, lanes = tangent.shape
     chunks = 8
+    hbm, vmem = pl.BlockSpec(memory_space=pltpu.HBM), pl.BlockSpec(memory_space=pltpu.VMEM)
+    matrix = [jax.ShapeDtypeStruct((cells + tail.shape[0], fields), BF16)
+              for cells, tail in zip((HALO * lanes, HALO * lanes, 2 * HALO * rows), tails)]
     return pl.pallas_call(
         turn_kernel,
-        in_specs=[pl.BlockSpec(memory_space=pltpu.HBM)],
-        out_specs=pl.BlockSpec(memory_space=pltpu.HBM),
-        out_shape=pltpu.HBM((rows, lanes, fields), BF16),
+        in_specs=[hbm, vmem, vmem, vmem],
+        out_specs=(hbm, vmem, vmem, vmem),
+        out_shape=(pltpu.HBM((rows, lanes, fields), BF16), *matrix),
         scratch_shapes=[
             pltpu.VMEM((fields, rows, lanes), BF16),
             pltpu.VMEM((fields * (rows + 1), lanes), F32),
@@ -155,7 +170,7 @@
             pltpu.SemaphoreType.DMA((chunks,)),
         ],
         compiler_params=pltpu.CompilerParams(vmem_limit_bytes=24 << 20),
-    )(pltpu.with_memory_space_constraint(tangent, pltpu.HBM))
+    )(pltpu.with_memory_space_constraint(tangent, pltpu.HBM), *tails)
 
 
 def evolve_kernel(source_block, low, high, sides, table, target_block, payload, first, second, coef, gram, own, read, write):
@@ -177,13 +192,10 @@
     halves = fields // LANES
     start_of = lambda r: GROUP + r * width
 
-    def spread(q, carry):
-        for m in range(3):
-            line = jnp.broadcast_to(table[m, pl.ds(q, 1)], (LANES, LANES))
-            coef[m, pl.ds(pl.multiple_of(q * LANES, LANES), LANES), :] = line.T
-        return carry
-
-    lax.fori_loop(0, table.shape[1], spread, 0, unroll=2)
+    for m in range(3):
+        turned_table = jnp.concatenate([table[m], jnp.zeros((LANES - table.shape[1], LANES), F32)]).T
+        for q in range(table.shape[1]):
+            coef[m, LANES * q:LANES * (q + 1), :] = jnp.broadcast_to(turned_table[:, q:q + 1], (LANES, LANES))
 
     def fill(row, block):
         for h in range(halves):
@@ -305,7 +317,7 @@
     )(pltpu.with_memory_space_constraint(own, pltpu.HBM), low, high, sides, table)
 
 
-def finish_kernel(total, pay, source, factor, exponents, basis, v, inverse, evolved, wide, out, read, write):
+def finish_kernel(total, pay, source, factor, exponents, basis, v, held, inverse, evolved, wide, out, read, write):
     rows, lanes, fields = evolved.shape
     chunks, step = out.shape[0], out.shape[2]
     pitch = step + 1
@@ -318,7 +330,7 @@
 
     for q in range(chunks):
         loading(q).start()
-    factor_kernel(total, pay, factor, inverse, exponents, v)
+    factor_kernel(total, pay, factor, inverse, exponents, v, held)
     for q in range(chunks):
         loading(q).wait()
         for r in range(0, step, 2):
@@ -352,7 +364,8 @@
             jax.ShapeDtypeStruct((fields, rows, lanes), BF16),
         ),
         scratch_shapes=[
-            pltpu.VMEM((LANES, 3 * LANES), F32),
+            pltpu.VMEM((3, LANES, LANES), F32),
+            pltpu.VMEM((2 * GROUP * GROUP, LANES), F32),
             pltpu.VMEM((fields, fields), BF16),
             pltpu.VMEM((rows, lanes, fields), BF16),
             pltpu.VMEM(((step + 1) * fields, lanes), F32),
@@ -408,11 +421,9 @@
     return wide[:count] + wide[count:2 * count] + wide[2 * count:]
 
 
-def loaded(state, parts):
-    fields = state.shape[-1]
+def tail_of(parts, fields):
     flat = parts.reshape(-1)
-    flat = jnp.pad(flat, (0, -flat.size % (PACKED * fields)))
-    return jnp.concatenate([state.reshape(-1, fields), flat.reshape(-1, fields)])
+    return jnp.pad(flat, (0, -flat.size % (PACKED * fields))).reshape(-1, fields)
 
 
 def unloaded(matrix, rows, cols):
@@ -426,30 +437,30 @@
     nx, ny = lax.axis_size("gx"), lax.axis_size("gy")
     block = jnp.stack([courant_x, courant_y, growth])
     parts = pieces(block)
-    own = turn(tangent)
 
     def edges(x, axis):
         size = x.shape[axis]
         return lax.slice_in_dim(x, size - HALO, size, axis=axis), lax.slice_in_dim(x, 0, HALO, axis=axis)
 
-    state_last, state_begin = edges(own, 1)
-    part_last, part_begin = edges(parts, 2)
-    if ny == 2:
-        both = loaded(jnp.concatenate([state_last, state_begin], axis=1), jnp.concatenate([part_last, part_begin], axis=2))
-        side, side_part = unloaded(shifted(both, 0, 1), rows, 2 * HALO)
-    else:
-        west, west_part = unloaded(shifted(loaded(state_last, part_last), 0, 1), rows, HALO)
-        east, east_part = unloaded(shifted(loaded(state_begin, part_begin), 0, -1), rows, HALO)
-        side, side_part = jnp.concatenate([west, east], axis=1), jnp.concatenate([west_part, east_part], axis=2)
-
-    def ends(state, part, count):
-        state_last, state_begin = edges(state, 0)
-        part_last, part_begin = edges(part, 1)
-        return (unloaded(shifted(loaded(state_last, part_last), 1, 0), HALO, count),
-                unloaded(shifted(loaded(state_begin, part_begin), -1, 0), HALO, count))
-
-    low, high = ends(own, parts, cols)
-    low_side, high_side = ends(side, side_part, 2 * HALO)
+    part_last, part_begin = edges(parts, 1)
+    part_side = jnp.concatenate(edges(parts, 2), axis=2)
+    own, last, begin, both = turn(tangent, [tail_of(part, fields) for part in (part_last, part_begin, part_side)])
+    low = unloaded(shifted(last, 1, 0), HALO, cols)
+    high = unloaded(shifted(begin, -1, 0), HALO, cols)
+    side, side_part = unloaded(shifted(both, 0, 1), rows, 2 * HALO)
+    if ny > 2:
+        east, east_part = unloaded(shifted(both, 0, -1), rows, 2 * HALO)
+        side = jnp.concatenate([side[:, :HALO], east[:, HALO:]], axis=1)
+        side_part = jnp.concatenate([side_part[:, :, :HALO], east_part[:, :, HALO:]], axis=2)
+
+    def corner(state, part, down):
+        matrix = jnp.concatenate([state.reshape(-1, fields), tail_of(part, fields)])
+        return unloaded(shifted(matrix, down, 0), HALO, 2 * HALO)
+
+    state_last, state_begin = edges(side, 0)
+    part_last, part_begin = edges(side_part, 1)
+    low_side = corner(state_last, part_last, 1)
+    high_side = corner(state_begin, part_begin, -1)
     sides = jnp.concatenate([low_side[0], side, high_side[0]])
     middle = jnp.concatenate([joined(low[1]), block, joined(high[1])], axis=1)
     around = joined(jnp.concatenate([low_side[1], side_part, high_side[1]], axis=1))

time: 93.7 us -> 87.2 us (0.931)
  Pallas kernels: 50.3 us -> 45.5 us
  starting transfers between devices: 13.6 us -> 18.3 us
  waiting for transfers between devices: 22.8 us -> 18.8 us
  local copies, waits for them, and re-layouts: 3.98 us -> 1.76 us
    ppermute x6, starting transfers between devices: 2.22 us -> 6.3 us  [swapped(): lax.ppermute(block, axis, [(i, i ^ bit) for i in range(lax.axis_size(axis...]
    ppermute x6, waiting for transfers between devices: 19 us -> 15.5 us  [swapped(): lax.ppermute(block, axis, [(i, i ^ bit) for i in range(lax.axis_size(axis...]
    pallas_call x1, Pallas kernels: 16.6 us -> 13.8 us  [finish(): pl.pallas_call(functools.partial(finish_kernel, total), in_specs=[vmem, h...]
    pallas_call x1, Pallas kernels: 27.1 us -> 25.2 us  [evolve(): pl.pallas_call(evolve_kernel, in_specs=[hbm, vmem, vmem, vmem, vmem], out...]
    slice x4 -> x3, local copies, waits for them, and re-layouts: 1.28 us -> 0.13 us  [edges(): lax.slice_in_dim(x, size - HALO, size, axis=axis)]
    slice x1 -> x0, local copies, waits for them, and re-layouts: 1.06 us -> none  [edges(): lax.slice_in_dim(x, 0, HALO, axis=axis)]
  transfers between devices with their start and end apart: 11 -> 11, of which waited for: 9 -> 8; matrix products, arithmetic and copies ran while one was open for 2% -> 1% of each run, Pallas kernels for 0% -> 0%
where the time goes in v4:
time: 87.2 us; the launch traced here: 87 us
  Pallas kernels  45.5 us (52%)
  waiting for transfers between devices  18.8 us (22%)
  starting transfers between devices  18.3 us (21%)
  local copies, waits for them, and re-layouts  1.76 us (2%)
  other arithmetic  1.36 us (2%)
  between operations  1.22 us (1%)
    pallas_call x1, Pallas kernels, evolve(): pl.pallas_call(evolve_kernel, in_specs=[hbm, vmem, vmem, vmem, vmem], out...  25.2 us
    ppermute x6, waiting for transfers between devices, swapped(): lax.ppermute(block, axis, [(i, i ^ bit) for i in range(lax.axis_size(axis...  15.5 us
    pallas_call x1, Pallas kernels, finish(): pl.pallas_call(functools.partial(finish_kernel, total), in_specs=[vmem, h...  13.8 us
    ppermute x5, starting transfers between devices, shifted(): return lax.ppermute(block, ('gx', 'gy'), pairs)  12 us
    pallas_call x1, Pallas kernels, turn(): pl.pallas_call(turn_kernel, in_specs=[hbm, vmem, vmem, vmem], out_specs=(...  6.56 us
    ppermute x6, starting transfers between devices, swapped(): lax.ppermute(block, axis, [(i, i ^ bit) for i in range(lax.axis_size(axis...  6.3 us
    ppermute x5, waiting for transfers between devices, shifted(): return lax.ppermute(block, ('gx', 'gy'), pairs)  3.37 us
  transfers between devices with their start and end apart: 11, of which 8 were waited for; matrix products, arithmetic and copies ran while one was open for 1% of the time, Pallas kernels for 0%

profile of v4, /device:TPU:0, one launch (start us, length us, event | category | flops | bytes accessed | tf_op | source)
XLA Modules:
  0.0 87.0 jit_solution(709349176704705787)
XLA Ops:
  0.6 0.8 reduce-precision_convert_fusion.1
  1.5 0.1 fusion.4
  1.6 0.1 pad_maximum_fusion.3
  1.7 0.2 reshape.104
  1.9 0.0 copy-start
  2.0 0.0 copy-start.1
  2.0 0.0 copy-start.2
  2.1 6.6 %shard_map.67 = (bf16[64,128,256]{2,1,0:T(8,128)(2,1)}, bf16[544,256]{1,0:T(8,128)(2,1)S(1)}, bf16[544,256]{1,0:T(8,128)(2,1)S(1)}, bf16[544,256]{1,0:T(8,128)(2,1)S(1)}) custom-call(bf16[256,64,128]{2,1,0:T(8,128)(2,1)} %source.1, bf16[32,256]{1,0:T(8,128)(2,1)S(1)} %reshape.101.low_tail, bf16[32,256]{1,0:T(8,128)(2,1)S(1)} %reshape.103.high_tail, ...), custom_call_target="tpu_custom_call" | custom-call | tf_op jit(solution)/shard_map/pallas_call | solution.py:160
  8.7 3.0 %collective-permute-start.2 = (bf16[544,256]{1,0:T(8,128)(2,1)S(1)}, bf16[544,256]{1,0:T(8,128)(2,1)S(1)}, u32[]{:S(2)}, u32[]{:S(2)}) collective-permute-start(bf16[544,256]{1,0:T(8,128)(2,1)S(1)} %get-tuple-element.15), channel_id=1, source_target_pairs={{0,1},{1,0},{2,3},{3,2},{4,5},{5,4},{6,7},{7,6},{8,9},{9,8},{10,11... | collective-permute-start | bytes 835592 | tf_op jit(solution)/shard_map/ppermute | solution.py:386
  11.7 0.0 collective-permute-start
  11.7 4.4 %collective-permute-start.1 = (bf16[544,256]{1,0:T(8,128)(2,1)S(1)}, bf16[544,256]{1,0:T(8,128)(2,1)S(1)}, u32[]{:S(2)}, u32[]{:S(2)}) collective-permute-start(bf16[544,256]{1,0:T(8,128)(2,1)S(1)} %get-tuple-element.14), channel_id=1, source_target_pairs={{0,30},{1,31},{2,0},{3,1},{4,2},{5,3},{6,4},{7,5},{8,6},{9,7},{10,... | collective-permute-start | bytes 835592 | tf_op jit(solution)/shard_map/ppermute | solution.py:386
  16.1 2.2 %collective-permute-done.2 = bf16[544,256]{1,0:T(8,128)(2,1)S(1)} collective-permute-done((bf16[544,256]{1,0:T(8,128)(2,1)S(1)}, bf16[544,256]{1,0:T(8,128)(2,1)S(1)}, u32[]{:S(2)}, u32[]{:S(2)}) %collective-permute-start.2) | collective-permute-done | bytes 278560 | tf_op jit(solution)/shard_map/ppermute | solution.py:386
  18.3 0.2 reshape.108
  18.6 0.1 reshape.109
  18.7 0.1 collective-permute-start.3
  18.8 0.1 reshape.113
  18.9 4.5 %collective-permute-start.4 = (bf16[48,256]{1,0:T(8,128)(2,1)S(1)}, bf16[48,256]{1,0:T(8,128)(2,1)S(1)}, u32[]{:S(2)}, u32[]{:S(2)}) collective-permute-start(bf16[48,256]{1,0:T(8,128)(2,1)S(1)} %pad_maximum_fusion.6), channel_id=1, source_target_pairs={{0,30},{1,31},{2,0},{3,1},{4,2},{5,3},{6,4},{7,5},{8,6},{9,7},{10,... | collective-permute-start | bytes 73736 | tf_op jit(solution)/shard_map/ppermute | solution.py:386
  23.4 0.0 collective-permute-done
  23.4 0.0 collective-permute-done.1
  23.5 1.2 %collective-permute-done.3 = bf16[48,256]{1,0:T(8,128)(2,1)S(1)} collective-permute-done((bf16[48,256]{1,0:T(8,128)(2,1)S(1)}, bf16[48,256]{1,0:T(8,128)(2,1)S(1)}, u32[]{:S(2)}, u32[]{:S(2)}) %collective-permute-start.3) | collective-permute-done | bytes 24608 | tf_op jit(solution)/shard_map/ppermute | solution.py:386
  24.7 0.2 slice.133
  24.9 0.0 collective-permute-done.4
  24.9 0.2 slice.136
  25.1 0.1 maximum_convert_fusion
  25.2 0.1 fusion.5
  25.3 0.0 copy-done
  25.3 0.0 copy-done.1
  25.4 0.0 copy-done.2
  25.4 0.2 pad_maximum_fusion.1
  25.5 0.2 reshape.116
  25.8 0.1 reshape.117.table
  26.0 25.2 %shard_map.68 = (bf16[64,128,256]{2,1,0:T(8,128)(2,1)}, f32[272,128]{1,0:T(8,128)S(1)}) custom-call(bf16[64,128,256]{2,1,0:T(8,128)(2,1)} %get-tuple-element.12.source_block, bf16[4,128,256]{2,1,0:T(8,128)(2,1)S(1)} %bitcast.12, bf16[4,128,256]{2,1,0:T(8,128)(2,1)S(1)} %bitcast.13, bf16[72,8,256]{2,1,0:T(8,128)(2,1)S(1)} %pad_maximum_fusion.sides, ...), custom_call_target="tpu_custom_call" | custom-call | tf_op jit(solution)/shard_map/pallas_call | solution.py:299
  51.2 0.1 collective-permute-start.5
  51.2 1.2 %collective-permute-done.5 = f32[136,128]{1,0:T(8,128)S(1)} collective-permute-done((f32[136,128]{1,0:T(8,128)S(1)}, f32[136,128]{1,0:T(8,128)S(1)}, u32[]{:S(2)}, u32[]{:S(2)}) %collective-permute-start.5) | collective-permute-done | bytes 69664 | tf_op jit(solution)/shard_map/ppermute | solution.py:390
  52.5 1.8 %collective-permute-start.6 = (f32[136,128]{1,0:T(8,128)S(1)}, f32[136,128]{1,0:T(8,128)S(1)}, u32[]{:S(2)}, u32[]{:S(2)}) collective-permute-start(f32[136,128]{1,0:T(8,128)S(1)} %dynamic-slice_add_fusion), channel_id=1, source_target_pairs={{0,1},{1,0},{2,3},{3,2},{4,5},{5,4},{6,7},{7,6},{8,9},{9,8},{10,11... | collective-permute-start | bytes 208904 | tf_op jit(solution)/shard_map/ppermute | solution.py:390
  54.3 2.6 %collective-permute-done.6 = f32[136,128]{1,0:T(8,128)S(1)} collective-permute-done((f32[136,128]{1,0:T(8,128)S(1)}, f32[136,128]{1,0:T(8,128)S(1)}, u32[]{:S(2)}, u32[]{:S(2)}) %collective-permute-start.6) | collective-permute-done | bytes 69664 | tf_op jit(solution)/shard_map/ppermute | solution.py:390
  56.9 1.4 %collective-permute-start.7 = (f32[136,128]{1,0:T(8,128)S(1)}, f32[136,128]{1,0:T(8,128)S(1)}, u32[]{:S(2)}, u32[]{:S(2)}) collective-permute-start(f32[136,128]{1,0:T(8,128)S(1)} %add.75), channel_id=1, source_target_pairs={{0,4},{2,6},{4,0},{6,2},{8,12},{10,14},{12,8},{14,10},{16,20},{18,... | collective-permute-start | bytes 208904 | tf_op jit(solution)/shard_map/ppermute | solution.py:390
  58.3 3.0 %collective-permute-done.7 = f32[136,128]{1,0:T(8,128)S(1)} collective-permute-done((f32[136,128]{1,0:T(8,128)S(1)}, f32[136,128]{1,0:T(8,128)S(1)}, u32[]{:S(2)}, u32[]{:S(2)}) %collective-permute-start.7) | collective-permute-done | bytes 69664 | tf_op jit(solution)/shard_map/ppermute | solution.py:390
  61.3 1.0 %collective-permute-start.8 = (f32[136,128]{1,0:T(8,128)S(1)}, f32[136,128]{1,0:T(8,128)S(1)}, u32[]{:S(2)}, u32[]{:S(2)}) collective-permute-start(f32[136,128]{1,0:T(8,128)S(1)} %add.76), channel_id=1, source_target_pairs={{0,8},{2,10},{4,12},{6,14},{8,0},{10,2},{12,4},{14,6},{16,24},{18,... | collective-permute-start | bytes 208904 | tf_op jit(solution)/shard_map/ppermute | solution.py:390
  62.2 3.4 %collective-permute-done.8 = f32[136,128]{1,0:T(8,128)S(1)} collective-permute-done((f32[136,128]{1,0:T(8,128)S(1)}, f32[136,128]{1,0:T(8,128)S(1)}, u32[]{:S(2)}, u32[]{:S(2)}) %collective-permute-start.8) | collective-permute-done | bytes 69664 | tf_op jit(solution)/shard_map/ppermute | solution.py:390
  65.7 2.0 %collective-permute-start.9 = (f32[136,128]{1,0:T(8,128)S(1)}, f32[136,128]{1,0:T(8,128)S(1)}, u32[]{:S(2)}, u32[]{:S(2)}) collective-permute-start(f32[136,128]{1,0:T(8,128)S(1)} %add.77), channel_id=1, source_target_pairs={{0,16},{2,18},{4,20},{6,22},{8,24},{10,26},{12,28},{14,30},{16,0},... | collective-permute-start | bytes 208904 | tf_op jit(solution)/shard_map/ppermute | solution.py:390
  67.6 4.0 %collective-permute-done.9 = f32[136,128]{1,0:T(8,128)S(1)} collective-permute-done((f32[136,128]{1,0:T(8,128)S(1)}, f32[136,128]{1,0:T(8,128)S(1)}, u32[]{:S(2)}, u32[]{:S(2)}) %collective-permute-start.9) | collective-permute-done | bytes 69664 | tf_op jit(solution)/shard_map/ppermute | solution.py:390
  71.7 0.1 collective-permute-start.10
  71.8 1.2 %collective-permute-done.10 = f32[136,128]{1,0:T(8,128)S(1)} collective-permute-done((f32[136,128]{1,0:T(8,128)S(1)}, f32[136,128]{1,0:T(8,128)S(1)}, u32[]{:S(2)}, u32[]{:S(2)}) %collective-permute-start.10) | collective-permute-done | bytes 69664 | tf_op jit(solution)/shard_map/ppermute | solution.py:390
  73.0 13.8 %shard_map.69 = (f32[256,256]{1,0:T(8,128)}, f32[1,256]{1,0:T(1,128)}, bf16[256,64,128]{2,1,0:T(8,128)(2,1)}) custom-call(f32[272,128]{1,0:T(8,128)S(1)} %maximum_select_fusion.pay, bf16[64,128,256]{2,1,0:T(8,128)(2,1)} %get-tuple-element.17.source), custom_call_target="tpu_custom_call" | custom-call | tf_op jit(solution)/shard_map/pallas_call | solution.py:357
  (44 shorter events, 0.5 us)
Async XLA Ops:
  1.9 23.4 %copy-start = (f32[64,128]{1,0:T(8,128)S(1)}, f32[64,128]{1,0:T(8,128)}, u32[]{:S(2)}) copy-start(f32[64,128]{1,0:T(8,128)} %param.7) | copy-start | bytes 98308
  2.0 23.4 %copy-start.1 = (f32[64,128]{1,0:T(8,128)S(1)}, f32[64,128]{1,0:T(8,128)}, u32[]{:S(2)}) copy-start(f32[64,128]{1,0:T(8,128)} %param.6) | copy-start | bytes 98308
  2.0 23.4 %copy-start.2 = (f32[64,128]{1,0:T(8,128)S(1)}, f32[64,128]{1,0:T(8,128)}, u32[]{:S(2)}) copy-start(f32[64,128]{1,0:T(8,128)} %param.5) | copy-start | bytes 98308
  8.7 9.7 %collective-permute-start.2 = (bf16[544,256]{1,0:T(8,128)(2,1)S(1)}, bf16[544,256]{1,0:T(8,128)(2,1)S(1)}, u32[]{:S(2)}, u32[]{:S(2)}) collective-permute-start(bf16[544,256]{1,0:T(8,128)(2,1)S(1)} %get-tuple-element.15), channel_id=1, source_target_pairs={{0,1},{1,0},{2,3},{3,2},{4,5},{5,4},{6,7},{7,6},{8,9},{9,8},{10,11... | collective-permute-start | bytes 835592 | tf_op jit(solution)/shard_map/ppermute | solution.py:386
  11.7 11.7 %collective-permute-start = (bf16[544,256]{1,0:T(8,128)(2,1)S(1)}, bf16[544,256]{1,0:T(8,128)(2,1)S(1)}, u32[]{:S(2)}, u32[]{:S(2)}) collective-permute-start(bf16[544,256]{1,0:T(8,128)(2,1)S(1)} %get-tuple-element.13), channel_id=1, source_target_pairs={{0,2},{1,3},{2,4},{3,5},{4,6},{5,7},{6,8},{7,9},{8,10},{9,11},{10,... | collective-permute-start | bytes 835592 | tf_op jit(solution)/shard_map/ppermute | solution.py:386
  11.7 11.8 %collective-permute-start.1 = (bf16[544,256]{1,0:T(8,128)(2,1)S(1)}, bf16[544,256]{1,0:T(8,128)(2,1)S(1)}, u32[]{:S(2)}, u32[]{:S(2)}) collective-permute-start(bf16[544,256]{1,0:T(8,128)(2,1)S(1)} %get-tuple-element.14), channel_id=1, source_target_pairs={{0,30},{1,31},{2,0},{3,1},{4,2},{5,3},{6,4},{7,5},{8,6},{9,7},{10,... | collective-permute-start | bytes 835592 | tf_op jit(solution)/shard_map/ppermute | solution.py:386
  18.7 6.0 %collective-permute-start.3 = (bf16[48,256]{1,0:T(8,128)(2,1)S(1)}, bf16[48,256]{1,0:T(8,128)(2,1)S(1)}, u32[]{:S(2)}, u32[]{:S(2)}) collective-permute-start(bf16[48,256]{1,0:T(8,128)(2,1)S(1)} %pad_maximum_fusion.5), channel_id=1, source_target_pairs={{0,2},{1,3},{2,4},{3,5},{4,6},{5,7},{6,8},{7,9},{8,10},{9,11},{10,... | collective-permute-start | bytes 73736 | tf_op jit(solution)/shard_map/ppermute | solution.py:386
  18.9 6.0 %collective-permute-start.4 = (bf16[48,256]{1,0:T(8,128)(2,1)S(1)}, bf16[48,256]{1,0:T(8,128)(2,1)S(1)}, u32[]{:S(2)}, u32[]{:S(2)}) collective-permute-start(bf16[48,256]{1,0:T(8,128)(2,1)S(1)} %pad_maximum_fusion.6), channel_id=1, source_target_pairs={{0,30},{1,31},{2,0},{3,1},{4,2},{5,3},{6,4},{7,5},{8,6},{9,7},{10,... | collective-permute-start | bytes 73736 | tf_op jit(solution)/shard_map/ppermute | solution.py:386
  51.2 1.3 %collective-permute-start.5 = (f32[136,128]{1,0:T(8,128)S(1)}, f32[136,128]{1,0:T(8,128)S(1)}, u32[]{:S(2)}, u32[]{:S(2)}) collective-permute-start(f32[136,128]{1,0:T(8,128)S(1)} %constant_dynamic-slice_fusion), channel_id=1, source_target_pairs={{0,2},{2,0},{4,6},{6,4},{8,10},{10,8},{12,14},{14,12},{16,18},{18,... | collective-permute-start | bytes 208904 | tf_op jit(solution)/shard_map/ppermute | solution.py:390
  52.5 4.4 %collective-permute-start.6 = (f32[136,128]{1,0:T(8,128)S(1)}, f32[136,128]{1,0:T(8,128)S(1)}, u32[]{:S(2)}, u32[]{:S(2)}) collective-permute-start(f32[136,128]{1,0:T(8,128)S(1)} %dynamic-slice_add_fusion), channel_id=1, source_target_pairs={{0,1},{1,0},{2,3},{3,2},{4,5},{5,4},{6,7},{7,6},{8,9},{9,8},{10,11... | collective-permute-start | bytes 208904 | tf_op jit(solution)/shard_map/ppermute | solution.py:390
  56.9 4.4 %collective-permute-start.7 = (f32[136,128]{1,0:T(8,128)S(1)}, f32[136,128]{1,0:T(8,128)S(1)}, u32[]{:S(2)}, u32[]{:S(2)}) collective-permute-start(f32[136,128]{1,0:T(8,128)S(1)} %add.75), channel_id=1, source_target_pairs={{0,4},{2,6},{4,0},{6,2},{8,12},{10,14},{12,8},{14,10},{16,20},{18,... | collective-permute-start | bytes 208904 | tf_op jit(solution)/shard_map/ppermute | solution.py:390
  61.3 4.4 %collective-permute-start.8 = (f32[136,128]{1,0:T(8,128)S(1)}, f32[136,128]{1,0:T(8,128)S(1)}, u32[]{:S(2)}, u32[]{:S(2)}) collective-permute-start(f32[136,128]{1,0:T(8,128)S(1)} %add.76), channel_id=1, source_target_pairs={{0,8},{2,10},{4,12},{6,14},{8,0},{10,2},{12,4},{14,6},{16,24},{18,... | collective-permute-start | bytes 208904 | tf_op jit(solution)/shard_map/ppermute | solution.py:390
  65.7 6.0 %collective-permute-start.9 = (f32[136,128]{1,0:T(8,128)S(1)}, f32[136,128]{1,0:T(8,128)S(1)}, u32[]{:S(2)}, u32[]{:S(2)}) collective-permute-start(f32[136,128]{1,0:T(8,128)S(1)} %add.77), channel_id=1, source_target_pairs={{0,16},{2,18},{4,20},{6,22},{8,24},{10,26},{12,28},{14,30},{16,0},... | collective-permute-start | bytes 208904 | tf_op jit(solution)/shard_map/ppermute | solution.py:390
  71.7 1.3 %collective-permute-start.10 = (f32[136,128]{1,0:T(8,128)S(1)}, f32[136,128]{1,0:T(8,128)S(1)}, u32[]{:S(2)}, u32[]{:S(2)}) collective-permute-start(f32[136,128]{1,0:T(8,128)S(1)} %add.78), channel_id=1, source_target_pairs={{0,2},{2,0},{4,6},{6,4},{8,10},{10,8},{12,14},{14,12},{16,18},{18,... | collective-permute-start | bytes 208904 | tf_op jit(solution)/shard_map/ppermute | solution.py:390

commit v5 on v4

--- a/solution.py
+++ b/solution.py
@@ -15,6 +15,7 @@
 GROUP = 8
 EDGE = 2 * HALO
 PACKED = 16
+TALL = 4
 
 
 def tree(terms):
@@ -106,40 +107,38 @@
 
 
 def turn_kernel(source, low_tail, high_tail, side_tail, target, last, begin, side, tangent, wide, turned, read, write):
-    fields, rows, lanes = tangent.shape
-    pitch = rows + 1
-    chunks = read.shape[0]
-    each, lines = fields // chunks, rows // chunks
+    chunks, fields, lines, lanes = tangent.shape
+    rows = chunks * lines
+    pitch = lines + 1
 
     def loading(q):
-        return pltpu.make_async_copy(source.at[pl.ds(q * each, each)], tangent.at[pl.ds(q * each, each)], read.at[q])
+        return pltpu.make_async_copy(source.at[:, pl.ds(q * lines, lines)], tangent.at[q], read.at[q])
 
     def storing(q):
         return pltpu.make_async_copy(turned.at[pl.ds(q * lines, lines)], target.at[pl.ds(q * lines, lines)], write.at[q])
 
     for q in range(chunks):
         loading(q).start()
-
-    def widen(f, carry):
-        wide[pl.ds(f * pitch, rows), :] = tangent[f].astype(F32)
-        return carry
-
     for q in range(chunks):
         loading(q).wait()
-        lax.fori_loop(q * each, (q + 1) * each, widen, 0, unroll=8)
-
-    def turn_rows(p, carry):
-        ends = []
-        for i in range(2):
-            r = 2 * p + i
-            line = wide[pl.ds(r, fields, stride=pitch), :].T
-            turned[r] = line.astype(BF16)
-            ends += [line[lanes - HALO:], line[:HALO]]
-        side[pl.ds(pl.multiple_of(p * 4 * HALO, 4 * HALO), 4 * HALO), :] = jnp.concatenate(ends).astype(BF16)
-        return carry
-
-    for q in range(chunks):
-        lax.fori_loop(q * lines // 2, (q + 1) * lines // 2, turn_rows, 0)
+
+        def widen(f, carry):
+            wide[pl.ds(f * pitch, lines), :] = tangent[q, f].astype(F32)
+            return carry
+
+        lax.fori_loop(0, fields, widen, 0, unroll=16)
+
+        def turn_rows(p, carry):
+            ends = []
+            for i in range(2):
+                line = wide[pl.ds(2 * p + i, fields, stride=pitch), :].T
+                turned[q * lines + 2 * p + i] = line.astype(BF16)
+                ends += [line[lanes - HALO:], line[:HALO]]
+            at = pl.multiple_of((q * lines + 2 * p) * 2 * HALO, 4 * HALO)
+            side[pl.ds(at, 4 * HALO), :] = jnp.concatenate(ends).astype(BF16)
+            return carry
+
+        lax.fori_loop(0, lines // 2, turn_rows, 0, unroll=2)
         storing(q).start()
     count = HALO * lanes
     last[0:count] = turned[rows - HALO:].reshape(count, fields)
@@ -153,7 +152,8 @@
 
 def turn(tangent, tails):
     fields, rows, lanes = tangent.shape
-    chunks = 8
+    lines = 16
+    chunks = rows // lines
     hbm, vmem = pl.BlockSpec(memory_space=pltpu.HBM), pl.BlockSpec(memory_space=pltpu.VMEM)
     matrix = [jax.ShapeDtypeStruct((cells + tail.shape[0], fields), BF16)
               for cells, tail in zip((HALO * lanes, HALO * lanes, 2 * HALO * rows), tails)]
@@ -163,8 +163,8 @@
         out_specs=(hbm, vmem, vmem, vmem),
         out_shape=(pltpu.HBM((rows, lanes, fields), BF16), *matrix),
         scratch_shapes=[
-            pltpu.VMEM((fields, rows, lanes), BF16),
-            pltpu.VMEM((fields * (rows + 1), lanes), F32),
+            pltpu.VMEM((chunks, fields, lines, lanes), BF16),
+            pltpu.VMEM((fields * (lines + 1), lanes), F32),
             pltpu.VMEM((rows, lanes, fields), BF16),
             pltpu.SemaphoreType.DMA((chunks,)),
             pltpu.SemaphoreType.DMA((chunks,)),
@@ -211,7 +211,7 @@
 
     for q in range(chunks):
         loading(q).wait()
-        lax.fori_loop(q * lines, (q + 1) * lines, fill_own, 0)
+        lax.fori_loop(q * lines, (q + 1) * lines, fill_own, 0, unroll=2)
 
     def fill_sides(r, carry):
         pair = sides[r].astype(F32)
@@ -220,34 +220,40 @@
             first[h, pl.ds(start_of(r) + HALO + lanes, HALO), :] = pair[HALO:, LANES * h:LANES * (h + 1)]
         return carry
 
-    lax.fori_loop(0, rows + 2 * HALO, fill_sides, 0)
+    lax.fori_loop(0, rows + 2 * HALO, fill_sides, 0, unroll=4)
 
     def weights(at):
-        cx, cy, gr = [coef[m, pl.ds(at, GROUP), :] for m in range(3)]
-        return 0.2 + gr, 0.2 - cx, 0.2 + cx, 0.2 - cy, 0.2 + cy
+        north, east, centre = [coef[m, pl.ds(at, GROUP), :] for m in range(3)]
+        return centre, north, 0.4 - north, east, 0.4 - east
 
     def combine(f, c, n, s, e, w):
         return f[0] * c + (f[1] * n + f[2] * s) + (f[3] * e + f[4] * w)
 
-    def pair_of(source, at, f):
+    def advanced(source, at, f):
+        count = len(f)
         for h in range(halves):
-            value = [source[h, pl.ds(at + width * i, GROUP), :] for i in range(-1, 3)]
-            east = [source[h, pl.ds(at + width * i + 1, GROUP), :] for i in range(2)]
-            west = [source[h, pl.ds(at + width * i - 1, GROUP), :] for i in range(2)]
-            yield [combine(f[i], value[i + 1], value[i + 2], value[i], east[i], west[i]) for i in range(2)]
+            value = [source[h, pl.ds(at + width * i, GROUP), :] for i in range(-1, count + 1)]
+            east = [source[h, pl.ds(at + width * i + 1, GROUP), :] for i in range(count)]
+            west = [source[h, pl.ds(at + width * i - 1, GROUP), :] for i in range(count)]
+            yield [combine(f[i], value[i + 1], value[i + 2], value[i], east[i], west[i]) for i in range(count)]
 
     def substep(source, target, step):
-        def pair(p, carry):
-            r = step + 2 * p
+        def some_rows(r, count):
             for t in range(width // GROUP):
                 at = pl.multiple_of(start_of(r) + GROUP * t, GROUP)
-                f = [weights(at - GROUP + width * i) for i in range(2)]
-                for h, out in enumerate(pair_of(source, at, f)):
-                    for i in range(2):
+                f = [weights(at - GROUP + width * i) for i in range(count)]
+                for h, out in enumerate(advanced(source, at, f)):
+                    for i in range(count):
                         target[h, pl.ds(at + width * i, GROUP), :] = out[i]
+
+        def block(p, carry):
+            some_rows(step + TALL * p, TALL)
             return carry
 
-        lax.fori_loop(0, (rows + 2 * (HALO - step)) // 2, pair, 0)
+        count = rows + 2 * (HALO - step)
+        lax.fori_loop(0, count // TALL, block, 0)
+        if count % TALL:
+            some_rows(step + count // TALL * TALL, count % TALL)
 
     buffers = [first, second]
     for step in range(1, SUBSTEPS):
@@ -257,21 +263,21 @@
     chunk = lines
 
     def last_chunk(q, carry):
-        def pair(p, inner):
-            r = q * chunk + 2 * p
+        def block(p, inner):
+            r = q * chunk + TALL * p
             for t in range(0, lanes // GROUP, 2):
                 parts = []
                 for u in range(2):
                     at = start_of(HALO + r) + HALO + GROUP * (t + u)
-                    f = [weights(at - GROUP + width * i) for i in range(2)]
-                    parts.append(list(pair_of(source, at, f)))
-                for i in range(2):
+                    f = [weights(at - GROUP + width * i) for i in range(TALL)]
+                    parts.append(list(advanced(source, at, f)))
+                for i in range(TALL):
                     for h in range(halves):
                         both = jnp.concatenate([parts[0][h][i], parts[1][h][i]], axis=0).astype(BF16)
                         evolved[r + i, GROUP * t:GROUP * (t + 2), LANES * h:LANES * (h + 1)] = both
             return inner
 
-        lax.fori_loop(0, chunk // 2, pair, 0)
+        lax.fori_loop(0, chunk // TALL, block, 0)
         part = evolved[pl.ds(q * chunk, chunk)].reshape(chunk * lanes, fields)
         gram[...] += lax.dot_general(part, part, (((0,), (0,)), ((), ())), preferred_element_type=F32)
         storing(q).start()
@@ -343,7 +349,7 @@
             out[q, f] = wide[pl.ds(f * pitch, step), :].astype(BF16)
             return carry
 
-        lax.fori_loop(0, fields, narrow, 0, unroll=8)
+        lax.fori_loop(0, fields, narrow, 0, unroll=64)
         storing(q).start()
     for q in range(chunks):
         storing(q).wait()
@@ -464,7 +470,8 @@
     sides = jnp.concatenate([low_side[0], side, high_side[0]])
     middle = jnp.concatenate([joined(low[1]), block, joined(high[1])], axis=1)
     around = joined(jnp.concatenate([low_side[1], side_part, high_side[1]], axis=1))
-    table = jnp.concatenate([around[:, :, :HALO], middle, around[:, :, HALO:]], axis=2).reshape(3, -1)
+    table = jnp.concatenate([around[:, :, :HALO], middle, around[:, :, HALO:]], axis=2)
+    table = jnp.stack([0.2 - table[0], 0.2 - table[1], 0.2 + table[2]]).reshape(3, -1)
     table = jnp.pad(table, ((0, 0), (0, -table.shape[1] % LANES))).reshape(3, -1, LANES)
     evolved, payload = evolve(own, low[0], high[0], sides, table)
     total = float(rows * nx * cols * ny)

time: 87.2 us -> 81.7 us (0.937)
  Pallas kernels: 45.5 us -> 39.7 us
    pallas_call x1, Pallas kernels: 25.2 us -> 21.2 us  [evolve(): pl.pallas_call(evolve_kernel, in_specs=[hbm, vmem, vmem, vmem, vmem], out...]
    pallas_call x1, Pallas kernels: 6.56 us -> 5.24 us  [turn(): pl.pallas_call(turn_kernel, in_specs=[hbm, vmem, vmem, vmem], out_specs=(...]
where the time goes in v5:
time: 81.7 us; the launch traced here: 81.5 us
  Pallas kernels  39.7 us (49%)
  waiting for transfers between devices  18.9 us (23%)
  starting transfers between devices  18.3 us (22%)
  local copies, waits for them, and re-layouts  1.92 us (2%)
  other arithmetic  1.49 us (2%)
  between operations  1.24 us (2%)
    pallas_call x1, Pallas kernels, evolve(): pl.pallas_call(evolve_kernel, in_specs=[hbm, vmem, vmem, vmem, vmem], out...  21.2 us
    ppermute x6, waiting for transfers between devices, swapped(): lax.ppermute(block, axis, [(i, i ^ bit) for i in range(lax.axis_size(axis...  15.5 us
    pallas_call x1, Pallas kernels, finish(): pl.pallas_call(functools.partial(finish_kernel, total), in_specs=[vmem, h...  13.2 us
    ppermute x5, starting transfers between devices, shifted(): return lax.ppermute(block, ('gx', 'gy'), pairs)  12 us
    ppermute x6, starting transfers between devices, swapped(): lax.ppermute(block, axis, [(i, i ^ bit) for i in range(lax.axis_size(axis...  6.27 us
    pallas_call x1, Pallas kernels, turn(): pl.pallas_call(turn_kernel, in_specs=[hbm, vmem, vmem, vmem], out_specs=(...  5.24 us
    ppermute x5, waiting for transfers between devices, shifted(): return lax.ppermute(block, ('gx', 'gy'), pairs)  3.37 us
  transfers between devices with their start and end apart: 11, of which 8 were waited for; matrix products, arithmetic and copies ran while one was open for 1% of the time, Pallas kernels for 0%

profile of v5, /device:TPU:0, one launch (start us, length us, event | category | flops | bytes accessed | tf_op | source)
XLA Modules:
  0.0 81.5 jit_solution(10297855186866418255)
XLA Ops:
  0.6 0.8 %reduce-precision_convert_fusion.1 = (bf16[3,64,128]{2,1,0:T(8,128)(2,1)S(1)}, bf16[3,64,128]{2,1,0:T(8,128)(2,1)S(1)}, bf16[3,64,128]{2,1,0:T(8,128)(2,1)S(1)}) fusion(f32[1,64,128]{2,1,0:T(8,128)} %bitcast.14, f32[1,64,128]{2,1,0:T(8,128)} %bitcast.16, f32[1,64,128]{2,1,0:T(8,128)} %bitcast.18), kind=kLoop, calls=%fused_computation.12 | loop fusion | flops 245760 | bytes 245760 | tf_op jit(solution)/shard_map/convert_element_type | solution.py:419
  1.5 0.1 fusion.4
  1.6 0.1 pad_maximum_fusion.3
  1.7 0.2 reshape.105
  1.9 0.0 copy-start
  2.0 0.0 copy-start.1
  2.0 0.0 copy-start.2
  2.1 5.2 %shard_map.67 = (bf16[64,128,256]{2,1,0:T(8,128)(2,1)}, bf16[544,256]{1,0:T(8,128)(2,1)S(1)}, bf16[544,256]{1,0:T(8,128)(2,1)S(1)}, bf16[544,256]{1,0:T(8,128)(2,1)S(1)}) custom-call(bf16[256,64,128]{2,1,0:T(8,128)(2,1)} %source.1, bf16[32,256]{1,0:T(8,128)(2,1)S(1)} %reshape.102.low_tail, bf16[32,256]{1,0:T(8,128)(2,1)S(1)} %reshape.104.high_tail, ...), custom_call_target="tpu_custom_call" | custom-call | tf_op jit(solution)/shard_map/pallas_call | solution.py:160
  7.3 3.0 %collective-permute-start.2 = (bf16[544,256]{1,0:T(8,128)(2,1)S(1)}, bf16[544,256]{1,0:T(8,128)(2,1)S(1)}, u32[]{:S(2)}, u32[]{:S(2)}) collective-permute-start(bf16[544,256]{1,0:T(8,128)(2,1)S(1)} %get-tuple-element.15), channel_id=1, source_target_pairs={{0,1},{1,0},{2,3},{3,2},{4,5},{5,4},{6,7},{7,6},{8,9},{9,8},{10,11... | collective-permute-start | bytes 835592 | tf_op jit(solution)/shard_map/ppermute | solution.py:392
  10.3 0.0 collective-permute-start
  10.3 4.4 %collective-permute-start.1 = (bf16[544,256]{1,0:T(8,128)(2,1)S(1)}, bf16[544,256]{1,0:T(8,128)(2,1)S(1)}, u32[]{:S(2)}, u32[]{:S(2)}) collective-permute-start(bf16[544,256]{1,0:T(8,128)(2,1)S(1)} %get-tuple-element.14), channel_id=1, source_target_pairs={{0,30},{1,31},{2,0},{3,1},{4,2},{5,3},{6,4},{7,5},{8,6},{9,7},{10,... | collective-permute-start | bytes 835592 | tf_op jit(solution)/shard_map/ppermute | solution.py:392
  14.8 2.2 %collective-permute-done.2 = bf16[544,256]{1,0:T(8,128)(2,1)S(1)} collective-permute-done((bf16[544,256]{1,0:T(8,128)(2,1)S(1)}, bf16[544,256]{1,0:T(8,128)(2,1)S(1)}, u32[]{:S(2)}, u32[]{:S(2)}) %collective-permute-start.2) | collective-permute-done | bytes 278560 | tf_op jit(solution)/shard_map/ppermute | solution.py:392
  17.0 0.2 reshape.109
  17.2 0.1 reshape.110
  17.4 0.1 collective-permute-start.3
  17.4 0.1 reshape.114
  17.6 4.5 %collective-permute-start.4 = (bf16[48,256]{1,0:T(8,128)(2,1)S(1)}, bf16[48,256]{1,0:T(8,128)(2,1)S(1)}, u32[]{:S(2)}, u32[]{:S(2)}) collective-permute-start(bf16[48,256]{1,0:T(8,128)(2,1)S(1)} %pad_maximum_fusion.6), channel_id=1, source_target_pairs={{0,30},{1,31},{2,0},{3,1},{4,2},{5,3},{6,4},{7,5},{8,6},{9,7},{10,... | collective-permute-start | bytes 73736 | tf_op jit(solution)/shard_map/ppermute | solution.py:392
  22.1 0.0 collective-permute-done
  22.1 0.0 collective-permute-done.1
  22.2 1.2 %collective-permute-done.3 = bf16[48,256]{1,0:T(8,128)(2,1)S(1)} collective-permute-done((bf16[48,256]{1,0:T(8,128)(2,1)S(1)}, bf16[48,256]{1,0:T(8,128)(2,1)S(1)}, u32[]{:S(2)}, u32[]{:S(2)}) %collective-permute-start.3) | collective-permute-done | bytes 24608 | tf_op jit(solution)/shard_map/ppermute | solution.py:392
  23.4 0.2 slice.142
  23.6 0.0 collective-permute-done.4
  23.6 0.2 slice.145
  23.8 0.1 maximum_convert_fusion
  23.9 0.1 fusion.5
  24.0 0.0 copy-done
  24.0 0.0 copy-done.1
  24.0 0.0 copy-done.2
  24.0 0.2 pad_maximum_fusion.1
  24.2 0.1 stack.28
  24.4 0.1 stack.29
  24.5 0.1 stack.30
  24.7 0.1 select_maximum_fusion
  24.8 0.1 reshape.117.table
  24.9 21.2 %shard_map.68 = (bf16[64,128,256]{2,1,0:T(8,128)(2,1)}, f32[272,128]{1,0:T(8,128)S(1)}) custom-call(bf16[64,128,256]{2,1,0:T(8,128)(2,1)} %get-tuple-element.12.source_block, bf16[4,128,256]{2,1,0:T(8,128)(2,1)S(1)} %bitcast.12, bf16[4,128,256]{2,1,0:T(8,128)(2,1)S(1)} %bitcast.13, bf16[72,8,256]{2,1,0:T(8,128)(2,1)S(1)} %pad_maximum_fusion.sides, ...), custom_call_target="tpu_custom_call" | custom-call | tf_op jit(solution)/shard_map/pallas_call | solution.py:305
  46.2 0.1 collective-permute-start.5
  46.3 1.2 %collective-permute-done.5 = f32[136,128]{1,0:T(8,128)S(1)} collective-permute-done((f32[136,128]{1,0:T(8,128)S(1)}, f32[136,128]{1,0:T(8,128)S(1)}, u32[]{:S(2)}, u32[]{:S(2)}) %collective-permute-start.5) | collective-permute-done | bytes 69664 | tf_op jit(solution)/shard_map/ppermute | solution.py:396
  47.6 1.8 %collective-permute-start.6 = (f32[136,128]{1,0:T(8,128)S(1)}, f32[136,128]{1,0:T(8,128)S(1)}, u32[]{:S(2)}, u32[]{:S(2)}) collective-permute-start(f32[136,128]{1,0:T(8,128)S(1)} %dynamic-slice_add_fusion), channel_id=1, source_target_pairs={{0,1},{1,0},{2,3},{3,2},{4,5},{5,4},{6,7},{7,6},{8,9},{9,8},{10,11... | collective-permute-start | bytes 208904 | tf_op jit(solution)/shard_map/ppermute | solution.py:396
  49.4 2.6 %collective-permute-done.6 = f32[136,128]{1,0:T(8,128)S(1)} collective-permute-done((f32[136,128]{1,0:T(8,128)S(1)}, f32[136,128]{1,0:T(8,128)S(1)}, u32[]{:S(2)}, u32[]{:S(2)}) %collective-permute-start.6) | collective-permute-done | bytes 69664 | tf_op jit(solution)/shard_map/ppermute | solution.py:396
  51.9 1.4 %collective-permute-start.7 = (f32[136,128]{1,0:T(8,128)S(1)}, f32[136,128]{1,0:T(8,128)S(1)}, u32[]{:S(2)}, u32[]{:S(2)}) collective-permute-start(f32[136,128]{1,0:T(8,128)S(1)} %add.80), channel_id=1, source_target_pairs={{0,4},{2,6},{4,0},{6,2},{8,12},{10,14},{12,8},{14,10},{16,20},{18,... | collective-permute-start | bytes 208904 | tf_op jit(solution)/shard_map/ppermute | solution.py:396
  53.3 3.0 %collective-permute-done.7 = f32[136,128]{1,0:T(8,128)S(1)} collective-permute-done((f32[136,128]{1,0:T(8,128)S(1)}, f32[136,128]{1,0:T(8,128)S(1)}, u32[]{:S(2)}, u32[]{:S(2)}) %collective-permute-start.7) | collective-permute-done | bytes 69664 | tf_op jit(solution)/shard_map/ppermute | solution.py:396
  56.3 1.0 %collective-permute-start.8 = (f32[136,128]{1,0:T(8,128)S(1)}, f32[136,128]{1,0:T(8,128)S(1)}, u32[]{:S(2)}, u32[]{:S(2)}) collective-permute-start(f32[136,128]{1,0:T(8,128)S(1)} %add.81), channel_id=1, source_target_pairs={{0,8},{2,10},{4,12},{6,14},{8,0},{10,2},{12,4},{14,6},{16,24},{18,... | collective-permute-start | bytes 208904 | tf_op jit(solution)/shard_map/ppermute | solution.py:396
  57.3 3.4 %collective-permute-done.8 = f32[136,128]{1,0:T(8,128)S(1)} collective-permute-done((f32[136,128]{1,0:T(8,128)S(1)}, f32[136,128]{1,0:T(8,128)S(1)}, u32[]{:S(2)}, u32[]{:S(2)}) %collective-permute-start.8) | collective-permute-done | bytes 69664 | tf_op jit(solution)/shard_map/ppermute | solution.py:396
  60.7 2.0 %collective-permute-start.9 = (f32[136,128]{1,0:T(8,128)S(1)}, f32[136,128]{1,0:T(8,128)S(1)}, u32[]{:S(2)}, u32[]{:S(2)}) collective-permute-start(f32[136,128]{1,0:T(8,128)S(1)} %add.82), channel_id=1, source_target_pairs={{0,16},{2,18},{4,20},{6,22},{8,24},{10,26},{12,28},{14,30},{16,0},... | collective-permute-start | bytes 208904 | tf_op jit(solution)/shard_map/ppermute | solution.py:396
  62.7 4.0 %collective-permute-done.9 = f32[136,128]{1,0:T(8,128)S(1)} collective-permute-done((f32[136,128]{1,0:T(8,128)S(1)}, f32[136,128]{1,0:T(8,128)S(1)}, u32[]{:S(2)}, u32[]{:S(2)}) %collective-permute-start.9) | collective-permute-done | bytes 69664 | tf_op jit(solution)/shard_map/ppermute | solution.py:396
  66.8 0.1 collective-permute-start.10
  66.8 1.2 %collective-permute-done.10 = f32[136,128]{1,0:T(8,128)S(1)} collective-permute-done((f32[136,128]{1,0:T(8,128)S(1)}, f32[136,128]{1,0:T(8,128)S(1)}, u32[]{:S(2)}, u32[]{:S(2)}) %collective-permute-start.10) | collective-permute-done | bytes 69664 | tf_op jit(solution)/shard_map/ppermute | solution.py:396
  68.1 13.2 %shard_map.69 = (f32[256,256]{1,0:T(8,128)}, f32[1,256]{1,0:T(1,128)}, bf16[256,64,128]{2,1,0:T(8,128)(2,1)}) custom-call(f32[272,128]{1,0:T(8,128)S(1)} %maximum_select_fusion.pay, bf16[64,128,256]{2,1,0:T(8,128)(2,1)} %get-tuple-element.17.source), custom_call_target="tpu_custom_call" | custom-call | tf_op jit(solution)/shard_map/pallas_call | solution.py:363
  (44 shorter events, 0.5 us)
Async XLA Ops:
  1.9 22.1 %copy-start = (f32[64,128]{1,0:T(8,128)S(1)}, f32[64,128]{1,0:T(8,128)}, u32[]{:S(2)}) copy-start(f32[64,128]{1,0:T(8,128)} %param.7) | copy-start | bytes 98308
  2.0 22.1 %copy-start.1 = (f32[64,128]{1,0:T(8,128)S(1)}, f32[64,128]{1,0:T(8,128)}, u32[]{:S(2)}) copy-start(f32[64,128]{1,0:T(8,128)} %param.6) | copy-start | bytes 98308
  2.0 22.1 %copy-start.2 = (f32[64,128]{1,0:T(8,128)S(1)}, f32[64,128]{1,0:T(8,128)}, u32[]{:S(2)}) copy-start(f32[64,128]{1,0:T(8,128)} %param.5) | copy-start | bytes 98308
  7.3 9.7 %collective-permute-start.2 = (bf16[544,256]{1,0:T(8,128)(2,1)S(1)}, bf16[544,256]{1,0:T(8,128)(2,1)S(1)}, u32[]{:S(2)}, u32[]{:S(2)}) collective-permute-start(bf16[544,256]{1,0:T(8,128)(2,1)S(1)} %get-tuple-element.15), channel_id=1, source_target_pairs={{0,1},{1,0},{2,3},{3,2},{4,5},{5,4},{6,7},{7,6},{8,9},{9,8},{10,11... | collective-permute-start | bytes 835592 | tf_op jit(solution)/shard_map/ppermute | solution.py:392
  10.3 11.7 %collective-permute-start = (bf16[544,256]{1,0:T(8,128)(2,1)S(1)}, bf16[544,256]{1,0:T(8,128)(2,1)S(1)}, u32[]{:S(2)}, u32[]{:S(2)}) collective-permute-start(bf16[544,256]{1,0:T(8,128)(2,1)S(1)} %get-tuple-element.13), channel_id=1, source_target_pairs={{0,2},{1,3},{2,4},{3,5},{4,6},{5,7},{6,8},{7,9},{8,10},{9,11},{10,... | collective-permute-start | bytes 835592 | tf_op jit(solution)/shard_map/ppermute | solution.py:392
  10.3 11.8 %collective-permute-start.1 = (bf16[544,256]{1,0:T(8,128)(2,1)S(1)}, bf16[544,256]{1,0:T(8,128)(2,1)S(1)}, u32[]{:S(2)}, u32[]{:S(2)}) collective-permute-start(bf16[544,256]{1,0:T(8,128)(2,1)S(1)} %get-tuple-element.14), channel_id=1, source_target_pairs={{0,30},{1,31},{2,0},{3,1},{4,2},{5,3},{6,4},{7,5},{8,6},{9,7},{10,... | collective-permute-start | bytes 835592 | tf_op jit(solution)/shard_map/ppermute | solution.py:392
  17.4 6.0 %collective-permute-start.3 = (bf16[48,256]{1,0:T(8,128)(2,1)S(1)}, bf16[48,256]{1,0:T(8,128)(2,1)S(1)}, u32[]{:S(2)}, u32[]{:S(2)}) collective-permute-start(bf16[48,256]{1,0:T(8,128)(2,1)S(1)} %pad_maximum_fusion.5), channel_id=1, source_target_pairs={{0,2},{1,3},{2,4},{3,5},{4,6},{5,7},{6,8},{7,9},{8,10},{9,11},{10,... | collective-permute-start | bytes 73736 | tf_op jit(solution)/shard_map/ppermute | solution.py:392
  17.6 6.0 %collective-permute-start.4 = (bf16[48,256]{1,0:T(8,128)(2,1)S(1)}, bf16[48,256]{1,0:T(8,128)(2,1)S(1)}, u32[]{:S(2)}, u32[]{:S(2)}) collective-permute-start(bf16[48,256]{1,0:T(8,128)(2,1)S(1)} %pad_maximum_fusion.6), channel_id=1, source_target_pairs={{0,30},{1,31},{2,0},{3,1},{4,2},{5,3},{6,4},{7,5},{8,6},{9,7},{10,... | collective-permute-start | bytes 73736 | tf_op jit(solution)/shard_map/ppermute | solution.py:392
  46.2 1.3 %collective-permute-start.5 = (f32[136,128]{1,0:T(8,128)S(1)}, f32[136,128]{1,0:T(8,128)S(1)}, u32[]{:S(2)}, u32[]{:S(2)}) collective-permute-start(f32[136,128]{1,0:T(8,128)S(1)} %constant_dynamic-slice_fusion), channel_id=1, source_target_pairs={{0,2},{2,0},{4,6},{6,4},{8,10},{10,8},{12,14},{14,12},{16,18},{18,... | collective-permute-start | bytes 208904 | tf_op jit(solution)/shard_map/ppermute | solution.py:396
  47.6 4.4 %collective-permute-start.6 = (f32[136,128]{1,0:T(8,128)S(1)}, f32[136,128]{1,0:T(8,128)S(1)}, u32[]{:S(2)}, u32[]{:S(2)}) collective-permute-start(f32[136,128]{1,0:T(8,128)S(1)} %dynamic-slice_add_fusion), channel_id=1, source_target_pairs={{0,1},{1,0},{2,3},{3,2},{4,5},{5,4},{6,7},{7,6},{8,9},{9,8},{10,11... | collective-permute-start | bytes 208904 | tf_op jit(solution)/shard_map/ppermute | solution.py:396
  51.9 4.4 %collective-permute-start.7 = (f32[136,128]{1,0:T(8,128)S(1)}, f32[136,128]{1,0:T(8,128)S(1)}, u32[]{:S(2)}, u32[]{:S(2)}) collective-permute-start(f32[136,128]{1,0:T(8,128)S(1)} %add.80), channel_id=1, source_target_pairs={{0,4},{2,6},{4,0},{6,2},{8,12},{10,14},{12,8},{14,10},{16,20},{18,... | collective-permute-start | bytes 208904 | tf_op jit(solution)/shard_map/ppermute | solution.py:396
  56.3 4.4 %collective-permute-start.8 = (f32[136,128]{1,0:T(8,128)S(1)}, f32[136,128]{1,0:T(8,128)S(1)}, u32[]{:S(2)}, u32[]{:S(2)}) collective-permute-start(f32[136,128]{1,0:T(8,128)S(1)} %add.81), channel_id=1, source_target_pairs={{0,8},{2,10},{4,12},{6,14},{8,0},{10,2},{12,4},{14,6},{16,24},{18,... | collective-permute-start | bytes 208904 | tf_op jit(solution)/shard_map/ppermute | solution.py:396
  60.7 6.0 %collective-permute-start.9 = (f32[136,128]{1,0:T(8,128)S(1)}, f32[136,128]{1,0:T(8,128)S(1)}, u32[]{:S(2)}, u32[]{:S(2)}) collective-permute-start(f32[136,128]{1,0:T(8,128)S(1)} %add.82), channel_id=1, source_target_pairs={{0,16},{2,18},{4,20},{6,22},{8,24},{10,26},{12,28},{14,30},{16,0},... | collective-permute-start | bytes 208904 | tf_op jit(solution)/shard_map/ppermute | solution.py:396
  66.8 1.3 %collective-permute-start.10 = (f32[136,128]{1,0:T(8,128)S(1)}, f32[136,128]{1,0:T(8,128)S(1)}, u32[]{:S(2)}, u32[]{:S(2)}) collective-permute-start(f32[136,128]{1,0:T(8,128)S(1)} %add.83), channel_id=1, source_target_pairs={{0,2},{2,0},{4,6},{6,4},{8,10},{10,8},{12,14},{14,12},{16,18},{18,... | collective-permute-start | bytes 208904 | tf_op jit(solution)/shard_map/ppermute | solution.py:396

commit v6 on v5

--- a/solution.py
+++ b/solution.py
@@ -193,7 +193,8 @@
     start_of = lambda r: GROUP + r * width
 
     for m in range(3):
-        turned_table = jnp.concatenate([table[m], jnp.zeros((LANES - table.shape[1], LANES), F32)]).T
+        line = 0.2 + table[m] if m == 2 else 0.2 - table[m]
+        turned_table = jnp.concatenate([line, jnp.zeros((LANES - table.shape[1], LANES), F32)]).T
         for q in range(table.shape[1]):
             coef[m, LANES * q:LANES * (q + 1), :] = jnp.broadcast_to(turned_table[:, q:q + 1], (LANES, LANES))
 
@@ -259,11 +260,10 @@
     for step in range(1, SUBSTEPS):
         substep(buffers[(step - 1) % 2], buffers[step % 2], step)
     source = buffers[(SUBSTEPS - 1) % 2]
-    gram[...] = jnp.zeros_like(gram)
     chunk = lines
 
-    def last_chunk(q, carry):
-        def block(p, inner):
+    def finish_chunk(q):
+        for p in range(chunk // TALL):
             r = q * chunk + TALL * p
             for t in range(0, lanes // GROUP, 2):
                 parts = []
@@ -275,15 +275,23 @@
                     for h in range(halves):
                         both = jnp.concatenate([parts[0][h][i], parts[1][h][i]], axis=0).astype(BF16)
                         evolved[r + i, GROUP * t:GROUP * (t + 2), LANES * h:LANES * (h + 1)] = both
-            return inner
-
-        lax.fori_loop(0, chunk // TALL, block, 0)
+
+    def product(q):
         part = evolved[pl.ds(q * chunk, chunk)].reshape(chunk * lanes, fields)
-        gram[...] += lax.dot_general(part, part, (((0,), (0,)), ((), ())), preferred_element_type=F32)
-        storing(q).start()
+        return lax.dot_general(part, part, (((0,), (0,)), ((), ())), preferred_element_type=F32)
+
+    finish_chunk(0)
+    gram[...] = jnp.zeros_like(gram)
+
+    def last_chunk(q, carry):
+        storing(q - 1).start()
+        gram[...] += product(q - 1)
+        finish_chunk(q)
         return carry
 
-    lax.fori_loop(0, chunks, last_chunk, 0)
+    lax.fori_loop(1, chunks, last_chunk, 0)
+    storing(chunks - 1).start()
+    gram[...] += product(chunks - 1)
     h = fields // 2
     ri = lax.broadcasted_iota(jnp.int32, (h, h), 0)
     ci = lax.broadcasted_iota(jnp.int32, (h, h), 1)
@@ -471,7 +479,7 @@
     middle = jnp.concatenate([joined(low[1]), block, joined(high[1])], axis=1)
     around = joined(jnp.concatenate([low_side[1], side_part, high_side[1]], axis=1))
     table = jnp.concatenate([around[:, :, :HALO], middle, around[:, :, HALO:]], axis=2)
-    table = jnp.stack([0.2 - table[0], 0.2 - table[1], 0.2 + table[2]]).reshape(3, -1)
+    table = table.reshape(3, -1)
     table = jnp.pad(table, ((0, 0), (0, -table.shape[1] % LANES))).reshape(3, -1, LANES)
     evolved, payload = evolve(own, low[0], high[0], sides, table)
     total = float(rows * nx * cols * ny)

time: 81.7 us -> 79.8 us (0.977)
  Pallas kernels: 39.7 us -> 38.1 us
    pallas_call x1, Pallas kernels: 21.2 us -> 19.7 us  [evolve(): pl.pallas_call(evolve_kernel, in_specs=[hbm, vmem, vmem, vmem, vmem], out...]
where the time goes in v6:
time: 79.8 us; the launch traced here: 79.6 us
  Pallas kernels  38.1 us (48%)
  waiting for transfers between devices  18.9 us (24%)
  starting transfers between devices  18.3 us (23%)
  local copies, waits for them, and re-layouts  1.76 us (2%)
  other arithmetic  1.36 us (2%)
  between operations  1.22 us (2%)
    pallas_call x1, Pallas kernels, evolve(): pl.pallas_call(evolve_kernel, in_specs=[hbm, vmem, vmem, vmem, vmem], out...  19.7 us
    ppermute x6, waiting for transfers between devices, swapped(): lax.ppermute(block, axis, [(i, i ^ bit) for i in range(lax.axis_size(axis...  15.5 us
    pallas_call x1, Pallas kernels, finish(): pl.pallas_call(functools.partial(finish_kernel, total), in_specs=[vmem, h...  13.2 us
    ppermute x5, starting transfers between devices, shifted(): return lax.ppermute(block, ('gx', 'gy'), pairs)  12 us
    ppermute x6, starting transfers between devices, swapped(): lax.ppermute(block, axis, [(i, i ^ bit) for i in range(lax.axis_size(axis...  6.28 us
    pallas_call x1, Pallas kernels, turn(): pl.pallas_call(turn_kernel, in_specs=[hbm, vmem, vmem, vmem], out_specs=(...  5.24 us
    ppermute x5, waiting for transfers between devices, shifted(): return lax.ppermute(block, ('gx', 'gy'), pairs)  3.37 us
  transfers between devices with their start and end apart: 11, of which 8 were waited for; matrix products, arithmetic and copies ran while one was open for 1% of the time, Pallas kernels for 0%

profile of v6, /device:TPU:0, one launch (start us, length us, event | category | flops | bytes accessed | tf_op | source)
XLA Modules:
  0.0 79.6 jit_solution(422903768754807405)
XLA Ops:
  0.6 0.8 %reduce-precision_convert_fusion.1 = (bf16[3,64,128]{2,1,0:T(8,128)(2,1)S(1)}, bf16[3,64,128]{2,1,0:T(8,128)(2,1)S(1)}, bf16[3,64,128]{2,1,0:T(8,128)(2,1)S(1)}) fusion(f32[1,64,128]{2,1,0:T(8,128)} %bitcast.14, f32[1,64,128]{2,1,0:T(8,128)} %bitcast.16, f32[1,64,128]{2,1,0:T(8,128)} %bitcast.18), kind=kLoop, calls=%fused_computation.9 | loop fusion | flops 245760 | bytes 245760 | tf_op jit(solution)/shard_map/convert_element_type | solution.py:427
  1.5 0.1 fusion.4
  1.6 0.1 pad_maximum_fusion.3
  1.7 0.2 reshape.104
  1.9 0.0 copy-start
  2.0 0.0 copy-start.1
  2.0 0.0 copy-start.2
  2.1 5.2 %shard_map.67 = (bf16[64,128,256]{2,1,0:T(8,128)(2,1)}, bf16[544,256]{1,0:T(8,128)(2,1)S(1)}, bf16[544,256]{1,0:T(8,128)(2,1)S(1)}, bf16[544,256]{1,0:T(8,128)(2,1)S(1)}) custom-call(bf16[256,64,128]{2,1,0:T(8,128)(2,1)} %source.1, bf16[32,256]{1,0:T(8,128)(2,1)S(1)} %reshape.101.low_tail, bf16[32,256]{1,0:T(8,128)(2,1)S(1)} %reshape.103.high_tail, ...), custom_call_target="tpu_custom_call" | custom-call | tf_op jit(solution)/shard_map/pallas_call | solution.py:160
  7.3 3.0 %collective-permute-start.2 = (bf16[544,256]{1,0:T(8,128)(2,1)S(1)}, bf16[544,256]{1,0:T(8,128)(2,1)S(1)}, u32[]{:S(2)}, u32[]{:S(2)}) collective-permute-start(bf16[544,256]{1,0:T(8,128)(2,1)S(1)} %get-tuple-element.15), channel_id=1, source_target_pairs={{0,1},{1,0},{2,3},{3,2},{4,5},{5,4},{6,7},{7,6},{8,9},{9,8},{10,11... | collective-permute-start | bytes 835592 | tf_op jit(solution)/shard_map/ppermute | solution.py:400
  10.3 0.0 collective-permute-start
  10.3 4.4 %collective-permute-start.1 = (bf16[544,256]{1,0:T(8,128)(2,1)S(1)}, bf16[544,256]{1,0:T(8,128)(2,1)S(1)}, u32[]{:S(2)}, u32[]{:S(2)}) collective-permute-start(bf16[544,256]{1,0:T(8,128)(2,1)S(1)} %get-tuple-element.14), channel_id=1, source_target_pairs={{0,30},{1,31},{2,0},{3,1},{4,2},{5,3},{6,4},{7,5},{8,6},{9,7},{10,... | collective-permute-start | bytes 835592 | tf_op jit(solution)/shard_map/ppermute | solution.py:400
  14.8 2.2 %collective-permute-done.2 = bf16[544,256]{1,0:T(8,128)(2,1)S(1)} collective-permute-done((bf16[544,256]{1,0:T(8,128)(2,1)S(1)}, bf16[544,256]{1,0:T(8,128)(2,1)S(1)}, u32[]{:S(2)}, u32[]{:S(2)}) %collective-permute-start.2) | collective-permute-done | bytes 278560 | tf_op jit(solution)/shard_map/ppermute | solution.py:400
  17.0 0.2 reshape.108
  17.2 0.1 reshape.109
  17.4 0.1 collective-permute-start.3
  17.4 0.1 reshape.113
  17.6 4.5 %collective-permute-start.4 = (bf16[48,256]{1,0:T(8,128)(2,1)S(1)}, bf16[48,256]{1,0:T(8,128)(2,1)S(1)}, u32[]{:S(2)}, u32[]{:S(2)}) collective-permute-start(bf16[48,256]{1,0:T(8,128)(2,1)S(1)} %pad_maximum_fusion.6), channel_id=1, source_target_pairs={{0,30},{1,31},{2,0},{3,1},{4,2},{5,3},{6,4},{7,5},{8,6},{9,7},{10,... | collective-permute-start | bytes 73736 | tf_op jit(solution)/shard_map/ppermute | solution.py:400
  22.1 0.0 collective-permute-done
  22.1 0.0 collective-permute-done.1
  22.2 1.2 %collective-permute-done.3 = bf16[48,256]{1,0:T(8,128)(2,1)S(1)} collective-permute-done((bf16[48,256]{1,0:T(8,128)(2,1)S(1)}, bf16[48,256]{1,0:T(8,128)(2,1)S(1)}, u32[]{:S(2)}, u32[]{:S(2)}) %collective-permute-start.3) | collective-permute-done | bytes 24608 | tf_op jit(solution)/shard_map/ppermute | solution.py:400
  23.4 0.2 slice.133
  23.6 0.0 collective-permute-done.4
  23.6 0.2 slice.136
  23.8 0.1 maximum_convert_fusion
  23.9 0.1 fusion.5
  24.0 0.0 copy-done
  24.0 0.0 copy-done.1
  24.0 0.0 copy-done.2
  24.0 0.2 pad_maximum_fusion.1
  24.2 0.2 reshape.116
  24.5 0.1 reshape.117.table
  24.6 19.7 %shard_map.68 = (bf16[64,128,256]{2,1,0:T(8,128)(2,1)}, f32[272,128]{1,0:T(8,128)S(1)}) custom-call(bf16[64,128,256]{2,1,0:T(8,128)(2,1)} %get-tuple-element.12.source_block, bf16[4,128,256]{2,1,0:T(8,128)(2,1)S(1)} %bitcast.12, bf16[4,128,256]{2,1,0:T(8,128)(2,1)S(1)} %bitcast.13, bf16[72,8,256]{2,1,0:T(8,128)(2,1)S(1)} %pad_maximum_fusion.sides, ...), custom_call_target="tpu_custom_call" | custom-call | tf_op jit(solution)/shard_map/pallas_call | solution.py:313
  44.3 0.1 collective-permute-start.5
  44.4 1.2 %collective-permute-done.5 = f32[136,128]{1,0:T(8,128)S(1)} collective-permute-done((f32[136,128]{1,0:T(8,128)S(1)}, f32[136,128]{1,0:T(8,128)S(1)}, u32[]{:S(2)}, u32[]{:S(2)}) %collective-permute-start.5) | collective-permute-done | bytes 69664 | tf_op jit(solution)/shard_map/ppermute | solution.py:404
  45.7 1.8 %collective-permute-start.6 = (f32[136,128]{1,0:T(8,128)S(1)}, f32[136,128]{1,0:T(8,128)S(1)}, u32[]{:S(2)}, u32[]{:S(2)}) collective-permute-start(f32[136,128]{1,0:T(8,128)S(1)} %dynamic-slice_add_fusion), channel_id=1, source_target_pairs={{0,1},{1,0},{2,3},{3,2},{4,5},{5,4},{6,7},{7,6},{8,9},{9,8},{10,11... | collective-permute-start | bytes 208904 | tf_op jit(solution)/shard_map/ppermute | solution.py:404
  47.5 2.6 %collective-permute-done.6 = f32[136,128]{1,0:T(8,128)S(1)} collective-permute-done((f32[136,128]{1,0:T(8,128)S(1)}, f32[136,128]{1,0:T(8,128)S(1)}, u32[]{:S(2)}, u32[]{:S(2)}) %collective-permute-start.6) | collective-permute-done | bytes 69664 | tf_op jit(solution)/shard_map/ppermute | solution.py:404
  50.1 1.4 %collective-permute-start.7 = (f32[136,128]{1,0:T(8,128)S(1)}, f32[136,128]{1,0:T(8,128)S(1)}, u32[]{:S(2)}, u32[]{:S(2)}) collective-permute-start(f32[136,128]{1,0:T(8,128)S(1)} %add.75), channel_id=1, source_target_pairs={{0,4},{2,6},{4,0},{6,2},{8,12},{10,14},{12,8},{14,10},{16,20},{18,... | collective-permute-start | bytes 208904 | tf_op jit(solution)/shard_map/ppermute | solution.py:404
  51.5 3.0 %collective-permute-done.7 = f32[136,128]{1,0:T(8,128)S(1)} collective-permute-done((f32[136,128]{1,0:T(8,128)S(1)}, f32[136,128]{1,0:T(8,128)S(1)}, u32[]{:S(2)}, u32[]{:S(2)}) %collective-permute-start.7) | collective-permute-done | bytes 69664 | tf_op jit(solution)/shard_map/ppermute | solution.py:404
  54.4 1.0 %collective-permute-start.8 = (f32[136,128]{1,0:T(8,128)S(1)}, f32[136,128]{1,0:T(8,128)S(1)}, u32[]{:S(2)}, u32[]{:S(2)}) collective-permute-start(f32[136,128]{1,0:T(8,128)S(1)} %add.76), channel_id=1, source_target_pairs={{0,8},{2,10},{4,12},{6,14},{8,0},{10,2},{12,4},{14,6},{16,24},{18,... | collective-permute-start | bytes 208904 | tf_op jit(solution)/shard_map/ppermute | solution.py:404
  55.4 3.4 %collective-permute-done.8 = f32[136,128]{1,0:T(8,128)S(1)} collective-permute-done((f32[136,128]{1,0:T(8,128)S(1)}, f32[136,128]{1,0:T(8,128)S(1)}, u32[]{:S(2)}, u32[]{:S(2)}) %collective-permute-start.8) | collective-permute-done | bytes 69664 | tf_op jit(solution)/shard_map/ppermute | solution.py:404
  58.8 2.0 %collective-permute-start.9 = (f32[136,128]{1,0:T(8,128)S(1)}, f32[136,128]{1,0:T(8,128)S(1)}, u32[]{:S(2)}, u32[]{:S(2)}) collective-permute-start(f32[136,128]{1,0:T(8,128)S(1)} %add.77), channel_id=1, source_target_pairs={{0,16},{2,18},{4,20},{6,22},{8,24},{10,26},{12,28},{14,30},{16,0},... | collective-permute-start | bytes 208904 | tf_op jit(solution)/shard_map/ppermute | solution.py:404
  60.8 4.0 %collective-permute-done.9 = f32[136,128]{1,0:T(8,128)S(1)} collective-permute-done((f32[136,128]{1,0:T(8,128)S(1)}, f32[136,128]{1,0:T(8,128)S(1)}, u32[]{:S(2)}, u32[]{:S(2)}) %collective-permute-start.9) | collective-permute-done | bytes 69664 | tf_op jit(solution)/shard_map/ppermute | solution.py:404
  64.9 0.1 collective-permute-start.10
  64.9 1.2 %collective-permute-done.10 = f32[136,128]{1,0:T(8,128)S(1)} collective-permute-done((f32[136,128]{1,0:T(8,128)S(1)}, f32[136,128]{1,0:T(8,128)S(1)}, u32[]{:S(2)}, u32[]{:S(2)}) %collective-permute-start.10) | collective-permute-done | bytes 69664 | tf_op jit(solution)/shard_map/ppermute | solution.py:404
  66.2 13.2 %shard_map.69 = (f32[256,256]{1,0:T(8,128)}, f32[1,256]{1,0:T(1,128)}, bf16[256,64,128]{2,1,0:T(8,128)(2,1)}) custom-call(f32[272,128]{1,0:T(8,128)S(1)} %maximum_select_fusion.pay, bf16[64,128,256]{2,1,0:T(8,128)(2,1)} %get-tuple-element.17.source), custom_call_target="tpu_custom_call" | custom-call | tf_op jit(solution)/shard_map/pallas_call | solution.py:371
  (44 shorter events, 0.5 us)
Async XLA Ops:
  1.9 22.1 %copy-start = (f32[64,128]{1,0:T(8,128)S(1)}, f32[64,128]{1,0:T(8,128)}, u32[]{:S(2)}) copy-start(f32[64,128]{1,0:T(8,128)} %param.7) | copy-start | bytes 98308
  2.0 22.1 %copy-start.1 = (f32[64,128]{1,0:T(8,128)S(1)}, f32[64,128]{1,0:T(8,128)}, u32[]{:S(2)}) copy-start(f32[64,128]{1,0:T(8,128)} %param.6) | copy-start | bytes 98308
  2.0 22.1 %copy-start.2 = (f32[64,128]{1,0:T(8,128)S(1)}, f32[64,128]{1,0:T(8,128)}, u32[]{:S(2)}) copy-start(f32[64,128]{1,0:T(8,128)} %param.5) | copy-start | bytes 98308
  7.3 9.7 %collective-permute-start.2 = (bf16[544,256]{1,0:T(8,128)(2,1)S(1)}, bf16[544,256]{1,0:T(8,128)(2,1)S(1)}, u32[]{:S(2)}, u32[]{:S(2)}) collective-permute-start(bf16[544,256]{1,0:T(8,128)(2,1)S(1)} %get-tuple-element.15), channel_id=1, source_target_pairs={{0,1},{1,0},{2,3},{3,2},{4,5},{5,4},{6,7},{7,6},{8,9},{9,8},{10,11... | collective-permute-start | bytes 835592 | tf_op jit(solution)/shard_map/ppermute | solution.py:400
  10.3 11.7 %collective-permute-start = (bf16[544,256]{1,0:T(8,128)(2,1)S(1)}, bf16[544,256]{1,0:T(8,128)(2,1)S(1)}, u32[]{:S(2)}, u32[]{:S(2)}) collective-permute-start(bf16[544,256]{1,0:T(8,128)(2,1)S(1)} %get-tuple-element.13), channel_id=1, source_target_pairs={{0,2},{1,3},{2,4},{3,5},{4,6},{5,7},{6,8},{7,9},{8,10},{9,11},{10,... | collective-permute-start | bytes 835592 | tf_op jit(solution)/shard_map/ppermute | solution.py:400
  10.3 11.8 %collective-permute-start.1 = (bf16[544,256]{1,0:T(8,128)(2,1)S(1)}, bf16[544,256]{1,0:T(8,128)(2,1)S(1)}, u32[]{:S(2)}, u32[]{:S(2)}) collective-permute-start(bf16[544,256]{1,0:T(8,128)(2,1)S(1)} %get-tuple-element.14), channel_id=1, source_target_pairs={{0,30},{1,31},{2,0},{3,1},{4,2},{5,3},{6,4},{7,5},{8,6},{9,7},{10,... | collective-permute-start | bytes 835592 | tf_op jit(solution)/shard_map/ppermute | solution.py:400
  17.4 6.0 %collective-permute-start.3 = (bf16[48,256]{1,0:T(8,128)(2,1)S(1)}, bf16[48,256]{1,0:T(8,128)(2,1)S(1)}, u32[]{:S(2)}, u32[]{:S(2)}) collective-permute-start(bf16[48,256]{1,0:T(8,128)(2,1)S(1)} %pad_maximum_fusion.5), channel_id=1, source_target_pairs={{0,2},{1,3},{2,4},{3,5},{4,6},{5,7},{6,8},{7,9},{8,10},{9,11},{10,... | collective-permute-start | bytes 73736 | tf_op jit(solution)/shard_map/ppermute | solution.py:400
  17.6 6.0 %collective-permute-start.4 = (bf16[48,256]{1,0:T(8,128)(2,1)S(1)}, bf16[48,256]{1,0:T(8,128)(2,1)S(1)}, u32[]{:S(2)}, u32[]{:S(2)}) collective-permute-start(bf16[48,256]{1,0:T(8,128)(2,1)S(1)} %pad_maximum_fusion.6), channel_id=1, source_target_pairs={{0,30},{1,31},{2,0},{3,1},{4,2},{5,3},{6,4},{7,5},{8,6},{9,7},{10,... | collective-permute-start | bytes 73736 | tf_op jit(solution)/shard_map/ppermute | solution.py:400
  44.3 1.3 %collective-permute-start.5 = (f32[136,128]{1,0:T(8,128)S(1)}, f32[136,128]{1,0:T(8,128)S(1)}, u32[]{:S(2)}, u32[]{:S(2)}) collective-permute-start(f32[136,128]{1,0:T(8,128)S(1)} %constant_dynamic-slice_fusion), channel_id=1, source_target_pairs={{0,2},{2,0},{4,6},{6,4},{8,10},{10,8},{12,14},{14,12},{16,18},{18,... | collective-permute-start | bytes 208904 | tf_op jit(solution)/shard_map/ppermute | solution.py:404
  45.7 4.4 %collective-permute-start.6 = (f32[136,128]{1,0:T(8,128)S(1)}, f32[136,128]{1,0:T(8,128)S(1)}, u32[]{:S(2)}, u32[]{:S(2)}) collective-permute-start(f32[136,128]{1,0:T(8,128)S(1)} %dynamic-slice_add_fusion), channel_id=1, source_target_pairs={{0,1},{1,0},{2,3},{3,2},{4,5},{5,4},{6,7},{7,6},{8,9},{9,8},{10,11... | collective-permute-start | bytes 208904 | tf_op jit(solution)/shard_map/ppermute | solution.py:404
  50.1 4.4 %collective-permute-start.7 = (f32[136,128]{1,0:T(8,128)S(1)}, f32[136,128]{1,0:T(8,128)S(1)}, u32[]{:S(2)}, u32[]{:S(2)}) collective-permute-start(f32[136,128]{1,0:T(8,128)S(1)} %add.75), channel_id=1, source_target_pairs={{0,4},{2,6},{4,0},{6,2},{8,12},{10,14},{12,8},{14,10},{16,20},{18,... | collective-permute-start | bytes 208904 | tf_op jit(solution)/shard_map/ppermute | solution.py:404
  54.4 4.4 %collective-permute-start.8 = (f32[136,128]{1,0:T(8,128)S(1)}, f32[136,128]{1,0:T(8,128)S(1)}, u32[]{:S(2)}, u32[]{:S(2)}) collective-permute-start(f32[136,128]{1,0:T(8,128)S(1)} %add.76), channel_id=1, source_target_pairs={{0,8},{2,10},{4,12},{6,14},{8,0},{10,2},{12,4},{14,6},{16,24},{18,... | collective-permute-start | bytes 208904 | tf_op jit(solution)/shard_map/ppermute | solution.py:404
  58.8 6.0 %collective-permute-start.9 = (f32[136,128]{1,0:T(8,128)S(1)}, f32[136,128]{1,0:T(8,128)S(1)}, u32[]{:S(2)}, u32[]{:S(2)}) collective-permute-start(f32[136,128]{1,0:T(8,128)S(1)} %add.77), channel_id=1, source_target_pairs={{0,16},{2,18},{4,20},{6,22},{8,24},{10,26},{12,28},{14,30},{16,0},... | collective-permute-start | bytes 208904 | tf_op jit(solution)/shard_map/ppermute | solution.py:404
  64.9 1.3 %collective-permute-start.10 = (f32[136,128]{1,0:T(8,128)S(1)}, f32[136,128]{1,0:T(8,128)S(1)}, u32[]{:S(2)}, u32[]{:S(2)}) collective-permute-start(f32[136,128]{1,0:T(8,128)S(1)} %add.78), channel_id=1, source_target_pairs={{0,2},{2,0},{4,6},{6,4},{8,10},{10,8},{12,14},{14,12},{16,18},{18,... | collective-permute-start | bytes 208904 | tf_op jit(solution)/shard_map/ppermute | solution.py:404
